TPU v7x, 512 devices: a whole 4x4x16 slice. The times are simulated.
512 devices in a mesh: seq: 32 (over z, core), head: 16 (over x, y).
Axes of the slice: x: 4, y: 4, z: 16, core: 2. Of those that a mesh axis runs over, the one named last changes fastest.
Arguments:
- query_vectors: bfloat16 [65536, 4096], P(('seq', 'head')), may hold values from -6 to 6
- key_vectors: bfloat16 [65536, 4096], P(('seq', 'head')), may hold values from -0.011962891 to 0.011962891
- out_grad: bfloat16 [65536, 4096], P(('seq', 'head')), may hold values from -6 to 6
- log_decay: bfloat16 [65536, 32], P(('seq', 'head')), may hold values from -1 to 0, as said below
- doc_lengths: int32 [8], replicated, may hold values from 1 to 32768, 65536 in all
Outputs:
- value_grad: bfloat16 [65536, 4096], P(('seq', 'head'))
Inputs may be any that keep to these rules, and one draw needn't show every extreme that they name: `log_decay`: every entry is negative. `doc_lengths`: the lengths sum to 65536.
All inputs are finite; a program needn't handle non-finite values.
Results may differ from a plain program's by a relative error of at most 0.0043.
Values may be sent and summed in bfloat16 or wider, within the bound.
No kernel may reach another device: no remote copies, remote signals or barrier semaphores. Data moves between devices by JAX's collectives and lax.ppermute only.
A program may use at most 64 MiB of HBM per device.

v0:
```python
import jax
import jax.numpy as jnp
from jax import lax
from jax.sharding import PartitionSpec as P


def from_behind(x, axis, by):
    size = lax.axis_size(axis)
    pairs = [(i, i + by) for i in range(size) if 0 <= i + by < size]
    return lax.ppermute(x, axis, pairs)


def segment_ids(token_positions, doc_starts):
    return jnp.sum((doc_starts <= token_positions[..., None]).astype(jnp.int32), axis=-1)


def body(query_vectors, key_vectors, out_grad, log_decay, doc_lengths):
    heads_total = log_decay.shape[1]
    head_size = query_vectors.shape[1] // heads_total
    queries, key_rows, grads, decays = (
        lax.all_to_all(query_vectors, "head", split_axis=1, concat_axis=0, tiled=True),
        lax.all_to_all(key_vectors, "head", split_axis=1, concat_axis=0, tiled=True),
        lax.all_to_all(out_grad, "head", split_axis=1, concat_axis=0, tiled=True),
        lax.all_to_all(log_decay, "head", split_axis=1, concat_axis=0, tiled=True),
    )
    group_len = queries.shape[0]
    heads_local = decays.shape[1]
    block_len = min(1024, group_len)
    blocks = group_len // block_len
    doc_starts = jnp.cumsum(doc_lengths) - doc_lengths
    offsets = jnp.arange(block_len, dtype=jnp.int32)
    token_positions = lax.axis_index("seq") * group_len + jnp.arange(
        group_len, dtype=jnp.int32
    ).reshape(blocks, block_len)
    segments = segment_ids(token_positions, doc_starts)
    before = segment_ids(token_positions[:, 0] - 1, doc_starts)
    block_shape = (blocks, block_len, heads_local, head_size)
    query_blocks = queries.reshape(block_shape)
    key_blocks = key_rows.reshape(block_shape)
    grad_blocks = grads.reshape(block_shape)
    cumulative = jnp.cumsum(
        decays.astype(jnp.float32).reshape(blocks, block_len, heads_local), axis=1
    )
    scores = jnp.einsum(
        "bihe,bthe->bhit", key_blocks, query_blocks, preferred_element_type=jnp.float32
    )
    by_head = jnp.transpose(cumulative, (0, 2, 1))
    decay_gaps = by_head[:, :, None, :] - by_head[:, :, :, None]
    causal = offsets[None, :] >= offsets[:, None]
    allowed = causal[None] & (segments[:, None, :] == segments[:, :, None])
    weights = (
        jnp.where(allowed[:, None], jnp.exp(jnp.minimum(decay_gaps, 0.0)), 0.0) * scores
    ).astype(jnp.bfloat16)
    inside = jnp.einsum("bhit,bthe->bihe", weights, grad_blocks, preferred_element_type=jnp.float32)
    last_segment = segments[:, -1]
    last_cum = cumulative[:, -1, :]
    tail_weight = jnp.where(
        (segments == last_segment[:, None])[:, :, None],
        jnp.exp(last_cum[:, None, :] - cumulative),
        0.0,
    )
    linked = segments == before[:, None]
    scaled = (
        jnp.where(linked[:, :, None], jnp.exp(cumulative), 0.0)[..., None]
        * query_blocks.astype(jnp.float32)
    ).astype(jnp.bfloat16)
    summaries = jnp.einsum(
        "bthe,bthf->bhef", scaled, grad_blocks, preferred_element_type=jnp.float32
    )
    factors = jnp.where((last_segment == before)[:, None], jnp.exp(last_cum), 0.0)
    zeros_state = jnp.zeros((heads_local, head_size, head_size), jnp.float32)
    unit_factor = jnp.ones((heads_local,), jnp.float32)

    def compose(carried_pair, block_item):
        factor_acc, summary_acc = carried_pair
        factor, summary = block_item
        return ((factor * factor_acc, summary + factor[:, None, None] * summary_acc), None)

    (device_factor, device_summary), unused = lax.scan(
        compose, (unit_factor, zeros_state), (factors, summaries), reverse=True
    )

    def pass_back(index_step, received):
        return from_behind(device_summary + device_factor[:, None, None] * received, "seq", -1)

    incoming = lax.fori_loop(0, lax.axis_size("seq") - 1, pass_back, zeros_state)

    def unroll(state, block_item):
        factor, summary = block_item
        return (summary + factor[:, None, None] * state, state)

    leftover, states = lax.scan(unroll, incoming, (factors, summaries), reverse=True)
    carried = (
        jnp.einsum(
            "bihe,bhef->bihf",
            key_blocks.astype(jnp.float32),
            states,
            precision=lax.Precision.HIGHEST,
        )
        * tail_weight[..., None]
    )
    value_grad = (inside + carried).astype(jnp.bfloat16).reshape(group_len, heads_local * head_size)
    return lax.all_to_all(value_grad, "head", split_axis=0, concat_axis=1, tiled=True)


def solution(mesh):
    in_specs = (
        P(("seq", "head"), None),
        P(("seq", "head"), None),
        P(("seq", "head"), None),
        P(("seq", "head"), None),
        P(),
    )
    out_specs = P(("seq", "head"), None)
    return jax.shard_map(body, mesh=mesh, in_specs=in_specs, out_specs=out_specs, check_vma=False)
```

profile of v0, /device:TPU:225, one launch (start us, length us, event | category | flops | bytes accessed | tf_op | source)
XLA Modules:
  0.0 353.7 jit_solution(9214605966489969311)
XLA Ops:
  0.0 6.8 %all-to-all-start = ((bf16[128,16,2]{0,2,1:T(2,128)(2,1)}), bf16[128,16,2]{0,2,1:T(2,128)(2,1)S(1)}, u32[]{:S(2)}, u32[]{:S(2)}) async-start(bf16[128,16,2]{0,2,1:T(2,128)(2,1)} %bitcast.78), calls=%async_computation | async-start | bytes 16384 | tf_op jit(solution)/shard_map/all_to_all | solution.py:24
  6.8 2.4 copy.155
  9.2 3.9 %all-to-all-done = bf16[128,16,2]{0,2,1:T(2,128)(2,1)S(1)} async-done(((bf16[128,16,2]{0,2,1:T(2,128)(2,1)}), bf16[128,16,2]{0,2,1:T(2,128)(2,1)S(1)}, u32[]{:S(2)}, u32[]{:S(2)}) %all-to-all-start) | async-done | bytes 8224 | tf_op jit(solution)/shard_map/all_to_all | solution.py:24
  13.1 3.7 %all-to-all-start.2 = ((bf16[128,16,256]{2,0,1:T(8,128)(2,1)}), bf16[128,16,256]{2,0,1:T(8,128)(2,1)S(1)}, u32[]{:S(2)}, u32[]{:S(2)}) async-start(bf16[128,16,256]{2,0,1:T(8,128)(2,1)} %bitcast.54), calls=%async_computation.2 | async-start | bytes 2097152 | tf_op jit(solution)/shard_map/all_to_all | solution.py:21
  19.7 11.8 %all-to-all-done.2 = bf16[128,16,256]{2,0,1:T(8,128)(2,1)S(1)} async-done(((bf16[128,16,256]{2,0,1:T(8,128)(2,1)}), bf16[128,16,256]{2,0,1:T(8,128)(2,1)S(1)}, u32[]{:S(2)}, u32[]{:S(2)}) %all-to-all-start.2) | async-done | bytes 1048608 | tf_op jit(solution)/shard_map/all_to_all | solution.py:21
  31.6 4.5 %all-to-all-start.1 = ((bf16[128,16,256]{2,0,1:T(8,128)(2,1)}), bf16[128,16,256]{2,0,1:T(8,128)(2,1)S(1)}, u32[]{:S(2)}, u32[]{:S(2)}) async-start(bf16[128,16,256]{2,0,1:T(8,128)(2,1)} %bitcast.69), calls=%async_computation.1 | async-start | bytes 2097152 | tf_op jit(solution)/shard_map/all_to_all | solution.py:22
  38.1 2.3 copy.154
  40.4 2.6 compare_and_fusion
  45.4 5.3 %all-to-all-done.1 = bf16[128,16,256]{2,0,1:T(8,128)(2,1)S(1)} async-done(((bf16[128,16,256]{2,0,1:T(8,128)(2,1)}), bf16[128,16,256]{2,0,1:T(8,128)(2,1)S(1)}, u32[]{:S(2)}, u32[]{:S(2)}) %all-to-all-start.1) | async-done | bytes 1048608 | tf_op jit(solution)/shard_map/all_to_all | solution.py:22
  50.7 4.8 %all-to-all-start.3 = ((bf16[128,16,256]{2,0,1:T(8,128)(2,1)}), bf16[128,16,256]{2,0,1:T(8,128)(2,1)}, u32[]{:S(2)}, u32[]{:S(2)}) async-start(bf16[128,16,256]{2,0,1:T(8,128)(2,1)} %bitcast.70), calls=%async_computation.3 | async-start | bytes 2097152 | tf_op jit(solution)/shard_map/all_to_all | solution.py:23
  55.5 5.3 %exponential_select_fusion = (f32[2,1024,2]{2,0,1:T(2,128)}, f32[2,1024,2]{2,0,1:T(2,128)}) fusion(pred[2,1024]{0,1:T(8,128)(4,1)S(1)} %copy.127, f32[2,2]{1,0:T(2,128)S(1)} %slice_bitcast_fusion, f32[2,2,1024]{1,0,2:T(2,128)S(1)} %copy.119, pred[2,1024]{0,1:T(8,128)(4,1)S(1)} %copy.120), kind=kLoop, calls=%fused_computation.26 | loop fusion | flops 12288 | bytes 53264 | tf_op jit(solution)/shard_map/jit(_where)/select_n | solution.py:57
  60.9 2.0 copy.128
  64.6 2.2 reshape.177
  66.7 3.1 all-to-all-done.3
  69.8 2.1 reshape.179
  71.9 5.3 %multiply_convert_fusion.2 = bf16[2,1024,2,128]{3,2,1,0:T(2,128)(2,1)S(1)} fusion(bf16[2,1024,2,128]{3,2,1,0:T(2,128)(2,1)S(1)} %reshape.178, f32[2,1024,2]{2,1,0:T(8,128)S(1)} %copy.121), kind=kLoop, calls=%fused_computation.19 | loop fusion | flops 1572864 | bytes 2113536 | tf_op jit(solution)/shard_map/convert_element_type | solution.py:66
  78.1 238.8 %while.43 = (s32[]{:T(128)}, f32[2,128,128]{2,1,0:T(8,128)S(1)}, f32[2]{0:T(128)S(1)}, f32[2,128,128]{2,1,0:T(8,128)S(1)}, s32[]{:T(128)}) while((s32[]{:T(128)}, f32[2,128,128]{2,1,0:T(8,128)S(1)}, f32[2]{0:T(128)S(1)}, f32[2,128,128]{2,1,0:T(8,128)S(1)}, s32[]{:T(128)}) %tuple.88), condition=%wide.region_8.9_spmd, body=%wide.region_7.8_spmd.sunk | while | flops 65538 | bytes 917613 | solution.py:86
  78.2 5.9 %collective-permute-start = (f32[2,128,128]{2,1,0:T(8,128)S(1)}, f32[2,128,128]{2,1,0:T(8,128)S(1)}, u32[]{:S(2)}, u32[]{:S(2)}) collective-permute-start(f32[2,128,128]{2,1,0:T(8,128)S(1)} %multiply_add_fusion.2), channel_id=1, source_target_pairs={{16,0},{32,16},{48,32},{64,48},{80,64},{96,80},{112,96},{128,112},... | collective-permute-start | bytes 393224 | tf_op jit(solution)/shard_map/while/body/eval_jaxpr/ppermute | solution.py:10
  84.1 5.4 %collective-permute-done = f32[2,128,128]{2,1,0:T(8,128)S(1)} collective-permute-done((f32[2,128,128]{2,1,0:T(8,128)S(1)}, f32[2,128,128]{2,1,0:T(8,128)S(1)}, u32[]{:S(2)}, u32[]{:S(2)}) %collective-permute-start) | collective-permute-done | bytes 131104 | tf_op jit(solution)/shard_map/while/body/eval_jaxpr/ppermute | solution.py:10
  89.5 1.9 collective-permute-start
  91.5 5.6 %collective-permute-done = f32[2,128,128]{2,1,0:T(8,128)S(1)} collective-permute-done((f32[2,128,128]{2,1,0:T(8,128)S(1)}, f32[2,128,128]{2,1,0:T(8,128)S(1)}, u32[]{:S(2)}, u32[]{:S(2)}) %collective-permute-start) | collective-permute-done | bytes 131104 | tf_op jit(solution)/shard_map/while/body/eval_jaxpr/ppermute | solution.py:10
  97.1 1.9 collective-permute-start
  99.1 5.6 %collective-permute-done = f32[2,128,128]{2,1,0:T(8,128)S(1)} collective-permute-done((f32[2,128,128]{2,1,0:T(8,128)S(1)}, f32[2,128,128]{2,1,0:T(8,128)S(1)}, u32[]{:S(2)}, u32[]{:S(2)}) %collective-permute-start) | collective-permute-done | bytes 131104 | tf_op jit(solution)/shard_map/while/body/eval_jaxpr/ppermute | solution.py:10
  106.6 5.6 %collective-permute-done = f32[2,128,128]{2,1,0:T(8,128)S(1)} collective-permute-done((f32[2,128,128]{2,1,0:T(8,128)S(1)}, f32[2,128,128]{2,1,0:T(8,128)S(1)}, u32[]{:S(2)}, u32[]{:S(2)}) %collective-permute-start) | collective-permute-done | bytes 131104 | tf_op jit(solution)/shard_map/while/body/eval_jaxpr/ppermute | solution.py:10
  114.2 5.6 %collective-permute-done = f32[2,128,128]{2,1,0:T(8,128)S(1)} collective-permute-done((f32[2,128,128]{2,1,0:T(8,128)S(1)}, f32[2,128,128]{2,1,0:T(8,128)S(1)}, u32[]{:S(2)}, u32[]{:S(2)}) %collective-permute-start) | collective-permute-done | bytes 131104 | tf_op jit(solution)/shard_map/while/body/eval_jaxpr/ppermute | solution.py:10
  121.8 5.6 %collective-permute-done = f32[2,128,128]{2,1,0:T(8,128)S(1)} collective-permute-done((f32[2,128,128]{2,1,0:T(8,128)S(1)}, f32[2,128,128]{2,1,0:T(8,128)S(1)}, u32[]{:S(2)}, u32[]{:S(2)}) %collective-permute-start) | collective-permute-done | bytes 131104 | tf_op jit(solution)/shard_map/while/body/eval_jaxpr/ppermute | solution.py:10
  129.4 5.6 %collective-permute-done = f32[2,128,128]{2,1,0:T(8,128)S(1)} collective-permute-done((f32[2,128,128]{2,1,0:T(8,128)S(1)}, f32[2,128,128]{2,1,0:T(8,128)S(1)}, u32[]{:S(2)}, u32[]{:S(2)}) %collective-permute-start) | collective-permute-done | bytes 131104 | tf_op jit(solution)/shard_map/while/body/eval_jaxpr/ppermute | solution.py:10
  137.0 5.6 %collective-permute-done = f32[2,128,128]{2,1,0:T(8,128)S(1)} collective-permute-done((f32[2,128,128]{2,1,0:T(8,128)S(1)}, f32[2,128,128]{2,1,0:T(8,128)S(1)}, u32[]{:S(2)}, u32[]{:S(2)}) %collective-permute-start) | collective-permute-done | bytes 131104 | tf_op jit(solution)/shard_map/while/body/eval_jaxpr/ppermute | solution.py:10
  144.5 5.6 %collective-permute-done = f32[2,128,128]{2,1,0:T(8,128)S(1)} collective-permute-done((f32[2,128,128]{2,1,0:T(8,128)S(1)}, f32[2,128,128]{2,1,0:T(8,128)S(1)}, u32[]{:S(2)}, u32[]{:S(2)}) %collective-permute-start) | collective-permute-done | bytes 131104 | tf_op jit(solution)/shard_map/while/body/eval_jaxpr/ppermute | solution.py:10
  150.2 1.9 collective-permute-start
  152.1 5.6 %collective-permute-done = f32[2,128,128]{2,1,0:T(8,128)S(1)} collective-permute-done((f32[2,128,128]{2,1,0:T(8,128)S(1)}, f32[2,128,128]{2,1,0:T(8,128)S(1)}, u32[]{:S(2)}, u32[]{:S(2)}) %collective-permute-start) | collective-permute-done | bytes 131104 | tf_op jit(solution)/shard_map/while/body/eval_jaxpr/ppermute | solution.py:10
  157.8 1.9 collective-permute-start
  159.7 5.6 %collective-permute-done = f32[2,128,128]{2,1,0:T(8,128)S(1)} collective-permute-done((f32[2,128,128]{2,1,0:T(8,128)S(1)}, f32[2,128,128]{2,1,0:T(8,128)S(1)}, u32[]{:S(2)}, u32[]{:S(2)}) %collective-permute-start) | collective-permute-done | bytes 131104 | tf_op jit(solution)/shard_map/while/body/eval_jaxpr/ppermute | solution.py:10
  165.4 1.9 collective-permute-start
  167.3 5.6 %collective-permute-done = f32[2,128,128]{2,1,0:T(8,128)S(1)} collective-permute-done((f32[2,128,128]{2,1,0:T(8,128)S(1)}, f32[2,128,128]{2,1,0:T(8,128)S(1)}, u32[]{:S(2)}, u32[]{:S(2)}) %collective-permute-start) | collective-permute-done | bytes 131104 | tf_op jit(solution)/shard_map/while/body/eval_jaxpr/ppermute | solution.py:10
  172.9 1.9 collective-permute-start
  174.9 5.6 %collective-permute-done = f32[2,128,128]{2,1,0:T(8,128)S(1)} collective-permute-done((f32[2,128,128]{2,1,0:T(8,128)S(1)}, f32[2,128,128]{2,1,0:T(8,128)S(1)}, u32[]{:S(2)}, u32[]{:S(2)}) %collective-permute-start) | collective-permute-done | bytes 131104 | tf_op jit(solution)/shard_map/while/body/eval_jaxpr/ppermute | solution.py:10
  180.5 1.9 collective-permute-start
  182.5 5.6 %collective-permute-done = f32[2,128,128]{2,1,0:T(8,128)S(1)} collective-permute-done((f32[2,128,128]{2,1,0:T(8,128)S(1)}, f32[2,128,128]{2,1,0:T(8,128)S(1)}, u32[]{:S(2)}, u32[]{:S(2)}) %collective-permute-start) | collective-permute-done | bytes 131104 | tf_op jit(solution)/shard_map/while/body/eval_jaxpr/ppermute | solution.py:10
  188.1 1.9 collective-permute-start
  190.0 5.6 %collective-permute-done = f32[2,128,128]{2,1,0:T(8,128)S(1)} collective-permute-done((f32[2,128,128]{2,1,0:T(8,128)S(1)}, f32[2,128,128]{2,1,0:T(8,128)S(1)}, u32[]{:S(2)}, u32[]{:S(2)}) %collective-permute-start) | collective-permute-done | bytes 131104 | tf_op jit(solution)/shard_map/while/body/eval_jaxpr/ppermute | solution.py:10
  197.6 5.6 %collective-permute-done = f32[2,128,128]{2,1,0:T(8,128)S(1)} collective-permute-done((f32[2,128,128]{2,1,0:T(8,128)S(1)}, f32[2,128,128]{2,1,0:T(8,128)S(1)}, u32[]{:S(2)}, u32[]{:S(2)}) %collective-permute-start) | collective-permute-done | bytes 131104 | tf_op jit(solution)/shard_map/while/body/eval_jaxpr/ppermute | solution.py:10
  205.2 5.6 %collective-permute-done = f32[2,128,128]{2,1,0:T(8,128)S(1)} collective-permute-done((f32[2,128,128]{2,1,0:T(8,128)S(1)}, f32[2,128,128]{2,1,0:T(8,128)S(1)}, u32[]{:S(2)}, u32[]{:S(2)}) %collective-permute-start) | collective-permute-done | bytes 131104 | tf_op jit(solution)/shard_map/while/body/eval_jaxpr/ppermute | solution.py:10
  212.8 5.6 %collective-permute-done = f32[2,128,128]{2,1,0:T(8,128)S(1)} collective-permute-done((f32[2,128,128]{2,1,0:T(8,128)S(1)}, f32[2,128,128]{2,1,0:T(8,128)S(1)}, u32[]{:S(2)}, u32[]{:S(2)}) %collective-permute-start) | collective-permute-done | bytes 131104 | tf_op jit(solution)/shard_map/while/body/eval_jaxpr/ppermute | solution.py:10
  220.4 5.6 %collective-permute-done = f32[2,128,128]{2,1,0:T(8,128)S(1)} collective-permute-done((f32[2,128,128]{2,1,0:T(8,128)S(1)}, f32[2,128,128]{2,1,0:T(8,128)S(1)}, u32[]{:S(2)}, u32[]{:S(2)}) %collective-permute-start) | collective-permute-done | bytes 131104 | tf_op jit(solution)/shard_map/while/body/eval_jaxpr/ppermute | solution.py:10
  227.9 5.6 %collective-permute-done = f32[2,128,128]{2,1,0:T(8,128)S(1)} collective-permute-done((f32[2,128,128]{2,1,0:T(8,128)S(1)}, f32[2,128,128]{2,1,0:T(8,128)S(1)}, u32[]{:S(2)}, u32[]{:S(2)}) %collective-permute-start) | collective-permute-done | bytes 131104 | tf_op jit(solution)/shard_map/while/body/eval_jaxpr/ppermute | solution.py:10
  235.5 5.6 %collective-permute-done = f32[2,128,128]{2,1,0:T(8,128)S(1)} collective-permute-done((f32[2,128,128]{2,1,0:T(8,128)S(1)}, f32[2,128,128]{2,1,0:T(8,128)S(1)}, u32[]{:S(2)}, u32[]{:S(2)}) %collective-permute-start) | collective-permute-done | bytes 131104 | tf_op jit(solution)/shard_map/while/body/eval_jaxpr/ppermute | solution.py:10
  243.1 5.6 %collective-permute-done = f32[2,128,128]{2,1,0:T(8,128)S(1)} collective-permute-done((f32[2,128,128]{2,1,0:T(8,128)S(1)}, f32[2,128,128]{2,1,0:T(8,128)S(1)}, u32[]{:S(2)}, u32[]{:S(2)}) %collective-permute-start) | collective-permute-done | bytes 131104 | tf_op jit(solution)/shard_map/while/body/eval_jaxpr/ppermute | solution.py:10
  250.7 5.6 %collective-permute-done = f32[2,128,128]{2,1,0:T(8,128)S(1)} collective-permute-done((f32[2,128,128]{2,1,0:T(8,128)S(1)}, f32[2,128,128]{2,1,0:T(8,128)S(1)}, u32[]{:S(2)}, u32[]{:S(2)}) %collective-permute-start) | collective-permute-done | bytes 131104 | tf_op jit(solution)/shard_map/while/body/eval_jaxpr/ppermute | solution.py:10
  258.3 5.6 %collective-permute-done = f32[2,128,128]{2,1,0:T(8,128)S(1)} collective-permute-done((f32[2,128,128]{2,1,0:T(8,128)S(1)}, f32[2,128,128]{2,1,0:T(8,128)S(1)}, u32[]{:S(2)}, u32[]{:S(2)}) %collective-permute-start) | collective-permute-done | bytes 131104 | tf_op jit(solution)/shard_map/while/body/eval_jaxpr/ppermute | solution.py:10
  265.9 5.6 %collective-permute-done = f32[2,128,128]{2,1,0:T(8,128)S(1)} collective-permute-done((f32[2,128,128]{2,1,0:T(8,128)S(1)}, f32[2,128,128]{2,1,0:T(8,128)S(1)}, u32[]{:S(2)}, u32[]{:S(2)}) %collective-permute-start) | collective-permute-done | bytes 131104 | tf_op jit(solution)/shard_map/while/body/eval_jaxpr/ppermute | solution.py:10
  273.4 5.6 %collective-permute-done = f32[2,128,128]{2,1,0:T(8,128)S(1)} collective-permute-done((f32[2,128,128]{2,1,0:T(8,128)S(1)}, f32[2,128,128]{2,1,0:T(8,128)S(1)}, u32[]{:S(2)}, u32[]{:S(2)}) %collective-permute-start) | collective-permute-done | bytes 131104 | tf_op jit(solution)/shard_map/while/body/eval_jaxpr/ppermute | solution.py:10
  281.0 5.6 %collective-permute-done = f32[2,128,128]{2,1,0:T(8,128)S(1)} collective-permute-done((f32[2,128,128]{2,1,0:T(8,128)S(1)}, f32[2,128,128]{2,1,0:T(8,128)S(1)}, u32[]{:S(2)}, u32[]{:S(2)}) %collective-permute-start) | collective-permute-done | bytes 131104 | tf_op jit(solution)/shard_map/while/body/eval_jaxpr/ppermute | solution.py:10
  288.6 5.6 %collective-permute-done = f32[2,128,128]{2,1,0:T(8,128)S(1)} collective-permute-done((f32[2,128,128]{2,1,0:T(8,128)S(1)}, f32[2,128,128]{2,1,0:T(8,128)S(1)}, u32[]{:S(2)}, u32[]{:S(2)}) %collective-permute-start) | collective-permute-done | bytes 131104 | tf_op jit(solution)/shard_map/while/body/eval_jaxpr/ppermute | solution.py:10
  294.2 1.9 collective-permute-start
  296.2 5.6 %collective-permute-done = f32[2,128,128]{2,1,0:T(8,128)S(1)} collective-permute-done((f32[2,128,128]{2,1,0:T(8,128)S(1)}, f32[2,128,128]{2,1,0:T(8,128)S(1)}, u32[]{:S(2)}, u32[]{:S(2)}) %collective-permute-start) | collective-permute-done | bytes 131104 | tf_op jit(solution)/shard_map/while/body/eval_jaxpr/ppermute | solution.py:10
  301.8 1.9 collective-permute-start
  303.8 5.6 %collective-permute-done = f32[2,128,128]{2,1,0:T(8,128)S(1)} collective-permute-done((f32[2,128,128]{2,1,0:T(8,128)S(1)}, f32[2,128,128]{2,1,0:T(8,128)S(1)}, u32[]{:S(2)}, u32[]{:S(2)}) %collective-permute-start) | collective-permute-done | bytes 131104 | tf_op jit(solution)/shard_map/while/body/eval_jaxpr/ppermute | solution.py:10
  309.4 1.9 collective-permute-start
  311.3 5.6 %collective-permute-done = f32[2,128,128]{2,1,0:T(8,128)S(1)} collective-permute-done((f32[2,128,128]{2,1,0:T(8,128)S(1)}, f32[2,128,128]{2,1,0:T(8,128)S(1)}, u32[]{:S(2)}, u32[]{:S(2)}) %collective-permute-start) | collective-permute-done | bytes 131104 | tf_op jit(solution)/shard_map/while/body/eval_jaxpr/ppermute | solution.py:10
  319.2 3.3 fusion.14
  322.5 9.3 %fusion.7 = bf16[2,1024,2,128]{3,1,2,0:T(8,128)(2,1)} fusion(f32[2,2,128,1024]{2,3,1,0:T(8,128)} %fusion.14, f32[2,2,1024]{2,1,0:T(2,128)S(1)} %reduce_window_sum.31, pred[2,1024,1024]{2,1,0:T(8,128)(4,1)} %compare_and_fusion, bf16[2,1024,2,128]{3,2,1,0:T(2,128)(2,1)S(1)} %reshape.178, f32[2,1024,2]{1,2,0:T(2,128)S(1)} %copy-done.6, ...), kind=kOutput, calls=%fused_computation.18 | convolution fusion | flops 2170028032 | bytes 8421376 | tf_op jit(solution)/shard_map/bhit,bthe->bihe/dot_general | solution.py:54
  331.8 2.3 copy.129
  334.8 17.0 %all_to_all.80 = bf16[16,128,256]{2,1,0:T(8,128)(2,1)S(1)} all-to-all(bf16[16,128,256]{2,1,0:T(8,128)(2,1)S(1)} %all_to_all.71), channel_id=1, replica_groups=mesh['seq'=32,'head'=16] {'head'}, dimensions={0} | all-to-all | bytes 2097152 | tf_op jit(solution)/shard_map/all_to_all | solution.py:103
  (114 shorter events, 55.4 us)
Async XLA Ops:
  0.0 13.1 %all-to-all-start = ((bf16[128,16,2]{0,2,1:T(2,128)(2,1)}), bf16[128,16,2]{0,2,1:T(2,128)(2,1)S(1)}, u32[]{:S(2)}, u32[]{:S(2)}) async-start(bf16[128,16,2]{0,2,1:T(2,128)(2,1)} %bitcast.78), calls=%async_computation | async-start | bytes 16384 | tf_op jit(solution)/shard_map/all_to_all | solution.py:24
  6.8 10.1 %copy-start.8 = (s32[8]{0:T(128)S(1)}, s32[8]{0:T(128)}, u32[]{:S(2)}) copy-start(s32[8]{0:T(128)} %param.15) | copy-start | bytes 100
  6.8 10.6 %copy-start.2 = (bf16[128,4096]{1,0:T(8,128)(2,1)S(1)}, bf16[128,4096]{1,0:T(8,128)(2,1)}, u32[]{:S(2)}) copy-start(bf16[128,4096]{1,0:T(8,128)(2,1)} %param.12) | copy-start | bytes 3145732
  13.1 18.5 %all-to-all-start.2 = ((bf16[128,16,256]{2,0,1:T(8,128)(2,1)}), bf16[128,16,256]{2,0,1:T(8,128)(2,1)S(1)}, u32[]{:S(2)}, u32[]{:S(2)}) async-start(bf16[128,16,256]{2,0,1:T(8,128)(2,1)} %bitcast.54), calls=%async_computation.2 | async-start | bytes 2097152 | tf_op jit(solution)/shard_map/all_to_all | solution.py:21
  31.6 19.2 %all-to-all-start.1 = ((bf16[128,16,256]{2,0,1:T(8,128)(2,1)}), bf16[128,16,256]{2,0,1:T(8,128)(2,1)S(1)}, u32[]{:S(2)}, u32[]{:S(2)}) async-start(bf16[128,16,256]{2,0,1:T(8,128)(2,1)} %bitcast.69), calls=%async_computation.1 | async-start | bytes 2097152 | tf_op jit(solution)/shard_map/all_to_all | solution.py:22
  50.7 10.2 %copy-start.1 = (bf16[128,16,256]{2,0,1:T(8,128)(2,1)}, bf16[128,16,256]{2,0,1:T(8,128)(2,1)S(1)}, u32[]{:S(2)}) copy-start(bf16[128,16,256]{2,0,1:T(8,128)(2,1)S(1)} %all-to-all-done.1) | copy-start | bytes 3145732
  50.7 19.1 %all-to-all-start.3 = ((bf16[128,16,256]{2,0,1:T(8,128)(2,1)}), bf16[128,16,256]{2,0,1:T(8,128)(2,1)}, u32[]{:S(2)}, u32[]{:S(2)}) async-start(bf16[128,16,256]{2,0,1:T(8,128)(2,1)} %bitcast.70), calls=%async_computation.3 | async-start | bytes 2097152 | tf_op jit(solution)/shard_map/all_to_all | solution.py:23
  60.9 3.3 copy-start.7
  71.9 5.3 %copy-start.3 = (bf16[2,1024,2,128]{3,2,1,0:T(2,128)(2,1)S(1)}, bf16[2,1024,2,128]{3,2,1,0:T(2,128)(2,1)}, u32[]{:S(2)}) copy-start(bf16[2,1024,2,128]{3,2,1,0:T(2,128)(2,1)} %reshape.179) | copy-start | bytes 3145732
  77.3 0.6 copy-start.5
  78.1 241.1 %copy-start = (bf16[2,1024,2,128]{3,2,1,0:T(2,128)(2,1)S(1)}, bf16[2,1024,2,128]{3,2,1,0:T(2,128)(2,1)}, u32[]{:S(2)}) copy-start(bf16[2,1024,2,128]{3,2,1,0:T(2,128)(2,1)} %reshape.177) | copy-start | bytes 3145732
  78.2 11.2 %collective-permute-start = (f32[2,128,128]{2,1,0:T(8,128)S(1)}, f32[2,128,128]{2,1,0:T(8,128)S(1)}, u32[]{:S(2)}, u32[]{:S(2)}) collective-permute-start(f32[2,128,128]{2,1,0:T(8,128)S(1)} %multiply_add_fusion.2), channel_id=1, source_target_pairs={{16,0},{32,16},{48,32},{64,48},{80,64},{96,80},{112,96},{128,112},... | collective-permute-start | bytes 393224 | tf_op jit(solution)/shard_map/while/body/eval_jaxpr/ppermute | solution.py:10
  89.5 7.5 %collective-permute-start = (f32[2,128,128]{2,1,0:T(8,128)S(1)}, f32[2,128,128]{2,1,0:T(8,128)S(1)}, u32[]{:S(2)}, u32[]{:S(2)}) collective-permute-start(f32[2,128,128]{2,1,0:T(8,128)S(1)} %multiply_add_fusion.2), channel_id=1, source_target_pairs={{16,0},{32,16},{48,32},{64,48},{80,64},{96,80},{112,96},{128,112},... | collective-permute-start | bytes 393224 | tf_op jit(solution)/shard_map/while/body/eval_jaxpr/ppermute | solution.py:10
  97.1 7.5 %collective-permute-start = (f32[2,128,128]{2,1,0:T(8,128)S(1)}, f32[2,128,128]{2,1,0:T(8,128)S(1)}, u32[]{:S(2)}, u32[]{:S(2)}) collective-permute-start(f32[2,128,128]{2,1,0:T(8,128)S(1)} %multiply_add_fusion.2), channel_id=1, source_target_pairs={{16,0},{32,16},{48,32},{64,48},{80,64},{96,80},{112,96},{128,112},... | collective-permute-start | bytes 393224 | tf_op jit(solution)/shard_map/while/body/eval_jaxpr/ppermute | solution.py:10
  104.7 7.5 %collective-permute-start = (f32[2,128,128]{2,1,0:T(8,128)S(1)}, f32[2,128,128]{2,1,0:T(8,128)S(1)}, u32[]{:S(2)}, u32[]{:S(2)}) collective-permute-start(f32[2,128,128]{2,1,0:T(8,128)S(1)} %multiply_add_fusion.2), channel_id=1, source_target_pairs={{16,0},{32,16},{48,32},{64,48},{80,64},{96,80},{112,96},{128,112},... | collective-permute-start | bytes 393224 | tf_op jit(solution)/shard_map/while/body/eval_jaxpr/ppermute | solution.py:10
  112.3 7.5 %collective-permute-start = (f32[2,128,128]{2,1,0:T(8,128)S(1)}, f32[2,128,128]{2,1,0:T(8,128)S(1)}, u32[]{:S(2)}, u32[]{:S(2)}) collective-permute-start(f32[2,128,128]{2,1,0:T(8,128)S(1)} %multiply_add_fusion.2), channel_id=1, source_target_pairs={{16,0},{32,16},{48,32},{64,48},{80,64},{96,80},{112,96},{128,112},... | collective-permute-start | bytes 393224 | tf_op jit(solution)/shard_map/while/body/eval_jaxpr/ppermute | solution.py:10
  119.9 7.5 %collective-permute-start = (f32[2,128,128]{2,1,0:T(8,128)S(1)}, f32[2,128,128]{2,1,0:T(8,128)S(1)}, u32[]{:S(2)}, u32[]{:S(2)}) collective-permute-start(f32[2,128,128]{2,1,0:T(8,128)S(1)} %multiply_add_fusion.2), channel_id=1, source_target_pairs={{16,0},{32,16},{48,32},{64,48},{80,64},{96,80},{112,96},{128,112},... | collective-permute-start | bytes 393224 | tf_op jit(solution)/shard_map/while/body/eval_jaxpr/ppermute | solution.py:10
  127.5 7.5 %collective-permute-start = (f32[2,128,128]{2,1,0:T(8,128)S(1)}, f32[2,128,128]{2,1,0:T(8,128)S(1)}, u32[]{:S(2)}, u32[]{:S(2)}) collective-permute-start(f32[2,128,128]{2,1,0:T(8,128)S(1)} %multiply_add_fusion.2), channel_id=1, source_target_pairs={{16,0},{32,16},{48,32},{64,48},{80,64},{96,80},{112,96},{128,112},... | collective-permute-start | bytes 393224 | tf_op jit(solution)/shard_map/while/body/eval_jaxpr/ppermute | solution.py:10
  135.0 7.5 %collective-permute-start = (f32[2,128,128]{2,1,0:T(8,128)S(1)}, f32[2,128,128]{2,1,0:T(8,128)S(1)}, u32[]{:S(2)}, u32[]{:S(2)}) collective-permute-start(f32[2,128,128]{2,1,0:T(8,128)S(1)} %multiply_add_fusion.2), channel_id=1, source_target_pairs={{16,0},{32,16},{48,32},{64,48},{80,64},{96,80},{112,96},{128,112},... | collective-permute-start | bytes 393224 | tf_op jit(solution)/shard_map/while/body/eval_jaxpr/ppermute | solution.py:10
  142.6 7.5 %collective-permute-start = (f32[2,128,128]{2,1,0:T(8,128)S(1)}, f32[2,128,128]{2,1,0:T(8,128)S(1)}, u32[]{:S(2)}, u32[]{:S(2)}) collective-permute-start(f32[2,128,128]{2,1,0:T(8,128)S(1)} %multiply_add_fusion.2), channel_id=1, source_target_pairs={{16,0},{32,16},{48,32},{64,48},{80,64},{96,80},{112,96},{128,112},... | collective-permute-start | bytes 393224 | tf_op jit(solution)/shard_map/while/body/eval_jaxpr/ppermute | solution.py:10
  150.2 7.5 %collective-permute-start = (f32[2,128,128]{2,1,0:T(8,128)S(1)}, f32[2,128,128]{2,1,0:T(8,128)S(1)}, u32[]{:S(2)}, u32[]{:S(2)}) collective-permute-start(f32[2,128,128]{2,1,0:T(8,128)S(1)} %multiply_add_fusion.2), channel_id=1, source_target_pairs={{16,0},{32,16},{48,32},{64,48},{80,64},{96,80},{112,96},{128,112},... | collective-permute-start | bytes 393224 | tf_op jit(solution)/shard_map/while/body/eval_jaxpr/ppermute | solution.py:10
  157.8 7.5 %collective-permute-start = (f32[2,128,128]{2,1,0:T(8,128)S(1)}, f32[2,128,128]{2,1,0:T(8,128)S(1)}, u32[]{:S(2)}, u32[]{:S(2)}) collective-permute-start(f32[2,128,128]{2,1,0:T(8,128)S(1)} %multiply_add_fusion.2), channel_id=1, source_target_pairs={{16,0},{32,16},{48,32},{64,48},{80,64},{96,80},{112,96},{128,112},... | collective-permute-start | bytes 393224 | tf_op jit(solution)/shard_map/while/body/eval_jaxpr/ppermute | solution.py:10
  165.4 7.5 %collective-permute-start = (f32[2,128,128]{2,1,0:T(8,128)S(1)}, f32[2,128,128]{2,1,0:T(8,128)S(1)}, u32[]{:S(2)}, u32[]{:S(2)}) collective-permute-start(f32[2,128,128]{2,1,0:T(8,128)S(1)} %multiply_add_fusion.2), channel_id=1, source_target_pairs={{16,0},{32,16},{48,32},{64,48},{80,64},{96,80},{112,96},{128,112},... | collective-permute-start | bytes 393224 | tf_op jit(solution)/shard_map/while/body/eval_jaxpr/ppermute | solution.py:10
  172.9 7.5 %collective-permute-start = (f32[2,128,128]{2,1,0:T(8,128)S(1)}, f32[2,128,128]{2,1,0:T(8,128)S(1)}, u32[]{:S(2)}, u32[]{:S(2)}) collective-permute-start(f32[2,128,128]{2,1,0:T(8,128)S(1)} %multiply_add_fusion.2), channel_id=1, source_target_pairs={{16,0},{32,16},{48,32},{64,48},{80,64},{96,80},{112,96},{128,112},... | collective-permute-start | bytes 393224 | tf_op jit(solution)/shard_map/while/body/eval_jaxpr/ppermute | solution.py:10
  180.5 7.5 %collective-permute-start = (f32[2,128,128]{2,1,0:T(8,128)S(1)}, f32[2,128,128]{2,1,0:T(8,128)S(1)}, u32[]{:S(2)}, u32[]{:S(2)}) collective-permute-start(f32[2,128,128]{2,1,0:T(8,128)S(1)} %multiply_add_fusion.2), channel_id=1, source_target_pairs={{16,0},{32,16},{48,32},{64,48},{80,64},{96,80},{112,96},{128,112},... | collective-permute-start | bytes 393224 | tf_op jit(solution)/shard_map/while/body/eval_jaxpr/ppermute | solution.py:10
  188.1 7.5 %collective-permute-start = (f32[2,128,128]{2,1,0:T(8,128)S(1)}, f32[2,128,128]{2,1,0:T(8,128)S(1)}, u32[]{:S(2)}, u32[]{:S(2)}) collective-permute-start(f32[2,128,128]{2,1,0:T(8,128)S(1)} %multiply_add_fusion.2), channel_id=1, source_target_pairs={{16,0},{32,16},{48,32},{64,48},{80,64},{96,80},{112,96},{128,112},... | collective-permute-start | bytes 393224 | tf_op jit(solution)/shard_map/while/body/eval_jaxpr/ppermute | solution.py:10
  195.7 7.5 %collective-permute-start = (f32[2,128,128]{2,1,0:T(8,128)S(1)}, f32[2,128,128]{2,1,0:T(8,128)S(1)}, u32[]{:S(2)}, u32[]{:S(2)}) collective-permute-start(f32[2,128,128]{2,1,0:T(8,128)S(1)} %multiply_add_fusion.2), channel_id=1, source_target_pairs={{16,0},{32,16},{48,32},{64,48},{80,64},{96,80},{112,96},{128,112},... | collective-permute-start | bytes 393224 | tf_op jit(solution)/shard_map/while/body/eval_jaxpr/ppermute | solution.py:10
  203.3 7.5 %collective-permute-start = (f32[2,128,128]{2,1,0:T(8,128)S(1)}, f32[2,128,128]{2,1,0:T(8,128)S(1)}, u32[]{:S(2)}, u32[]{:S(2)}) collective-permute-start(f32[2,128,128]{2,1,0:T(8,128)S(1)} %multiply_add_fusion.2), channel_id=1, source_target_pairs={{16,0},{32,16},{48,32},{64,48},{80,64},{96,80},{112,96},{128,112},... | collective-permute-start | bytes 393224 | tf_op jit(solution)/shard_map/while/body/eval_jaxpr/ppermute | solution.py:10
  210.9 7.5 %collective-permute-start = (f32[2,128,128]{2,1,0:T(8,128)S(1)}, f32[2,128,128]{2,1,0:T(8,128)S(1)}, u32[]{:S(2)}, u32[]{:S(2)}) collective-permute-start(f32[2,128,128]{2,1,0:T(8,128)S(1)} %multiply_add_fusion.2), channel_id=1, source_target_pairs={{16,0},{32,16},{48,32},{64,48},{80,64},{96,80},{112,96},{128,112},... | collective-permute-start | bytes 393224 | tf_op jit(solution)/shard_map/while/body/eval_jaxpr/ppermute | solution.py:10
  218.4 7.5 %collective-permute-start = (f32[2,128,128]{2,1,0:T(8,128)S(1)}, f32[2,128,128]{2,1,0:T(8,128)S(1)}, u32[]{:S(2)}, u32[]{:S(2)}) collective-permute-start(f32[2,128,128]{2,1,0:T(8,128)S(1)} %multiply_add_fusion.2), channel_id=1, source_target_pairs={{16,0},{32,16},{48,32},{64,48},{80,64},{96,80},{112,96},{128,112},... | collective-permute-start | bytes 393224 | tf_op jit(solution)/shard_map/while/body/eval_jaxpr/ppermute | solution.py:10
  226.0 7.5 %collective-permute-start = (f32[2,128,128]{2,1,0:T(8,128)S(1)}, f32[2,128,128]{2,1,0:T(8,128)S(1)}, u32[]{:S(2)}, u32[]{:S(2)}) collective-permute-start(f32[2,128,128]{2,1,0:T(8,128)S(1)} %multiply_add_fusion.2), channel_id=1, source_target_pairs={{16,0},{32,16},{48,32},{64,48},{80,64},{96,80},{112,96},{128,112},... | collective-permute-start | bytes 393224 | tf_op jit(solution)/shard_map/while/body/eval_jaxpr/ppermute | solution.py:10
  233.6 7.5 %collective-permute-start = (f32[2,128,128]{2,1,0:T(8,128)S(1)}, f32[2,128,128]{2,1,0:T(8,128)S(1)}, u32[]{:S(2)}, u32[]{:S(2)}) collective-permute-start(f32[2,128,128]{2,1,0:T(8,128)S(1)} %multiply_add_fusion.2), channel_id=1, source_target_pairs={{16,0},{32,16},{48,32},{64,48},{80,64},{96,80},{112,96},{128,112},... | collective-permute-start | bytes 393224 | tf_op jit(solution)/shard_map/while/body/eval_jaxpr/ppermute | solution.py:10
  241.2 7.5 %collective-permute-start = (f32[2,128,128]{2,1,0:T(8,128)S(1)}, f32[2,128,128]{2,1,0:T(8,128)S(1)}, u32[]{:S(2)}, u32[]{:S(2)}) collective-permute-start(f32[2,128,128]{2,1,0:T(8,128)S(1)} %multiply_add_fusion.2), channel_id=1, source_target_pairs={{16,0},{32,16},{48,32},{64,48},{80,64},{96,80},{112,96},{128,112},... | collective-permute-start | bytes 393224 | tf_op jit(solution)/shard_map/while/body/eval_jaxpr/ppermute | solution.py:10
  248.8 7.5 %collective-permute-start = (f32[2,128,128]{2,1,0:T(8,128)S(1)}, f32[2,128,128]{2,1,0:T(8,128)S(1)}, u32[]{:S(2)}, u32[]{:S(2)}) collective-permute-start(f32[2,128,128]{2,1,0:T(8,128)S(1)} %multiply_add_fusion.2), channel_id=1, source_target_pairs={{16,0},{32,16},{48,32},{64,48},{80,64},{96,80},{112,96},{128,112},... | collective-permute-start | bytes 393224 | tf_op jit(solution)/shard_map/while/body/eval_jaxpr/ppermute | solution.py:10
  256.3 7.5 %collective-permute-start = (f32[2,128,128]{2,1,0:T(8,128)S(1)}, f32[2,128,128]{2,1,0:T(8,128)S(1)}, u32[]{:S(2)}, u32[]{:S(2)}) collective-permute-start(f32[2,128,128]{2,1,0:T(8,128)S(1)} %multiply_add_fusion.2), channel_id=1, source_target_pairs={{16,0},{32,16},{48,32},{64,48},{80,64},{96,80},{112,96},{128,112},... | collective-permute-start | bytes 393224 | tf_op jit(solution)/shard_map/while/body/eval_jaxpr/ppermute | solution.py:10
  263.9 7.5 %collective-permute-start = (f32[2,128,128]{2,1,0:T(8,128)S(1)}, f32[2,128,128]{2,1,0:T(8,128)S(1)}, u32[]{:S(2)}, u32[]{:S(2)}) collective-permute-start(f32[2,128,128]{2,1,0:T(8,128)S(1)} %multiply_add_fusion.2), channel_id=1, source_target_pairs={{16,0},{32,16},{48,32},{64,48},{80,64},{96,80},{112,96},{128,112},... | collective-permute-start | bytes 393224 | tf_op jit(solution)/shard_map/while/body/eval_jaxpr/ppermute | solution.py:10
  271.5 7.5 %collective-permute-start = (f32[2,128,128]{2,1,0:T(8,128)S(1)}, f32[2,128,128]{2,1,0:T(8,128)S(1)}, u32[]{:S(2)}, u32[]{:S(2)}) collective-permute-start(f32[2,128,128]{2,1,0:T(8,128)S(1)} %multiply_add_fusion.2), channel_id=1, source_target_pairs={{16,0},{32,16},{48,32},{64,48},{80,64},{96,80},{112,96},{128,112},... | collective-permute-start | bytes 393224 | tf_op jit(solution)/shard_map/while/body/eval_jaxpr/ppermute | solution.py:10
  279.1 7.5 %collective-permute-start = (f32[2,128,128]{2,1,0:T(8,128)S(1)}, f32[2,128,128]{2,1,0:T(8,128)S(1)}, u32[]{:S(2)}, u32[]{:S(2)}) collective-permute-start(f32[2,128,128]{2,1,0:T(8,128)S(1)} %multiply_add_fusion.2), channel_id=1, source_target_pairs={{16,0},{32,16},{48,32},{64,48},{80,64},{96,80},{112,96},{128,112},... | collective-permute-start | bytes 393224 | tf_op jit(solution)/shard_map/while/body/eval_jaxpr/ppermute | solution.py:10
  286.7 7.5 %collective-permute-start = (f32[2,128,128]{2,1,0:T(8,128)S(1)}, f32[2,128,128]{2,1,0:T(8,128)S(1)}, u32[]{:S(2)}, u32[]{:S(2)}) collective-permute-start(f32[2,128,128]{2,1,0:T(8,128)S(1)} %multiply_add_fusion.2), channel_id=1, source_target_pairs={{16,0},{32,16},{48,32},{64,48},{80,64},{96,80},{112,96},{128,112},... | collective-permute-start | bytes 393224 | tf_op jit(solution)/shard_map/while/body/eval_jaxpr/ppermute | solution.py:10
  294.2 7.5 %collective-permute-start = (f32[2,128,128]{2,1,0:T(8,128)S(1)}, f32[2,128,128]{2,1,0:T(8,128)S(1)}, u32[]{:S(2)}, u32[]{:S(2)}) collective-permute-start(f32[2,128,128]{2,1,0:T(8,128)S(1)} %multiply_add_fusion.2), channel_id=1, source_target_pairs={{16,0},{32,16},{48,32},{64,48},{80,64},{96,80},{112,96},{128,112},... | collective-permute-start | bytes 393224 | tf_op jit(solution)/shard_map/while/body/eval_jaxpr/ppermute | solution.py:10
  301.8 7.5 %collective-permute-start = (f32[2,128,128]{2,1,0:T(8,128)S(1)}, f32[2,128,128]{2,1,0:T(8,128)S(1)}, u32[]{:S(2)}, u32[]{:S(2)}) collective-permute-start(f32[2,128,128]{2,1,0:T(8,128)S(1)} %multiply_add_fusion.2), channel_id=1, source_target_pairs={{16,0},{32,16},{48,32},{64,48},{80,64},{96,80},{112,96},{128,112},... | collective-permute-start | bytes 393224 | tf_op jit(solution)/shard_map/while/body/eval_jaxpr/ppermute | solution.py:10
  309.4 7.5 %collective-permute-start = (f32[2,128,128]{2,1,0:T(8,128)S(1)}, f32[2,128,128]{2,1,0:T(8,128)S(1)}, u32[]{:S(2)}, u32[]{:S(2)}) collective-permute-start(f32[2,128,128]{2,1,0:T(8,128)S(1)} %multiply_add_fusion.2), channel_id=1, source_target_pairs={{16,0},{32,16},{48,32},{64,48},{80,64},{96,80},{112,96},{128,112},... | collective-permute-start | bytes 393224 | tf_op jit(solution)/shard_map/while/body/eval_jaxpr/ppermute | solution.py:10
  319.1 3.3 copy-start.4
  319.2 3.3 copy-start.6
where the time goes:
time: 360 us; the launch traced here: 354 us
  waiting for transfers between devices  196 us (54%)
  starting transfers between devices  83.1 us (23%)
  local copies, waits for them, and re-layouts  23.1 us (6%)
  other arithmetic  20.2 us (6%)
  blocking collectives  17 us (5%)
  matrix products  13.1 us (4%)
    ppermute x31, waiting for transfers between devices, from_behind(): return lax.ppermute(x, axis, pairs)  172 us
    ppermute x31, starting transfers between devices, from_behind(): return lax.ppermute(x, axis, pairs)  63.5 us
    all_to_all x1, blocking collectives, body(): lax.all_to_all(value_grad, 'head', split_axis=0, concat_axis=1, tiled=True)  17 us
    all_to_all x1, waiting for transfers between devices, body(): lax.all_to_all(query_vectors, 'head', split_axis=1, concat_axis=0, tiled=...  11.8 us
    dot_general x1, matrix products, body(): jnp.einsum('bhit,bthe->bihe', weights, grad_blocks, preferred_element_typ...  9.27 us
  transfers between devices with their start and end apart: 35, of which 35 were waited for; matrix products, arithmetic and copies ran while one was open for 7% of the time, Pallas kernels for 0%

commit v1 on v0

v1 whole, which is shorter than its diff:
```python
import jax
import jax.numpy as jnp
from jax import lax
from jax.experimental import pallas as pl
from jax.experimental.pallas import tpu as pltpu
from jax.sharding import Mesh, PartitionSpec as P

HEAD = 128
PAD = 16
NEG = -1e30
PLANE = ("core", "x", "y")


def token_segments(lengths_ref, positions):
    start = jnp.int32(0)
    total = jnp.zeros(positions.shape, jnp.int32)
    for d in range(lengths_ref.shape[0]):
        total = total + (start <= positions).astype(jnp.int32)
        start = start + lengths_ref[d]
    return total


def scalar_segment(lengths_ref, position):
    start = jnp.int32(0)
    total = jnp.int32(0)
    for d in range(lengths_ref.shape[0]):
        total = total + (start <= position).astype(jnp.int32)
        start = start + lengths_ref[d]
    return total


def running_sum(decay):
    rows = decay.shape[0]
    later = lax.broadcasted_iota(jnp.int32, (rows, rows), 0) >= lax.broadcasted_iota(jnp.int32, (rows, rows), 1)
    return jnp.dot(later.astype(jnp.bfloat16), decay, preferred_element_type=jnp.float32)


def running_sum_rows(decay):
    rows = decay.shape[0]
    earlier = lax.broadcasted_iota(jnp.int32, (rows, rows), 0) <= lax.broadcasted_iota(jnp.int32, (rows, rows), 1)
    return lax.dot_general(
        decay, earlier.astype(jnp.bfloat16), (((0,), (0,)), ((), ())), preferred_element_type=jnp.float32
    )


def summary_kernel(lengths_ref, base_ref, q_ref, g_ref, decay_ref, out_ref):
    rows = q_ref.shape[0]
    heads = decay_ref.shape[1]
    base = base_ref[0]
    cum = running_sum(decay_ref[...])
    before = scalar_segment(lengths_ref, base - 1)
    last = scalar_segment(lengths_ref, base + rows - 1)
    seg = token_segments(lengths_ref, base + lax.broadcasted_iota(jnp.int32, (rows, heads), 0))
    scale = jnp.where(seg == before, jnp.exp(cum), 0.0)
    factor = jnp.where(last == before, jnp.exp(cum[rows - 1 : rows, :]), 0.0)
    f_hi = factor.astype(jnp.bfloat16)
    rest = factor - f_hi.astype(jnp.float32)
    f_mid = rest.astype(jnp.bfloat16)
    f_lo = (rest - f_mid.astype(jnp.float32)).astype(jnp.bfloat16)
    which = lax.broadcasted_iota(jnp.int32, (PAD, HEAD), 0)
    for h in range(heads):
        cols = slice(h * HEAD, (h + 1) * HEAD)
        scaled = q_ref[:, cols].astype(jnp.float32) * scale[:, h : h + 1]
        hi = scaled.astype(jnp.bfloat16)
        lo = (scaled - hi.astype(jnp.float32)).astype(jnp.bfloat16)
        g_t = g_ref[:, cols].T
        summary = jnp.dot(
            jnp.concatenate([g_t, g_t], axis=1),
            jnp.concatenate([hi, lo], axis=0),
            preferred_element_type=jnp.float32,
        )
        out_ref[h, 0:HEAD, :] = summary.astype(jnp.bfloat16)
        parts = [jnp.broadcast_to(f[:, h : h + 1].astype(jnp.float32), (PAD, HEAD)) for f in (f_hi, f_mid, f_lo)]
        tail = jnp.where(which == 0, parts[0], jnp.where(which == 1, parts[1], jnp.where(which == 2, parts[2], 0.0)))
        out_ref[h, HEAD : HEAD + PAD, :] = tail.astype(jnp.bfloat16)


def inside_kernel(lengths_ref, base_ref, q_ref, k_ref, g_ref, decay_ref, out_ref):
    rows = q_ref.shape[0]
    heads = decay_ref.shape[1]
    base = base_ref[0]
    cum = running_sum(decay_ref[...])
    cum_rows = running_sum_rows(decay_ref[...])
    i_pos = lax.broadcasted_iota(jnp.int32, (rows, rows), 0)
    t_pos = lax.broadcasted_iota(jnp.int32, (rows, rows), 1)
    same = token_segments(lengths_ref, base + i_pos) == token_segments(lengths_ref, base + t_pos)
    bias = jnp.where(same & (t_pos >= i_pos), 0.0, NEG)
    for h in range(heads):
        cols = slice(h * HEAD, (h + 1) * HEAD)
        scores = lax.dot_general(
            k_ref[:, cols], q_ref[:, cols], (((1,), (1,)), ((), ())), preferred_element_type=jnp.float32
        )
        gaps = jnp.minimum(cum_rows[h : h + 1, :] - cum[:, h : h + 1], 0.0)
        weights = (jnp.exp(gaps + bias) * scores).astype(jnp.bfloat16)
        out_ref[:, cols] = jnp.dot(weights, g_ref[:, cols], preferred_element_type=jnp.float32)


def factor_row(ref, p):
    tail = ref[p, HEAD : HEAD + PAD, :].astype(jnp.float32)
    return tail[0:1, :] + tail[1:2, :] + tail[2:3, :]


def reduce_kernel(parts_ref, out_ref):
    count = parts_ref.shape[0]
    state = jnp.zeros((HEAD, HEAD), jnp.float32)
    factor = jnp.ones((1, HEAD), jnp.float32)
    for p in reversed(range(count)):
        f = factor_row(parts_ref, p)
        state = parts_ref[p, 0:HEAD, :].astype(jnp.float32) + f * state
        factor = factor * f
    out_ref[0:HEAD, :] = state
    out_ref[HEAD : HEAD + 8, :] = jnp.broadcast_to(factor, (8, HEAD))


def join_kernel(own_ref, a_ref, b_ref, c_ref, near_ref, wide_ref):
    def read(ref):
        return ref[0:HEAD, :], ref[HEAD : HEAD + 1, :]

    s0, f0 = read(own_ref)
    s1, f1 = read(a_ref)
    s2, f2 = read(b_ref)
    s3, f3 = read(c_ref)
    near = s1 + f1 * (s2 + f2 * s3)
    near_f = f1 * f2 * f3
    near_ref[0:HEAD, :] = near
    near_ref[HEAD : HEAD + 8, :] = jnp.broadcast_to(near_f, (8, HEAD))
    wide_ref[0:HEAD, :] = s0 + f0 * near
    wide_ref[HEAD : HEAD + 8, :] = jnp.broadcast_to(f0 * near_f, (8, HEAD))


def states_kernel(parts_ref, near_ref, a_ref, b_ref, c_ref, out_ref):
    def read(ref):
        return ref[0:HEAD, :], ref[HEAD : HEAD + 1, :]

    s0, f0 = read(near_ref)
    s1, f1 = read(a_ref)
    s2, f2 = read(b_ref)
    s3, f3 = read(c_ref)
    state = s0 + f0 * (s1 + f1 * (s2 + f2 * s3))
    for p in reversed(range(parts_ref.shape[0])):
        out_ref[p] = state.astype(jnp.bfloat16)
        state = parts_ref[p, 0:HEAD, :].astype(jnp.float32) + factor_row(parts_ref, p) * state


def output_kernel(lengths_ref, base_ref, k_ref, decay_ref, inside_ref, states_ref, out_ref):
    rows = k_ref.shape[0]
    heads = decay_ref.shape[1]
    base = base_ref[0]
    cum = running_sum(decay_ref[...])
    last = scalar_segment(lengths_ref, base + rows - 1)
    seg = token_segments(lengths_ref, base + lax.broadcasted_iota(jnp.int32, (rows, heads), 0))
    tail = jnp.where(seg == last, jnp.exp(cum[rows - 1 : rows, :] - cum), 0.0)
    for h in range(heads):
        cols = slice(h * HEAD, (h + 1) * HEAD)
        carried = lax.dot_general(
            k_ref[:, cols], states_ref[h], (((1,), (1,)), ((), ())), preferred_element_type=jnp.float32
        )
        out_ref[:, cols] = (inside_ref[:, cols] + tail[:, h : h + 1] * carried).astype(jnp.bfloat16)


def call(kernel, out_shape, scalars, arrays):
    smem = pl.BlockSpec(memory_space=pltpu.SMEM)
    vmem = pl.BlockSpec(memory_space=pltpu.VMEM)
    single = not isinstance(out_shape, (list, tuple))
    return pl.pallas_call(
        kernel,
        out_shape=out_shape,
        in_specs=[smem] * len(scalars) + [vmem] * len(arrays),
        out_specs=vmem if single else [vmem] * len(out_shape),
        compiler_params=pltpu.CompilerParams(vmem_limit_bytes=48 * 1024 * 1024),
    )(*scalars, *arrays)


def from_ahead(x, by):
    size = lax.axis_size("z")
    return lax.ppermute(x, "z", [(i + by, i) for i in range(size - by)])


def body(query_vectors, key_vectors, out_grad, log_decay, doc_lengths):
    rows, heads = log_decay.shape
    index = lax.axis_index(("z", "core", "x", "y"))
    base = (index * rows).astype(jnp.int32).reshape(1)
    scalars = (doc_lengths, base)
    shape = jax.ShapeDtypeStruct
    summaries = call(
        summary_kernel,
        shape((heads, HEAD + PAD, HEAD), jnp.bfloat16),
        scalars,
        (query_vectors, out_grad, log_decay),
    )
    parts = lax.all_to_all(summaries, PLANE, split_axis=0, concat_axis=0, tiled=True)
    inside = call(
        inside_kernel,
        shape(query_vectors.shape, jnp.float32),
        scalars,
        (query_vectors, key_vectors, out_grad, log_decay),
    )
    pair = shape((HEAD + 8, HEAD), jnp.float32)
    plane_total = call(reduce_kernel, pair, (), (parts,))
    ahead = [from_ahead(plane_total, by) for by in (1, 2, 3)]
    near, wide = call(join_kernel, (pair, pair), (), (plane_total, *ahead))
    far = [from_ahead(wide, by) for by in (4, 8, 12)]
    states = call(states_kernel, shape((heads, HEAD, HEAD), jnp.bfloat16), (), (parts, near, *far))
    mine = lax.all_to_all(states, PLANE, split_axis=0, concat_axis=0, tiled=True)
    return call(
        output_kernel,
        shape(query_vectors.shape, jnp.bfloat16),
        scalars,
        (key_vectors, log_decay, inside, mine),
    )


def solution(mesh):
    side = 4
    fine = Mesh(
        mesh.devices.reshape(mesh.shape["seq"] // 2, 2, side, mesh.shape["head"] // side), ("z", "core", "x", "y")
    )
    tokens = P(("z", "core", "x", "y"), None)
    return jax.shard_map(
        body, mesh=fine, in_specs=(tokens, tokens, tokens, tokens, P()), out_specs=tokens, check_vma=False
    )
```

time: 360 us -> 98.1 us (0.27)
  the two profiles are of different devices: /device:TPU:225 before, /device:TPU:64 now
where the time goes in v1:
time: 98.1 us; the launch traced here: 97.5 us
  waiting for transfers between devices  36.6 us (37%)
  blocking collectives  26.5 us (27%)
  starting transfers between devices  14.6 us (15%)
  Pallas kernels  12.1 us (12%)
  local copies, waits for them, and re-layouts  7.58 us (8%)
    ppermute x6, waiting for transfers between devices, from_ahead(): return lax.ppermute(x, 'z', [(i + by, i) for i in range(size - by)])  27.3 us
    all_to_all x1, blocking collectives, body(): lax.all_to_all(summaries, PLANE, split_axis=0, concat_axis=0, tiled=True)  26.5 us
    pallas_call x6, Pallas kernels, call(): pl.pallas_call(kernel, out_shape=out_shape, in_specs=[smem] * len(scalars...  12.1 us
    ppermute x6, starting transfers between devices, from_ahead(): return lax.ppermute(x, 'z', [(i + by, i) for i in range(size - by)])  9.81 us
    all_to_all x1, waiting for transfers between devices, body(): lax.all_to_all(states, PLANE, split_axis=0, concat_axis=0, tiled=True)  9.28 us
    unnamed x17, local copies, waits for them, and re-layouts  7.58 us
    all_to_all x1, starting transfers between devices, body(): lax.all_to_all(states, PLANE, split_axis=0, concat_axis=0, tiled=True)  4.8 us
  transfers between devices with their start and end apart: 7, of which 5 were waited for; matrix products, arithmetic and copies ran while one was open for 0% of the time, Pallas kernels for 6%

profile of v1, /device:TPU:64, one launch (start us, length us, event | category | flops | bytes accessed | tf_op | source)
XLA Modules:
  0.0 97.5 jit_solution(7213120790711369753)
XLA Ops:
  0.0 0.8 copy.8.decay_ref
  0.8 0.0 copy-start
  0.8 1.2 %copy-done = bf16[128,4096]{1,0:T(8,128)(2,1)S(1)} copy-done((bf16[128,4096]{1,0:T(8,128)(2,1)S(1)}, bf16[128,4096]{1,0:T(8,128)(2,1)}, u32[]{:S(2)}) %copy-start) | copy-done | bytes 1048600
  2.1 0.0 copy-start.2
  2.1 1.2 %copy-done.2 = bf16[128,4096]{1,0:T(8,128)(2,1)S(1)} copy-done((bf16[128,4096]{1,0:T(8,128)(2,1)S(1)}, bf16[128,4096]{1,0:T(8,128)(2,1)}, u32[]{:S(2)}) %copy-start.2) | copy-done | bytes 1048600
  3.3 0.0 copy-start.6
  3.3 0.7 copy-done.6
  3.9 1.8 %shard_map.56 = bf16[32,144,128]{2,1,0:T(8,128)(2,1)S(1)} custom-call(s32[8]{0:T(128)S(1)} %copy-done.6, s32[1]{0:T(128)} %bitcast.base_ref, bf16[128,4096]{1,0:T(8,128)(2,1)S(1)} %copy-done, bf16[128,4096]{1,0:T(8,128)(2,1)S(1)} %copy-done.2, bf16[128,32]{1,0:T(8,128)(2,1)S(1)} %copy.8.decay_ref), custom_call_target="tpu_custom_call" | custom-call | tf_op jit(solution)/shard_map/pallas_call | solution.py:165
  5.7 26.5 %all_to_all.10.parts_ref = bf16[32,144,128]{2,1,0:T(8,128)(2,1)S(1)} all-to-all(bf16[32,144,128]{2,1,0:T(8,128)(2,1)S(1)} %shard_map.56), channel_id=1, replica_groups=mesh['z'=16,'core'=2,'x'=4,'y'=4] {'core','x','y'}, dimensions={0} | all-to-all | bytes 2359296 | tf_op jit(solution)/shard_map/all_to_all | solution.py:191
  32.2 0.3 shard_map.57.own_ref
  32.5 1.3 %collective-permute-start.2 = (f32[136,128]{1,0:T(8,128)S(1)}, f32[136,128]{1,0:T(8,128)S(1)}, u32[]{:S(2)}, u32[]{:S(2)}) collective-permute-start(f32[136,128]{1,0:T(8,128)S(1)} %shard_map.57.own_ref), channel_id=1, source_target_pairs={{96,0},{128,32},{160,64},{192,96},{224,128},{256,160},{288,192},{3... | collective-permute-start | bytes 208904 | tf_op jit(solution)/shard_map/ppermute | solution.py:176
  33.8 2.7 %collective-permute-start.1 = (f32[136,128]{1,0:T(8,128)S(1)}, f32[136,128]{1,0:T(8,128)S(1)}, u32[]{:S(2)}, u32[]{:S(2)}) collective-permute-start(f32[136,128]{1,0:T(8,128)S(1)} %shard_map.57.own_ref), channel_id=1, source_target_pairs={{64,0},{96,32},{128,64},{160,96},{192,128},{224,160},{256,192},{28... | collective-permute-start | bytes 208904 | tf_op jit(solution)/shard_map/ppermute | solution.py:176
  36.5 1.9 %collective-permute-start = (f32[136,128]{1,0:T(8,128)S(1)}, f32[136,128]{1,0:T(8,128)S(1)}, u32[]{:S(2)}, u32[]{:S(2)}) collective-permute-start(f32[136,128]{1,0:T(8,128)S(1)} %shard_map.57.own_ref), channel_id=1, source_target_pairs={{32,0},{64,32},{96,64},{128,96},{160,128},{192,160},{224,192},{256... | collective-permute-start | bytes 208904 | tf_op jit(solution)/shard_map/ppermute | solution.py:176
  38.4 7.4 %collective-permute-done.2.c_ref = f32[136,128]{1,0:T(8,128)S(1)} collective-permute-done((f32[136,128]{1,0:T(8,128)S(1)}, f32[136,128]{1,0:T(8,128)S(1)}, u32[]{:S(2)}, u32[]{:S(2)}) %collective-permute-start.2) | collective-permute-done | bytes 69664 | tf_op jit(solution)/shard_map/ppermute | solution.py:176
  45.8 1.1 %collective-permute-done.1.b_ref = f32[136,128]{1,0:T(8,128)S(1)} collective-permute-done((f32[136,128]{1,0:T(8,128)S(1)}, f32[136,128]{1,0:T(8,128)S(1)}, u32[]{:S(2)}, u32[]{:S(2)}) %collective-permute-start.1) | collective-permute-done | bytes 69664 | tf_op jit(solution)/shard_map/ppermute | solution.py:176
  47.0 0.0 collective-permute-done.a_ref
  47.0 1.3 %collective-permute-start.5 = (f32[136,128]{1,0:T(8,128)S(1)}, f32[136,128]{1,0:T(8,128)S(1)}, u32[]{:S(2)}, u32[]{:S(2)}) collective-permute-start(f32[136,128]{1,0:T(8,128)S(1)} %get-tuple-element.8), channel_id=1, source_target_pairs={{384,0},{416,32},{448,64},{480,96},{385,1},{417,33},{449,65},{481,... | collective-permute-start | bytes 208904 | tf_op jit(solution)/shard_map/ppermute | solution.py:176
  48.3 1.3 %collective-permute-start.4 = (f32[136,128]{1,0:T(8,128)S(1)}, f32[136,128]{1,0:T(8,128)S(1)}, u32[]{:S(2)}, u32[]{:S(2)}) collective-permute-start(f32[136,128]{1,0:T(8,128)S(1)} %get-tuple-element.8), channel_id=1, source_target_pairs={{256,0},{288,32},{320,64},{352,96},{384,128},{416,160},{448,192},{... | collective-permute-start | bytes 208904 | tf_op jit(solution)/shard_map/ppermute | solution.py:176
  49.6 1.3 %collective-permute-start.3 = (f32[136,128]{1,0:T(8,128)S(1)}, f32[136,128]{1,0:T(8,128)S(1)}, u32[]{:S(2)}, u32[]{:S(2)}) collective-permute-start(f32[136,128]{1,0:T(8,128)S(1)} %get-tuple-element.8), channel_id=1, source_target_pairs={{128,0},{160,32},{192,64},{224,96},{256,128},{288,160},{320,192},{... | collective-permute-start | bytes 208904 | tf_op jit(solution)/shard_map/ppermute | solution.py:176
  50.9 15.6 %collective-permute-done.5.c_ref = f32[136,128]{1,0:T(8,128)S(1)} collective-permute-done((f32[136,128]{1,0:T(8,128)S(1)}, f32[136,128]{1,0:T(8,128)S(1)}, u32[]{:S(2)}, u32[]{:S(2)}) %collective-permute-start.5) | collective-permute-done | bytes 69664 | tf_op jit(solution)/shard_map/ppermute | solution.py:176
  66.5 0.0 collective-permute-done.4.b_ref
  66.5 3.1 %collective-permute-done.3.a_ref = f32[136,128]{1,0:T(8,128)S(1)} collective-permute-done((f32[136,128]{1,0:T(8,128)S(1)}, f32[136,128]{1,0:T(8,128)S(1)}, u32[]{:S(2)}, u32[]{:S(2)}) %collective-permute-start.3) | collective-permute-done | bytes 69664 | tf_op jit(solution)/shard_map/ppermute | solution.py:176
  69.7 1.3 %shard_map.59 = bf16[32,128,128]{2,1,0:T(8,128)(2,1)} custom-call(bf16[32,144,128]{2,1,0:T(8,128)(2,1)S(1)} %all_to_all.10.parts_ref, f32[136,128]{1,0:T(8,128)S(1)} %get-tuple-element.7.near_ref, f32[136,128]{1,0:T(8,128)S(1)} %collective-permute-done.3.a_ref, f32[136,128]{1,0:T(8,128)S(1)} %collective-permute-done.4.b_ref, ...), custom_call_target="tpu_custom_call" | custom-call | tf_op jit(solution)/shard_map/pallas_call | solution.py:165
  70.9 0.0 copy-start.1
  70.9 0.0 copy-start.7
  70.9 4.8 %all-to-all-start.1 = ((bf16[32,128,128]{2,1,0:T(8,128)(2,1)}), bf16[32,128,128]{2,1,0:T(8,128)(2,1)}, u32[]{:S(2)}, u32[]{:S(2)}) async-start(bf16[32,128,128]{2,1,0:T(8,128)(2,1)} %shard_map.59), calls=%async_computation.1 | async-start | bytes 2097152 | tf_op jit(solution)/shard_map/all_to_all | solution.py:204
  75.7 0.0 copy-done.1
  75.7 0.0 copy-done.7
  75.8 0.0 copy-start.3
  75.8 1.2 %copy-done.3 = bf16[128,4096]{1,0:T(8,128)(2,1)S(1)} copy-done((bf16[128,4096]{1,0:T(8,128)(2,1)S(1)}, bf16[128,4096]{1,0:T(8,128)(2,1)}, u32[]{:S(2)}) %copy-start.3) | copy-done | bytes 1048600
  77.0 0.0 copy-start.4
  77.0 1.2 %copy-done.4 = bf16[128,4096]{1,0:T(8,128)(2,1)S(1)} copy-done((bf16[128,4096]{1,0:T(8,128)(2,1)S(1)}, bf16[128,4096]{1,0:T(8,128)(2,1)}, u32[]{:S(2)}) %copy-start.4) | copy-done | bytes 1048600
  78.2 5.7 %shard_map.55.inside_ref = f32[128,4096]{1,0:T(8,128)S(1)} custom-call(s32[8]{0:T(128)S(1)} %copy-done.7, s32[1]{0:T(128)} %bitcast.base_ref, bf16[128,4096]{1,0:T(8,128)(2,1)S(1)} %copy-done.1, bf16[128,4096]{1,0:T(8,128)(2,1)S(1)} %copy-done.4, bf16[128,4096]{1,0:T(8,128)(2,1)S(1)} %copy-done.3, bf16[128,32]{1,0:T(8,128)(2,1)S(1)} %copy.8.decay_ref), custom_call_target="tpu_custom_call" | custom-call | tf_op jit(solution)/shard_map/pallas_call | solution.py:165
  83.9 9.3 %all-to-all-done.1.states_ref = bf16[32,128,128]{2,1,0:T(8,128)(2,1)} async-done(((bf16[32,128,128]{2,1,0:T(8,128)(2,1)}), bf16[32,128,128]{2,1,0:T(8,128)(2,1)}, u32[]{:S(2)}, u32[]{:S(2)}) %all-to-all-start.1) | async-done | bytes 1048608 | tf_op jit(solution)/shard_map/all_to_all | solution.py:204
  93.2 0.0 copy-start.5
  93.2 1.2 %copy-done.5 = bf16[128,4096]{1,0:T(8,128)(2,1)S(1)} copy-done((bf16[128,4096]{1,0:T(8,128)(2,1)S(1)}, bf16[128,4096]{1,0:T(8,128)(2,1)}, u32[]{:S(2)}) %copy-start.5) | copy-done | bytes 1048600
  94.4 3.1 %shard_map.60 = bf16[128,4096]{1,0:T(8,128)(2,1)} custom-call(s32[8]{0:T(128)S(1)} %copy-done.7, s32[1]{0:T(128)} %bitcast.base_ref, bf16[128,4096]{1,0:T(8,128)(2,1)S(1)} %copy-done.5, bf16[128,32]{1,0:T(8,128)(2,1)S(1)} %copy.8.decay_ref, f32[128,4096]{1,0:T(8,128)S(1)} %shard_map.55.inside_ref, bf16[32,128,128]{2,1,0:T(8,128)(2,1)} %all-to-all-done.1.states_ref), custom_call_target="tpu_custom_call" | custom-call | tf_op jit(solution)/shard_map/pallas_call | solution.py:165
  (1 shorter events, 0.0 us)
Async XLA Ops:
  0.8 1.2 %copy-start = (bf16[128,4096]{1,0:T(8,128)(2,1)S(1)}, bf16[128,4096]{1,0:T(8,128)(2,1)}, u32[]{:S(2)}) copy-start(bf16[128,4096]{1,0:T(8,128)(2,1)} %q_ref.3) | copy-start | bytes 3145732
  2.1 1.2 %copy-start.2 = (bf16[128,4096]{1,0:T(8,128)(2,1)S(1)}, bf16[128,4096]{1,0:T(8,128)(2,1)}, u32[]{:S(2)}) copy-start(bf16[128,4096]{1,0:T(8,128)(2,1)} %g_ref.3) | copy-start | bytes 3145732
  3.3 0.7 copy-start.6
  32.5 13.3 %collective-permute-start.2 = (f32[136,128]{1,0:T(8,128)S(1)}, f32[136,128]{1,0:T(8,128)S(1)}, u32[]{:S(2)}, u32[]{:S(2)}) collective-permute-start(f32[136,128]{1,0:T(8,128)S(1)} %shard_map.57.own_ref), channel_id=1, source_target_pairs={{96,0},{128,32},{160,64},{192,96},{224,128},{256,160},{288,192},{3... | collective-permute-start | bytes 208904 | tf_op jit(solution)/shard_map/ppermute | solution.py:176
  33.8 13.2 %collective-permute-start.1 = (f32[136,128]{1,0:T(8,128)S(1)}, f32[136,128]{1,0:T(8,128)S(1)}, u32[]{:S(2)}, u32[]{:S(2)}) collective-permute-start(f32[136,128]{1,0:T(8,128)S(1)} %shard_map.57.own_ref), channel_id=1, source_target_pairs={{64,0},{96,32},{128,64},{160,96},{192,128},{224,160},{256,192},{28... | collective-permute-start | bytes 208904 | tf_op jit(solution)/shard_map/ppermute | solution.py:176
  36.5 10.5 %collective-permute-start = (f32[136,128]{1,0:T(8,128)S(1)}, f32[136,128]{1,0:T(8,128)S(1)}, u32[]{:S(2)}, u32[]{:S(2)}) collective-permute-start(f32[136,128]{1,0:T(8,128)S(1)} %shard_map.57.own_ref), channel_id=1, source_target_pairs={{32,0},{64,32},{96,64},{128,96},{160,128},{192,160},{224,192},{256... | collective-permute-start | bytes 208904 | tf_op jit(solution)/shard_map/ppermute | solution.py:176
  47.0 19.5 %collective-permute-start.5 = (f32[136,128]{1,0:T(8,128)S(1)}, f32[136,128]{1,0:T(8,128)S(1)}, u32[]{:S(2)}, u32[]{:S(2)}) collective-permute-start(f32[136,128]{1,0:T(8,128)S(1)} %get-tuple-element.8), channel_id=1, source_target_pairs={{384,0},{416,32},{448,64},{480,96},{385,1},{417,33},{449,65},{481,... | collective-permute-start | bytes 208904 | tf_op jit(solution)/shard_map/ppermute | solution.py:176
  48.3 18.2 %collective-permute-start.4 = (f32[136,128]{1,0:T(8,128)S(1)}, f32[136,128]{1,0:T(8,128)S(1)}, u32[]{:S(2)}, u32[]{:S(2)}) collective-permute-start(f32[136,128]{1,0:T(8,128)S(1)} %get-tuple-element.8), channel_id=1, source_target_pairs={{256,0},{288,32},{320,64},{352,96},{384,128},{416,160},{448,192},{... | collective-permute-start | bytes 208904 | tf_op jit(solution)/shard_map/ppermute | solution.py:176
  49.6 20.1 %collective-permute-start.3 = (f32[136,128]{1,0:T(8,128)S(1)}, f32[136,128]{1,0:T(8,128)S(1)}, u32[]{:S(2)}, u32[]{:S(2)}) collective-permute-start(f32[136,128]{1,0:T(8,128)S(1)} %get-tuple-element.8), channel_id=1, source_target_pairs={{128,0},{160,32},{192,64},{224,96},{256,128},{288,160},{320,192},{... | collective-permute-start | bytes 208904 | tf_op jit(solution)/shard_map/ppermute | solution.py:176
  70.9 4.8 %copy-start.1 = (bf16[128,4096]{1,0:T(8,128)(2,1)S(1)}, bf16[128,4096]{1,0:T(8,128)(2,1)}, u32[]{:S(2)}) copy-start(bf16[128,4096]{1,0:T(8,128)(2,1)} %q_ref.3) | copy-start | bytes 3145732
  70.9 4.8 %copy-start.7 = (s32[8]{0:T(128)S(1)}, s32[8]{0:T(128)}, u32[]{:S(2)}) copy-start(s32[8]{0:T(128)} %lengths_ref.5) | copy-start | bytes 100
  70.9 22.2 %all-to-all-start.1 = ((bf16[32,128,128]{2,1,0:T(8,128)(2,1)}), bf16[32,128,128]{2,1,0:T(8,128)(2,1)}, u32[]{:S(2)}, u32[]{:S(2)}) async-start(bf16[32,128,128]{2,1,0:T(8,128)(2,1)} %shard_map.59), calls=%async_computation.1 | async-start | bytes 2097152 | tf_op jit(solution)/shard_map/all_to_all | solution.py:204
  75.8 1.2 %copy-start.3 = (bf16[128,4096]{1,0:T(8,128)(2,1)S(1)}, bf16[128,4096]{1,0:T(8,128)(2,1)}, u32[]{:S(2)}) copy-start(bf16[128,4096]{1,0:T(8,128)(2,1)} %g_ref.3) | copy-start | bytes 3145732
  77.0 1.2 %copy-start.4 = (bf16[128,4096]{1,0:T(8,128)(2,1)S(1)}, bf16[128,4096]{1,0:T(8,128)(2,1)}, u32[]{:S(2)}) copy-start(bf16[128,4096]{1,0:T(8,128)(2,1)} %k_ref.3) | copy-start | bytes 3145732
  93.2 1.2 %copy-start.5 = (bf16[128,4096]{1,0:T(8,128)(2,1)S(1)}, bf16[128,4096]{1,0:T(8,128)(2,1)}, u32[]{:S(2)}) copy-start(bf16[128,4096]{1,0:T(8,128)(2,1)} %k_ref.3) | copy-start | bytes 3145732

commit v2 on v1

v2 whole, which is shorter than its diff:
```python
import jax
import jax.numpy as jnp
from jax import lax
from jax.experimental import pallas as pl
from jax.experimental.pallas import tpu as pltpu
from jax.sharding import Mesh, PartitionSpec as P

HEAD = 128
PAD = 16
NEG = -1e30
TINY = 1e-36
OCTAVES = 120.0
GROUPS = 4
PLANE = ("core", "x", "y")


def token_segments(lengths_ref, positions):
    start = jnp.int32(0)
    total = jnp.zeros(positions.shape, jnp.int32)
    for d in range(lengths_ref.shape[0]):
        total = total + (start <= positions).astype(jnp.int32)
        start = start + lengths_ref[d]
    return total


def scalar_segment(lengths_ref, position):
    start = jnp.int32(0)
    total = jnp.int32(0)
    for d in range(lengths_ref.shape[0]):
        total = total + (start <= position).astype(jnp.int32)
        start = start + lengths_ref[d]
    return total


def running_sums(decay_rows):
    size = decay_rows.shape[1]
    upto = lax.broadcasted_iota(jnp.int32, (size, size), 0) <= lax.broadcasted_iota(jnp.int32, (size, size), 1)
    by_row = jnp.dot(decay_rows, upto.astype(jnp.bfloat16), preferred_element_type=jnp.float32)
    since = lax.broadcasted_iota(jnp.int32, (size, size), 0) >= lax.broadcasted_iota(jnp.int32, (size, size), 1)
    by_col = lax.dot_general(
        since.astype(jnp.bfloat16), decay_rows, (((1,), (1,)), ((), ())), preferred_element_type=jnp.float32
    )
    return by_row, by_col


def split3(value):
    hi = value.astype(jnp.bfloat16)
    rest = value - hi.astype(jnp.float32)
    mid = rest.astype(jnp.bfloat16)
    lo = (rest - mid.astype(jnp.float32)).astype(jnp.bfloat16)
    return [part.astype(jnp.float32) for part in (hi, mid, lo)]


def pad_rows(rows):
    which = lax.broadcasted_iota(jnp.int32, (PAD, HEAD), 0)
    out = jnp.zeros((PAD, HEAD), jnp.float32)
    for number, row in enumerate(rows):
        out = jnp.where(which == number, jnp.broadcast_to(row, (PAD, HEAD)), out)
    return out.astype(jnp.bfloat16)


def summary_kernel(
    base_ref, lengths_hbm, q_hbm, g_hbm, decay_hbm, out_ref, q_buf, g_buf, decay_ref, lengths_ref, sems, small_sems
):
    rows = q_buf.shape[0]
    heads = decay_ref.shape[0]
    groups = sems.shape[1]
    width = q_buf.shape[1] // groups
    small = [
        pltpu.make_async_copy(lengths_hbm, lengths_ref, small_sems.at[0]),
        pltpu.make_async_copy(decay_hbm, decay_ref, small_sems.at[1]),
    ]
    for copy in small:
        copy.start()
    large = []
    for n in range(groups):
        span = slice(n * width, (n + 1) * width)
        pair = [
            pltpu.make_async_copy(q_hbm.at[:, span], q_buf.at[:, span], sems.at[0, n]),
            pltpu.make_async_copy(g_hbm.at[:, span], g_buf.at[:, span], sems.at[1, n]),
        ]
        for copy in pair:
            copy.start()
        large.append(pair)
    for copy in small:
        copy.wait()
    base = base_ref[0]
    by_row, cum = running_sums(decay_ref[...])
    before = scalar_segment(lengths_ref, base - 1)
    last = scalar_segment(lengths_ref, base + rows - 1)
    seg = token_segments(lengths_ref, base + lax.broadcasted_iota(jnp.int32, (rows, heads), 0))
    scale = jnp.where(seg == before, jnp.exp(cum), 0.0)
    factors = split3(jnp.where(last == before, jnp.exp(cum[rows - 1 : rows, :]), 0.0))
    for h in range(heads):
        cols = slice(h * HEAD, (h + 1) * HEAD)
        if (h * HEAD) % width == 0:
            for copy in large[h * HEAD // width]:
                copy.wait()
        scaled = q_buf[:, cols].astype(jnp.float32) * scale[:, h : h + 1]
        hi = scaled.astype(jnp.bfloat16)
        lo = (scaled - hi.astype(jnp.float32)).astype(jnp.bfloat16)
        g_t = g_buf[:, cols].T
        summary = jnp.dot(
            jnp.concatenate([g_t, g_t], axis=1),
            jnp.concatenate([hi, lo], axis=0),
            preferred_element_type=jnp.float32,
        )
        out_ref[h, 0:HEAD, :] = summary.astype(jnp.bfloat16)
        out_ref[h, HEAD : HEAD + PAD, :] = pad_rows([f[:, h : h + 1] for f in factors])


def inside_kernel(
    base_ref, lengths_ref, q_ref, k_ref, g_ref, decay_ref, after_ref, inside_ref, tail_ref, keys_ref
):
    rows = q_ref.shape[0]
    heads = decay_ref.shape[0]
    base = base_ref[0]
    cum_rows, cum = running_sums(decay_ref[...])
    last = scalar_segment(lengths_ref, base + rows - 1)
    seg = token_segments(lengths_ref, base + lax.broadcasted_iota(jnp.int32, (rows, heads), 0))
    tail_ref[...] = jnp.where(seg == last, jnp.exp(cum[rows - 1 : rows, :] - cum), 0.0)
    i_pos = lax.broadcasted_iota(jnp.int32, (rows, rows), 0)
    t_pos = lax.broadcasted_iota(jnp.int32, (rows, rows), 1)
    same = token_segments(lengths_ref, base + i_pos) == token_segments(lengths_ref, base + t_pos)
    bias = jnp.where(same & (t_pos >= i_pos), 0.0, NEG)
    for h in range(heads):
        cols = slice(h * HEAD, (h + 1) * HEAD)
        keys = k_ref[:, cols]
        keys_ref[:, cols] = keys
        scores = lax.dot_general(
            keys, q_ref[:, cols], (((1,), (1,)), ((), ())), preferred_element_type=jnp.float32
        )
        gaps = jnp.minimum(cum_rows[h : h + 1, :] - cum[:, h : h + 1], 0.0)
        weights = (jnp.exp(gaps + bias) * scores).astype(jnp.bfloat16)
        inside_ref[:, cols] = jnp.dot(weights, g_ref[:, cols], preferred_element_type=jnp.float32)


def factor_row(ref, p):
    tail = ref[p, HEAD : HEAD + PAD, :].astype(jnp.float32)
    return tail[0:1, :] + tail[1:2, :] + tail[2:3, :]


def write_packet(ref, state, factor):
    size = jnp.abs(state)
    largest = jnp.max(jnp.max(size, axis=0, keepdims=True), axis=1, keepdims=True)
    bound = (largest * 1.01 + TINY).astype(jnp.bfloat16).astype(jnp.float32)
    code = jnp.exp2(size * ((2.0 * OCTAVES) / bound) - OCTAVES)
    ref[0:HEAD, :] = jnp.where(state < 0.0, -code, code).astype(jnp.bfloat16)
    ref[HEAD : HEAD + PAD, :] = pad_rows([bound] + split3(factor))


def read_packet(ref):
    code = ref[0:HEAD, :].astype(jnp.float32)
    tail = ref[HEAD : HEAD + PAD, :].astype(jnp.float32)
    octaves = jnp.log2(jnp.maximum(jnp.abs(code), 2.0**-OCTAVES)) + OCTAVES
    size = octaves * (tail[0:1, :] * (0.5 / OCTAVES))
    return jnp.where(code < 0.0, -size, size), tail[1:2, :] + tail[2:3, :] + tail[3:4, :]


def reduce_kernel(parts_ref, total_ref, factor_ref, packet_ref):
    state = jnp.zeros((HEAD, HEAD), jnp.float32)
    factor = jnp.ones((1, HEAD), jnp.float32)
    for p in reversed(range(parts_ref.shape[0])):
        f = factor_row(parts_ref, p)
        state = parts_ref[p, 0:HEAD, :].astype(jnp.float32) + f * state
        factor = factor * f
    total_ref[...] = state
    factor_ref[...] = factor
    write_packet(packet_ref, state, factor)


def join(refs):
    state, factor = read_packet(refs[-1])
    for ref in reversed(refs[:-1]):
        s, f = read_packet(ref)
        state = s + f * state
        factor = f * factor
    return state, factor


def join_kernel(total_ref, factor_ref, a_ref, b_ref, c_ref, near_ref, near_factor_ref, packet_ref):
    state, factor = join([a_ref, b_ref, c_ref])
    near_ref[...] = state
    near_factor_ref[...] = factor
    own = factor_ref[...]
    write_packet(packet_ref, total_ref[...] + own * state, own * factor)


def states_kernel(parts_ref, near_ref, near_factor_ref, a_ref, b_ref, c_ref, after_ref, out_ref):
    far, far_factor = join([a_ref, b_ref, c_ref])
    state = near_ref[...] + near_factor_ref[...] * far
    for p in reversed(range(parts_ref.shape[0])):
        out_ref[p] = state.astype(jnp.bfloat16)
        state = parts_ref[p, 0:HEAD, :].astype(jnp.float32) + factor_row(parts_ref, p) * state


def output_kernel(keys_ref, tail_ref, inside_ref, states_ref, out_hbm, out_buf, sems):
    groups = sems.shape[0]
    width = out_buf.shape[1] // groups
    tail = tail_ref[...]
    copies = []
    for h in range(states_ref.shape[0]):
        cols = slice(h * HEAD, (h + 1) * HEAD)
        carried = lax.dot_general(
            keys_ref[:, cols], states_ref[h], (((1,), (1,)), ((), ())), preferred_element_type=jnp.float32
        )
        out_buf[:, cols] = (inside_ref[:, cols] + tail[:, h : h + 1] * carried).astype(jnp.bfloat16)
        if ((h + 1) * HEAD) % width == 0:
            n = h * HEAD // width
            span = slice(n * width, (n + 1) * width)
            copies.append(pltpu.make_async_copy(out_buf.at[:, span], out_hbm.at[:, span], sems.at[n]))
            copies[-1].start()
    for copy in copies:
        copy.wait()


SMEM = pl.BlockSpec(memory_space=pltpu.SMEM)
VMEM = pl.BlockSpec(memory_space=pltpu.VMEM)
REST = pl.BlockSpec(memory_space=pltpu.HBM)


def call(kernel, out_shape, in_specs, args, out_specs=None, scratch=()):
    if out_specs is None:
        out_specs = [VMEM] * len(out_shape) if isinstance(out_shape, (list, tuple)) else VMEM
    return pl.pallas_call(
        kernel,
        out_shape=out_shape,
        in_specs=in_specs,
        out_specs=out_specs,
        scratch_shapes=list(scratch),
        compiler_params=pltpu.CompilerParams(vmem_limit_bytes=40 * 1024 * 1024),
    )(*args)


def from_ahead(x, by):
    size = lax.axis_size("z")
    return lax.ppermute(x, "z", [(i + by, i) for i in range(size - by)])


def body(query_vectors, key_vectors, out_grad, log_decay, doc_lengths):
    rows, heads = log_decay.shape
    columns = query_vectors.shape[1]
    index = lax.axis_index(("z", "core", "x", "y"))
    base = (index * rows).astype(jnp.int32).reshape(1)
    decay_rows = log_decay.T
    shape = jax.ShapeDtypeStruct
    dma = pltpu.SemaphoreType.DMA
    summaries = call(
        summary_kernel,
        shape((heads, HEAD + PAD, HEAD), jnp.bfloat16),
        [SMEM] + [REST] * 4,
        (base, doc_lengths, query_vectors, out_grad, decay_rows),
        scratch=(
            pltpu.VMEM((rows, columns), jnp.bfloat16),
            pltpu.VMEM((rows, columns), jnp.bfloat16),
            pltpu.VMEM((heads, rows), jnp.bfloat16),
            pltpu.SMEM(doc_lengths.shape, jnp.int32),
            dma((2, GROUPS)),
            dma((2,)),
        ),
    )
    parts = lax.all_to_all(summaries, PLANE, split_axis=0, concat_axis=0, tiled=True)
    state = shape((HEAD, HEAD), jnp.float32)
    factor = shape((1, HEAD), jnp.float32)
    packet = shape((HEAD + PAD, HEAD), jnp.bfloat16)
    total, total_factor, own = call(reduce_kernel, (state, factor, packet), [VMEM], (parts,))
    ahead = [from_ahead(own, by) for by in (1, 2, 3)]
    near, near_factor, wide = call(
        join_kernel, (state, factor, packet), [VMEM] * 5, (total, total_factor, *ahead)
    )
    far = [from_ahead(wide, by) for by in (4, 8, 12)]
    inside, tail, keys = call(
        inside_kernel,
        (
            shape((rows, columns), jnp.float32),
            shape((rows, heads), jnp.float32),
            shape((rows, columns), jnp.bfloat16),
        ),
        [SMEM] * 2 + [VMEM] * 5,
        (base, doc_lengths, query_vectors, key_vectors, out_grad, decay_rows, wide),
    )
    states = call(
        states_kernel,
        shape((heads, HEAD, HEAD), jnp.bfloat16),
        [VMEM] * 7,
        (parts, near, near_factor, *far, tail),
    )
    mine = lax.all_to_all(states, PLANE, split_axis=0, concat_axis=0, tiled=True)
    return call(
        output_kernel,
        shape((rows, columns), jnp.bfloat16),
        [VMEM] * 4,
        (keys, tail, inside, mine),
        out_specs=REST,
        scratch=(pltpu.VMEM((rows, columns), jnp.bfloat16), dma((GROUPS,))),
    )


def solution(mesh):
    side = 4
    fine = Mesh(
        mesh.devices.reshape(mesh.shape["seq"] // 2, 2, side, mesh.shape["head"] // side), ("z", "core", "x", "y")
    )
    tokens = P(("z", "core", "x", "y"), None)
    return jax.shard_map(
        body, mesh=fine, in_specs=(tokens, tokens, tokens, tokens, P()), out_specs=tokens, check_vma=False
    )
```

time: 98.1 us -> 91 us (0.928)
  the two profiles are of different devices: /device:TPU:64 before, /device:TPU:1 now
where the time goes in v2:
time: 91 us; the launch traced here: 90.4 us
  blocking collectives  51.4 us (56%)
  waiting for transfers between devices  16.3 us (18%)
  Pallas kernels  11 us (12%)
  starting transfers between devices  7.75 us (9%)
  local copies, waits for them, and re-layouts  3.82 us (4%)
    all_to_all x1, blocking collectives, body(): lax.all_to_all(summaries, PLANE, split_axis=0, concat_axis=0, tiled=True)  28.6 us
    all_to_all x1, blocking collectives, body(): lax.all_to_all(states, PLANE, split_axis=0, concat_axis=0, tiled=True)  22.8 us
    ppermute x6, waiting for transfers between devices, from_ahead(): return lax.ppermute(x, 'z', [(i + by, i) for i in range(size - by)])  16.3 us
    pallas_call x6, Pallas kernels, call(): pl.pallas_call(kernel, out_shape=out_shape, in_specs=in_specs, out_specs=...  11 us
    ppermute x6, starting transfers between devices, from_ahead(): return lax.ppermute(x, 'z', [(i + by, i) for i in range(size - by)])  7.75 us
    unnamed x16, local copies, waits for them, and re-layouts  3.82 us
  transfers between devices with their start and end apart: 6, of which 5 were waited for; matrix products, arithmetic and copies ran while one was open for 0% of the time, Pallas kernels for 6%

profile of v2, /device:TPU:1, one launch (start us, length us, event | category | flops | bytes accessed | tf_op | source)
XLA Modules:
  0.0 90.4 jit_solution(14824287024556583205)
XLA Ops:
  0.0 0.0 copy-start
  0.0 1.2 %copy-done = bf16[128,4096]{1,0:T(8,128)(2,1)S(1)} copy-done((bf16[128,4096]{1,0:T(8,128)(2,1)S(1)}, bf16[128,4096]{1,0:T(8,128)(2,1)}, u32[]{:S(2)}) %copy-start) | copy-done | bytes 1048600
  1.2 0.0 copy-start.2
  1.2 1.2 %copy-done.2 = bf16[128,4096]{1,0:T(8,128)(2,1)S(1)} copy-done((bf16[128,4096]{1,0:T(8,128)(2,1)S(1)}, bf16[128,4096]{1,0:T(8,128)(2,1)}, u32[]{:S(2)}) %copy-start.2) | copy-done | bytes 1048600
  2.5 0.0 copy-start.5
  2.5 0.7 copy-done.5
  3.1 0.0 copy-start.6
  3.2 0.7 copy-done.6
  3.8 2.8 %shard_map.55 = bf16[32,144,128]{2,1,0:T(8,128)(2,1)S(1)} custom-call(s32[1]{0:T(128)} %bitcast.base_ref, s32[8]{0:T(128)S(1)} %copy-done.6, bf16[128,4096]{1,0:T(8,128)(2,1)S(1)} %copy-done, bf16[128,4096]{1,0:T(8,128)(2,1)S(1)} %copy-done.2, bf16[32,128]{1,0:T(8,128)(2,1)S(1)} %bitcast.2), custom_call_target="tpu_custom_call" | custom-call | tf_op jit(solution)/shard_map/pallas_call | solution.py:225
  6.6 0.0 copy-start.3
  6.7 0.0 copy-start.4
  6.7 28.6 %all_to_all.10.parts_ref = bf16[32,144,128]{2,1,0:T(8,128)(2,1)S(1)} all-to-all(bf16[32,144,128]{2,1,0:T(8,128)(2,1)S(1)} %shard_map.55), channel_id=1, replica_groups=mesh['z'=16,'core'=2,'x'=4,'y'=4] {'core','x','y'}, dimensions={0} | all-to-all | bytes 2359296 | tf_op jit(solution)/shard_map/all_to_all | solution.py:262
  35.3 0.0 copy-start.1
  35.3 0.0 copy-start.7
  35.3 0.3 shard_map.56
  35.7 1.3 %collective-permute-start = (bf16[144,128]{1,0:T(8,128)(2,1)S(1)}, bf16[144,128]{1,0:T(8,128)(2,1)S(1)}, u32[]{:S(2)}, u32[]{:S(2)}) collective-permute-start(bf16[144,128]{1,0:T(8,128)(2,1)S(1)} %get-tuple-element.16), channel_id=1, source_target_pairs={{32,0},{64,32},{96,64},{128,96},{160,128},{192,160},{224,192},{256... | collective-permute-start | bytes 110600 | tf_op jit(solution)/shard_map/ppermute | solution.py:237
  37.0 1.3 %collective-permute-start.1 = (bf16[144,128]{1,0:T(8,128)(2,1)S(1)}, bf16[144,128]{1,0:T(8,128)(2,1)S(1)}, u32[]{:S(2)}, u32[]{:S(2)}) collective-permute-start(bf16[144,128]{1,0:T(8,128)(2,1)S(1)} %get-tuple-element.16), channel_id=1, source_target_pairs={{64,0},{96,32},{128,64},{160,96},{192,128},{224,160},{256,192},{28... | collective-permute-start | bytes 110600 | tf_op jit(solution)/shard_map/ppermute | solution.py:237
  38.3 1.3 %collective-permute-start.2 = (bf16[144,128]{1,0:T(8,128)(2,1)S(1)}, bf16[144,128]{1,0:T(8,128)(2,1)S(1)}, u32[]{:S(2)}, u32[]{:S(2)}) collective-permute-start(bf16[144,128]{1,0:T(8,128)(2,1)S(1)} %get-tuple-element.16), channel_id=1, source_target_pairs={{96,0},{128,32},{160,64},{192,96},{224,128},{256,160},{288,192},{3... | collective-permute-start | bytes 110600 | tf_op jit(solution)/shard_map/ppermute | solution.py:237
  39.6 0.8 collective-permute-done.a_ref
  40.4 2.2 %collective-permute-done.1.b_ref = bf16[144,128]{1,0:T(8,128)(2,1)S(1)} collective-permute-done((bf16[144,128]{1,0:T(8,128)(2,1)S(1)}, bf16[144,128]{1,0:T(8,128)(2,1)S(1)}, u32[]{:S(2)}, u32[]{:S(2)}) %collective-permute-start.1) | collective-permute-done | bytes 36896 | tf_op jit(solution)/shard_map/ppermute | solution.py:237
  42.6 4.1 %collective-permute-done.2.c_ref = bf16[144,128]{1,0:T(8,128)(2,1)S(1)} collective-permute-done((bf16[144,128]{1,0:T(8,128)(2,1)S(1)}, bf16[144,128]{1,0:T(8,128)(2,1)S(1)}, u32[]{:S(2)}, u32[]{:S(2)}) %collective-permute-start.2) | collective-permute-done | bytes 36896 | tf_op jit(solution)/shard_map/ppermute | solution.py:237
  46.7 0.2 shard_map.57
  46.9 1.3 %collective-permute-start.3 = (bf16[144,128]{1,0:T(8,128)(2,1)S(1)}, bf16[144,128]{1,0:T(8,128)(2,1)S(1)}, u32[]{:S(2)}, u32[]{:S(2)}) collective-permute-start(bf16[144,128]{1,0:T(8,128)(2,1)S(1)} %get-tuple-element.17.after_ref), channel_id=1, source_target_pairs={{128,0},{160,32},{192,64},{224,96},{256,128},{288,160},{320,192},{... | collective-permute-start | bytes 110600 | tf_op jit(solution)/shard_map/ppermute | solution.py:237
  48.2 1.3 %collective-permute-start.4 = (bf16[144,128]{1,0:T(8,128)(2,1)S(1)}, bf16[144,128]{1,0:T(8,128)(2,1)S(1)}, u32[]{:S(2)}, u32[]{:S(2)}) collective-permute-start(bf16[144,128]{1,0:T(8,128)(2,1)S(1)} %get-tuple-element.17.after_ref), channel_id=1, source_target_pairs={{256,0},{288,32},{320,64},{352,96},{384,128},{416,160},{448,192},{... | collective-permute-start | bytes 110600 | tf_op jit(solution)/shard_map/ppermute | solution.py:237
  49.5 1.3 %collective-permute-start.5 = (bf16[144,128]{1,0:T(8,128)(2,1)S(1)}, bf16[144,128]{1,0:T(8,128)(2,1)S(1)}, u32[]{:S(2)}, u32[]{:S(2)}) collective-permute-start(bf16[144,128]{1,0:T(8,128)(2,1)S(1)} %get-tuple-element.17.after_ref), channel_id=1, source_target_pairs={{384,0},{416,32},{448,64},{480,96},{385,1},{417,33},{449,65},{481,... | collective-permute-start | bytes 110600 | tf_op jit(solution)/shard_map/ppermute | solution.py:237
  50.8 0.0 copy-done.3
  50.8 0.0 copy-done.4
  50.8 0.0 copy-done.1
  50.8 0.0 copy-done.7
  50.8 5.7 %shard_map.58 = (f32[128,4096]{1,0:T(8,128)S(1)}, f32[128,32]{1,0:T(8,128)S(1)}, bf16[128,4096]{1,0:T(8,128)(2,1)S(1)}) custom-call(s32[1]{0:T(128)} %bitcast.base_ref, s32[8]{0:T(128)S(1)} %copy-done.7, bf16[128,4096]{1,0:T(8,128)(2,1)S(1)} %copy-done.1, bf16[128,4096]{1,0:T(8,128)(2,1)S(1)} %copy-done.4, bf16[128,4096]{1,0:T(8,128)(2,1)S(1)} %copy-done.3, ...), custom_call_target="tpu_custom_call" | custom-call | tf_op jit(solution)/shard_map/pallas_call | solution.py:225
  56.5 0.0 collective-permute-done.3.a_ref
  56.5 7.3 %collective-permute-done.4.b_ref = bf16[144,128]{1,0:T(8,128)(2,1)S(1)} collective-permute-done((bf16[144,128]{1,0:T(8,128)(2,1)S(1)}, bf16[144,128]{1,0:T(8,128)(2,1)S(1)}, u32[]{:S(2)}, u32[]{:S(2)}) %collective-permute-start.4) | collective-permute-done | bytes 36896 | tf_op jit(solution)/shard_map/ppermute | solution.py:237
  63.8 1.9 %collective-permute-done.5.c_ref = bf16[144,128]{1,0:T(8,128)(2,1)S(1)} collective-permute-done((bf16[144,128]{1,0:T(8,128)(2,1)S(1)}, bf16[144,128]{1,0:T(8,128)(2,1)S(1)}, u32[]{:S(2)}, u32[]{:S(2)}) %collective-permute-start.5) | collective-permute-done | bytes 36896 | tf_op jit(solution)/shard_map/ppermute | solution.py:237
  65.6 0.3 shard_map.59
  66.0 22.8 %all_to_all.11.states_ref = bf16[32,128,128]{2,1,0:T(8,128)(2,1)S(1)} all-to-all(bf16[32,128,128]{2,1,0:T(8,128)(2,1)S(1)} %shard_map.59), channel_id=1, replica_groups=mesh['z'=16,'core'=2,'x'=4,'y'=4] {'core','x','y'}, dimensions={0} | all-to-all | bytes 2097152 | tf_op jit(solution)/shard_map/all_to_all | solution.py:288
  88.7 1.6 %shard_map.60 = bf16[128,4096]{1,0:T(8,128)(2,1)} custom-call(bf16[128,4096]{1,0:T(8,128)(2,1)S(1)} %get-tuple-element.18.keys_ref, f32[128,32]{1,0:T(8,128)S(1)} %get-tuple-element.19.after_ref.tail_ref, f32[128,4096]{1,0:T(8,128)S(1)} %get-tuple-element.20.inside_ref, bf16[32,128,128]{2,1,0:T(8,128)(2,1)S(1)} %all_to_all.11.states_ref), custom_call_target="tpu_custom_call" | custom-call | tf_op jit(solution)/shard_map/pallas_call | solution.py:225
Async XLA Ops:
  0.0 1.2 %copy-start = (bf16[128,4096]{1,0:T(8,128)(2,1)S(1)}, bf16[128,4096]{1,0:T(8,128)(2,1)}, u32[]{:S(2)}) copy-start(bf16[128,4096]{1,0:T(8,128)(2,1)} %q_ref.1) | copy-start | bytes 3145732
  1.2 1.2 %copy-start.2 = (bf16[128,4096]{1,0:T(8,128)(2,1)S(1)}, bf16[128,4096]{1,0:T(8,128)(2,1)}, u32[]{:S(2)}) copy-start(bf16[128,4096]{1,0:T(8,128)(2,1)} %g_ref.1) | copy-start | bytes 3145732
  2.5 0.7 copy-start.5
  3.1 0.7 copy-start.6
  6.6 44.1 %copy-start.3 = (bf16[128,4096]{1,0:T(8,128)(2,1)S(1)}, bf16[128,4096]{1,0:T(8,128)(2,1)}, u32[]{:S(2)}) copy-start(bf16[128,4096]{1,0:T(8,128)(2,1)} %g_ref.1) | copy-start | bytes 3145732
  6.7 44.1 %copy-start.4 = (bf16[128,4096]{1,0:T(8,128)(2,1)S(1)}, bf16[128,4096]{1,0:T(8,128)(2,1)}, u32[]{:S(2)}) copy-start(bf16[128,4096]{1,0:T(8,128)(2,1)} %k_ref.1) | copy-start | bytes 3145732
  35.3 15.5 %copy-start.1 = (bf16[128,4096]{1,0:T(8,128)(2,1)S(1)}, bf16[128,4096]{1,0:T(8,128)(2,1)}, u32[]{:S(2)}) copy-start(bf16[128,4096]{1,0:T(8,128)(2,1)} %q_ref.1) | copy-start | bytes 3145732
  35.3 15.5 %copy-start.7 = (s32[8]{0:T(128)S(1)}, s32[8]{0:T(128)}, u32[]{:S(2)}) copy-start(s32[8]{0:T(128)} %lengths_ref.1) | copy-start | bytes 100
  35.7 4.7 %collective-permute-start = (bf16[144,128]{1,0:T(8,128)(2,1)S(1)}, bf16[144,128]{1,0:T(8,128)(2,1)S(1)}, u32[]{:S(2)}, u32[]{:S(2)}) collective-permute-start(bf16[144,128]{1,0:T(8,128)(2,1)S(1)} %get-tuple-element.16), channel_id=1, source_target_pairs={{32,0},{64,32},{96,64},{128,96},{160,128},{192,160},{224,192},{256... | collective-permute-start | bytes 110600 | tf_op jit(solution)/shard_map/ppermute | solution.py:237
  37.0 5.6 %collective-permute-start.1 = (bf16[144,128]{1,0:T(8,128)(2,1)S(1)}, bf16[144,128]{1,0:T(8,128)(2,1)S(1)}, u32[]{:S(2)}, u32[]{:S(2)}) collective-permute-start(bf16[144,128]{1,0:T(8,128)(2,1)S(1)} %get-tuple-element.16), channel_id=1, source_target_pairs={{64,0},{96,32},{128,64},{160,96},{192,128},{224,160},{256,192},{28... | collective-permute-start | bytes 110600 | tf_op jit(solution)/shard_map/ppermute | solution.py:237
  38.3 8.4 %collective-permute-start.2 = (bf16[144,128]{1,0:T(8,128)(2,1)S(1)}, bf16[144,128]{1,0:T(8,128)(2,1)S(1)}, u32[]{:S(2)}, u32[]{:S(2)}) collective-permute-start(bf16[144,128]{1,0:T(8,128)(2,1)S(1)} %get-tuple-element.16), channel_id=1, source_target_pairs={{96,0},{128,32},{160,64},{192,96},{224,128},{256,160},{288,192},{3... | collective-permute-start | bytes 110600 | tf_op jit(solution)/shard_map/ppermute | solution.py:237
  46.9 9.6 %collective-permute-start.3 = (bf16[144,128]{1,0:T(8,128)(2,1)S(1)}, bf16[144,128]{1,0:T(8,128)(2,1)S(1)}, u32[]{:S(2)}, u32[]{:S(2)}) collective-permute-start(bf16[144,128]{1,0:T(8,128)(2,1)S(1)} %get-tuple-element.17.after_ref), channel_id=1, source_target_pairs={{128,0},{160,32},{192,64},{224,96},{256,128},{288,160},{320,192},{... | collective-permute-start | bytes 110600 | tf_op jit(solution)/shard_map/ppermute | solution.py:237
  48.2 15.6 %collective-permute-start.4 = (bf16[144,128]{1,0:T(8,128)(2,1)S(1)}, bf16[144,128]{1,0:T(8,128)(2,1)S(1)}, u32[]{:S(2)}, u32[]{:S(2)}) collective-permute-start(bf16[144,128]{1,0:T(8,128)(2,1)S(1)} %get-tuple-element.17.after_ref), channel_id=1, source_target_pairs={{256,0},{288,32},{320,64},{352,96},{384,128},{416,160},{448,192},{... | collective-permute-start | bytes 110600 | tf_op jit(solution)/shard_map/ppermute | solution.py:237
  49.5 16.1 %collective-permute-start.5 = (bf16[144,128]{1,0:T(8,128)(2,1)S(1)}, bf16[144,128]{1,0:T(8,128)(2,1)S(1)}, u32[]{:S(2)}, u32[]{:S(2)}) collective-permute-start(bf16[144,128]{1,0:T(8,128)(2,1)S(1)} %get-tuple-element.17.after_ref), channel_id=1, source_target_pairs={{384,0},{416,32},{448,64},{480,96},{385,1},{417,33},{449,65},{481,... | collective-permute-start | bytes 110600 | tf_op jit(solution)/shard_map/ppermute | solution.py:237

commit v3 on v2

--- a/solution.py
+++ b/solution.py
@@ -1,3 +1,4 @@
+import functools
 import jax
 import jax.numpy as jnp
 from jax import lax
@@ -6,12 +7,13 @@
 from jax.sharding import Mesh, PartitionSpec as P
 
 HEAD = 128
-PAD = 16
+PAD = 8
+HALF = 64
 NEG = -1e30
 TINY = 1e-36
 OCTAVES = 120.0
 GROUPS = 4
-PLANE = ("core", "x", "y")
+GROUP = ("zl", "core", "x", "y")
 
 
 def token_segments(lengths_ref, positions):
@@ -105,12 +107,16 @@
             jnp.concatenate([hi, lo], axis=0),
             preferred_element_type=jnp.float32,
         )
-        out_ref[h, 0:HEAD, :] = summary.astype(jnp.bfloat16)
-        out_ref[h, HEAD : HEAD + PAD, :] = pad_rows([f[:, h : h + 1] for f in factors])
+        summary = summary.astype(jnp.bfloat16)
+        extra = pad_rows([f[:, h : h + 1] for f in factors])
+        for part in range(HEAD // HALF):
+            slot = h * (HEAD // HALF) + part
+            out_ref[slot, 0:HALF, :] = summary[part * HALF : (part + 1) * HALF, :]
+            out_ref[slot, HALF : HALF + PAD, :] = extra
 
 
 def inside_kernel(
-    base_ref, lengths_ref, q_ref, k_ref, g_ref, decay_ref, after_ref, inside_ref, tail_ref, keys_ref
+    first, base_ref, lengths_ref, q_ref, k_ref, g_ref, decay_ref, after_ref, inside_ref, tail_ref, keys_ref
 ):
     rows = q_ref.shape[0]
     heads = decay_ref.shape[0]
@@ -123,20 +129,22 @@
     t_pos = lax.broadcasted_iota(jnp.int32, (rows, rows), 1)
     same = token_segments(lengths_ref, base + i_pos) == token_segments(lengths_ref, base + t_pos)
     bias = jnp.where(same & (t_pos >= i_pos), 0.0, NEG)
-    for h in range(heads):
+    for n in range(inside_ref.shape[1] // HEAD):
+        h = first + n
         cols = slice(h * HEAD, (h + 1) * HEAD)
+        here = slice(n * HEAD, (n + 1) * HEAD)
         keys = k_ref[:, cols]
-        keys_ref[:, cols] = keys
+        keys_ref[:, here] = keys
         scores = lax.dot_general(
             keys, q_ref[:, cols], (((1,), (1,)), ((), ())), preferred_element_type=jnp.float32
         )
         gaps = jnp.minimum(cum_rows[h : h + 1, :] - cum[:, h : h + 1], 0.0)
         weights = (jnp.exp(gaps + bias) * scores).astype(jnp.bfloat16)
-        inside_ref[:, cols] = jnp.dot(weights, g_ref[:, cols], preferred_element_type=jnp.float32)
+        inside_ref[:, here] = jnp.dot(weights, g_ref[:, cols], preferred_element_type=jnp.float32)
 
 
 def factor_row(ref, p):
-    tail = ref[p, HEAD : HEAD + PAD, :].astype(jnp.float32)
+    tail = ref[p, HALF : HALF + PAD, :].astype(jnp.float32)
     return tail[0:1, :] + tail[1:2, :] + tail[2:3, :]
 
 
@@ -145,24 +153,24 @@
     largest = jnp.max(jnp.max(size, axis=0, keepdims=True), axis=1, keepdims=True)
     bound = (largest * 1.01 + TINY).astype(jnp.bfloat16).astype(jnp.float32)
     code = jnp.exp2(size * ((2.0 * OCTAVES) / bound) - OCTAVES)
-    ref[0:HEAD, :] = jnp.where(state < 0.0, -code, code).astype(jnp.bfloat16)
-    ref[HEAD : HEAD + PAD, :] = pad_rows([bound] + split3(factor))
+    ref[0:HALF, :] = jnp.where(state < 0.0, -code, code).astype(jnp.bfloat16)
+    ref[HALF : HALF + PAD, :] = pad_rows([bound] + split3(factor))
 
 
 def read_packet(ref):
-    code = ref[0:HEAD, :].astype(jnp.float32)
-    tail = ref[HEAD : HEAD + PAD, :].astype(jnp.float32)
+    code = ref[0:HALF, :].astype(jnp.float32)
+    tail = ref[HALF : HALF + PAD, :].astype(jnp.float32)
     octaves = jnp.log2(jnp.maximum(jnp.abs(code), 2.0**-OCTAVES)) + OCTAVES
     size = octaves * (tail[0:1, :] * (0.5 / OCTAVES))
     return jnp.where(code < 0.0, -size, size), tail[1:2, :] + tail[2:3, :] + tail[3:4, :]
 
 
 def reduce_kernel(parts_ref, total_ref, factor_ref, packet_ref):
-    state = jnp.zeros((HEAD, HEAD), jnp.float32)
+    state = jnp.zeros((HALF, HEAD), jnp.float32)
     factor = jnp.ones((1, HEAD), jnp.float32)
     for p in reversed(range(parts_ref.shape[0])):
         f = factor_row(parts_ref, p)
-        state = parts_ref[p, 0:HEAD, :].astype(jnp.float32) + f * state
+        state = parts_ref[p, 0:HALF, :].astype(jnp.float32) + f * state
         factor = factor * f
     total_ref[...] = state
     factor_ref[...] = factor
@@ -178,33 +186,40 @@
     return state, factor
 
 
-def join_kernel(total_ref, factor_ref, a_ref, b_ref, c_ref, near_ref, near_factor_ref, packet_ref):
-    state, factor = join([a_ref, b_ref, c_ref])
+def join_kernel(after_ref, total_ref, factor_ref, *refs):
+    near_ref, near_factor_ref, packet_ref = refs[-3:]
+    state, factor = join(refs[:-3])
     near_ref[...] = state
     near_factor_ref[...] = factor
     own = factor_ref[...]
     write_packet(packet_ref, total_ref[...] + own * state, own * factor)
 
 
-def states_kernel(parts_ref, near_ref, near_factor_ref, a_ref, b_ref, c_ref, after_ref, out_ref):
-    far, far_factor = join([a_ref, b_ref, c_ref])
+def states_kernel(after_ref, parts_ref, near_ref, near_factor_ref, *refs):
+    out_ref = refs[-1]
+    far, far_factor = join(refs[:-1])
     state = near_ref[...] + near_factor_ref[...] * far
     for p in reversed(range(parts_ref.shape[0])):
         out_ref[p] = state.astype(jnp.bfloat16)
-        state = parts_ref[p, 0:HEAD, :].astype(jnp.float32) + factor_row(parts_ref, p) * state
-
-
-def output_kernel(keys_ref, tail_ref, inside_ref, states_ref, out_hbm, out_buf, sems):
+        state = parts_ref[p, 0:HALF, :].astype(jnp.float32) + factor_row(parts_ref, p) * state
+
+
+def output_kernel(tail_ref, states_ref, *refs):
+    halves = refs[:-3]
+    out_hbm, out_buf, sems = refs[-3:]
     groups = sems.shape[0]
     width = out_buf.shape[1] // groups
     tail = tail_ref[...]
     copies = []
+    each = states_ref.shape[0] // (len(halves) // 2)
     for h in range(states_ref.shape[0]):
+        keys_ref, inside_ref = halves[h // each * 2 : h // each * 2 + 2]
         cols = slice(h * HEAD, (h + 1) * HEAD)
+        here = slice(h % each * HEAD, (h % each + 1) * HEAD)
         carried = lax.dot_general(
-            keys_ref[:, cols], states_ref[h], (((1,), (1,)), ((), ())), preferred_element_type=jnp.float32
+            keys_ref[:, here], states_ref[h], (((1,), (1,)), ((), ())), preferred_element_type=jnp.float32
         )
-        out_buf[:, cols] = (inside_ref[:, cols] + tail[:, h : h + 1] * carried).astype(jnp.bfloat16)
+        out_buf[:, cols] = (inside_ref[:, here] + tail[:, h : h + 1] * carried).astype(jnp.bfloat16)
         if ((h + 1) * HEAD) % width == 0:
             n = h * HEAD // width
             span = slice(n * width, (n + 1) * width)
@@ -233,23 +248,27 @@
 
 
 def from_ahead(x, by):
-    size = lax.axis_size("z")
-    return lax.ppermute(x, "z", [(i + by, i) for i in range(size - by)])
+    size = lax.axis_size("zh")
+    return lax.ppermute(x, "zh", [(i + by, i) for i in range(size - by)])
 
 
 def body(query_vectors, key_vectors, out_grad, log_decay, doc_lengths):
     rows, heads = log_decay.shape
     columns = query_vectors.shape[1]
-    index = lax.axis_index(("z", "core", "x", "y"))
+    slots = columns // HALF
+    index = lax.axis_index(("zh",) + GROUP)
     base = (index * rows).astype(jnp.int32).reshape(1)
     decay_rows = log_decay.T
     shape = jax.ShapeDtypeStruct
     dma = pltpu.SemaphoreType.DMA
+    pinned = [
+        pltpu.with_memory_space_constraint(x, pltpu.HBM) for x in (doc_lengths, query_vectors, out_grad, decay_rows)
+    ]
     summaries = call(
         summary_kernel,
-        shape((heads, HEAD + PAD, HEAD), jnp.bfloat16),
+        shape((slots, HALF + PAD, HEAD), jnp.bfloat16),
         [SMEM] + [REST] * 4,
-        (base, doc_lengths, query_vectors, out_grad, decay_rows),
+        (base, *pinned),
         scratch=(
             pltpu.VMEM((rows, columns), jnp.bfloat16),
             pltpu.VMEM((rows, columns), jnp.bfloat16),
@@ -259,38 +278,44 @@
             dma((2,)),
         ),
     )
-    parts = lax.all_to_all(summaries, PLANE, split_axis=0, concat_axis=0, tiled=True)
-    state = shape((HEAD, HEAD), jnp.float32)
+    parts = lax.all_to_all(summaries, GROUP, split_axis=0, concat_axis=0, tiled=True)
+    state = shape((HALF, HEAD), jnp.float32)
     factor = shape((1, HEAD), jnp.float32)
-    packet = shape((HEAD + PAD, HEAD), jnp.bfloat16)
+    packet = shape((HALF + PAD, HEAD), jnp.bfloat16)
     total, total_factor, own = call(reduce_kernel, (state, factor, packet), [VMEM], (parts,))
-    ahead = [from_ahead(own, by) for by in (1, 2, 3)]
+
+    def inside_part(number, after):
+        return call(
+            functools.partial(inside_kernel, number * heads // 2),
+            (
+                shape((rows, columns // 2), jnp.float32),
+                shape((rows, heads), jnp.float32),
+                shape((rows, columns // 2), jnp.bfloat16),
+            ),
+            [SMEM] * 2 + [VMEM] * 5,
+            (base, doc_lengths, query_vectors, key_vectors, out_grad, decay_rows, after),
+        )
+
+    ahead = [from_ahead(own, by) for by in (1, 2)]
+    inside_a, tail, keys_a = inside_part(0, own)
     near, near_factor, wide = call(
-        join_kernel, (state, factor, packet), [VMEM] * 5, (total, total_factor, *ahead)
-    )
-    far = [from_ahead(wide, by) for by in (4, 8, 12)]
-    inside, tail, keys = call(
-        inside_kernel,
-        (
-            shape((rows, columns), jnp.float32),
-            shape((rows, heads), jnp.float32),
-            shape((rows, columns), jnp.bfloat16),
-        ),
-        [SMEM] * 2 + [VMEM] * 5,
-        (base, doc_lengths, query_vectors, key_vectors, out_grad, decay_rows, wide),
-    )
+        join_kernel, (state, factor, packet), [VMEM] * 5, (tail, total, total_factor, *ahead)
+    )
+    far = [from_ahead(wide, by) for by in (3, 6)]
+    inside_b, tail_b, keys_b = inside_part(1, wide)
     states = call(
         states_kernel,
-        shape((heads, HEAD, HEAD), jnp.bfloat16),
-        [VMEM] * 7,
-        (parts, near, near_factor, *far, tail),
-    )
-    mine = lax.all_to_all(states, PLANE, split_axis=0, concat_axis=0, tiled=True)
+        shape((slots, HALF, HEAD), jnp.bfloat16),
+        [VMEM] * 6,
+        (tail_b, parts, near, near_factor, *far),
+    )
+    mine = lax.all_to_all(states, GROUP, split_axis=0, concat_axis=0, tiled=True)
+    mine = mine.reshape(heads, HEAD, HEAD)
     return call(
         output_kernel,
         shape((rows, columns), jnp.bfloat16),
-        [VMEM] * 4,
-        (keys, tail, inside, mine),
+        [VMEM] * 6,
+        (tail, mine, keys_a, inside_a, keys_b, inside_b),
         out_specs=REST,
         scratch=(pltpu.VMEM((rows, columns), jnp.bfloat16), dma((GROUPS,))),
     )
@@ -299,9 +324,9 @@
 def solution(mesh):
     side = 4
     fine = Mesh(
-        mesh.devices.reshape(mesh.shape["seq"] // 2, 2, side, mesh.shape["head"] // side), ("z", "core", "x", "y")
-    )
-    tokens = P(("z", "core", "x", "y"), None)
+        mesh.devices.reshape(mesh.shape["seq"] // 4, 2, 2, side, mesh.shape["head"] // side), ("zh",) + GROUP
+    )
+    tokens = P(("zh",) + GROUP, None)
     return jax.shard_map(
         body, mesh=fine, in_specs=(tokens, tokens, tokens, tokens, P()), out_specs=tokens, check_vma=False
     )

time: 91 us -> 81.9 us (0.900)
  waiting for transfers between devices: 16.3 us -> 11.1 us
  local copies, waits for them, and re-layouts: 3.82 us -> 0.02 us
  starting transfers between devices: 7.75 us -> 5.17 us
  Pallas kernels: 11 us -> 12.5 us
  blocking collectives: 51.4 us -> 52.7 us
    ppermute x6 -> x4, waiting for transfers between devices: 16.3 us -> 11.1 us  [from_ahead(): return lax.ppermute(x, 'zh', [(i + by, i) for i in range(size - by)])]
    unnamed x16 -> x10, local copies, waits for them, and re-layouts: 3.82 us -> 0.02 us
    ppermute x6 -> x4, starting transfers between devices: 7.75 us -> 5.17 us  [from_ahead(): return lax.ppermute(x, 'zh', [(i + by, i) for i in range(size - by)])]
    pallas_call x6 -> x7, Pallas kernels: 11 us -> 12.5 us  [call(): pl.pallas_call(kernel, out_shape=out_shape, in_specs=in_specs, out_specs=...]
    all_to_all x2, blocking collectives: 51.4 us -> 52.7 us  [the longest x1 28.4 us: body(): lax.all_to_all(summaries, GROUP, split_axis=0, concat_axis=0, tiled=True)]
  transfers between devices with their start and end apart: 6 -> 4, of which waited for: 5 -> 2; matrix products, arithmetic and copies ran while one was open for 0% -> 0% of each run, Pallas kernels for 6% -> 8%
where the time goes in v3:
time: 81.9 us; the launch traced here: 81.6 us
  blocking collectives  52.7 us (64%)
  Pallas kernels  12.5 us (15%)
  waiting for transfers between devices  11.1 us (14%)
  starting transfers between devices  5.17 us (6%)
    all_to_all x1, blocking collectives, body(): lax.all_to_all(summaries, GROUP, split_axis=0, concat_axis=0, tiled=True)  28.4 us
    all_to_all x1, blocking collectives, body(): lax.all_to_all(states, GROUP, split_axis=0, concat_axis=0, tiled=True)  24.3 us
    pallas_call x7, Pallas kernels, call(): pl.pallas_call(kernel, out_shape=out_shape, in_specs=in_specs, out_specs=...  12.5 us
    ppermute x4, waiting for transfers between devices, from_ahead(): return lax.ppermute(x, 'zh', [(i + by, i) for i in range(size - by)])  11.1 us
    ppermute x4, starting transfers between devices, from_ahead(): return lax.ppermute(x, 'zh', [(i + by, i) for i in range(size - by)])  5.17 us
  transfers between devices with their start and end apart: 4, of which 2 were waited for; matrix products, arithmetic and copies ran while one was open for 0% of the time, Pallas kernels for 8%

profile of v3, /device:TPU:1, one launch (start us, length us, event | category | flops | bytes accessed | tf_op | source)
XLA Modules:
  0.0 81.6 jit_solution(11769320628793387994)
XLA Ops:
  0.0 3.6 %shard_map.55 = bf16[64,72,128]{2,1,0:T(8,128)(2,1)S(1)} custom-call(s32[1]{0:T(128)} %bitcast.base_ref, s32[8]{0:T(128)} %lengths_ref.3, bf16[128,4096]{1,0:T(8,128)(2,1)} %q_ref.3, bf16[128,4096]{1,0:T(8,128)(2,1)} %g_ref.3, bf16[32,128]{1,0:T(8,128)(2,1)} %bitcast.4), custom_call_target="tpu_custom_call" | custom-call | tf_op jit(solution)/shard_map/pallas_call | solution.py:240
  3.6 0.0 copy-start.1
  3.7 0.0 copy-start.2
  3.7 28.4 %all_to_all.10.parts_ref = bf16[64,72,128]{2,1,0:T(8,128)(2,1)S(1)} all-to-all(bf16[64,72,128]{2,1,0:T(8,128)(2,1)S(1)} %shard_map.55), channel_id=1, replica_groups=mesh['zh'=8,'zl'=2,'core'=2,'x'=4,'y'=4] {'zl','core','x','y'}, dimensions={0} | all-to-all | bytes 2359296 | tf_op jit(solution)/shard_map/all_to_all | solution.py:281
  32.1 0.0 copy-start
  32.1 0.0 copy-start.3
  32.1 0.0 copy-start.4
  32.1 0.4 shard_map.56
  32.5 1.3 %collective-permute-start.1 = (bf16[72,128]{1,0:T(8,128)(2,1)S(1)}, bf16[72,128]{1,0:T(8,128)(2,1)S(1)}, u32[]{:S(2)}, u32[]{:S(2)}) collective-permute-start(bf16[72,128]{1,0:T(8,128)(2,1)S(1)} %get-tuple-element.17.after_ref), channel_id=1, source_target_pairs={{128,0},{192,64},{256,128},{320,192},{384,256},{448,320},{129,1},{... | collective-permute-start | bytes 55304 | tf_op jit(solution)/shard_map/ppermute | solution.py:252
  33.8 1.3 %collective-permute-start = (bf16[72,128]{1,0:T(8,128)(2,1)S(1)}, bf16[72,128]{1,0:T(8,128)(2,1)S(1)}, u32[]{:S(2)}, u32[]{:S(2)}) collective-permute-start(bf16[72,128]{1,0:T(8,128)(2,1)S(1)} %get-tuple-element.17.after_ref), channel_id=1, source_target_pairs={{64,0},{128,64},{192,128},{256,192},{320,256},{384,320},{448,384},... | collective-permute-start | bytes 55304 | tf_op jit(solution)/shard_map/ppermute | solution.py:252
  35.1 0.0 copy-done.1
  35.1 0.0 copy-done.2
  35.1 0.0 copy-done
  35.1 0.0 copy-done.3
  35.1 0.0 copy-done.4
  35.1 3.2 %shard_map.57 = (f32[128,2048]{1,0:T(8,128)S(1)}, f32[128,32]{1,0:T(8,128)S(1)}, bf16[128,2048]{1,0:T(8,128)(2,1)S(1)}) custom-call(s32[1]{0:T(128)} %bitcast.base_ref, s32[8]{0:T(128)S(1)} %copy-done.4, bf16[128,4096]{1,0:T(8,128)(2,1)S(1)} %copy-done, bf16[128,4096]{1,0:T(8,128)(2,1)S(1)} %copy-done.2, bf16[128,4096]{1,0:T(8,128)(2,1)S(1)} %copy-done.1, ...), custom_call_target="tpu_custom_call" | custom-call | tf_op jit(solution)/shard_map/pallas_call | solution.py:240
  38.3 4.1 %collective-permute-done.1.refs_1_ = bf16[72,128]{1,0:T(8,128)(2,1)S(1)} collective-permute-done((bf16[72,128]{1,0:T(8,128)(2,1)S(1)}, bf16[72,128]{1,0:T(8,128)(2,1)S(1)}, u32[]{:S(2)}, u32[]{:S(2)}) %collective-permute-start.1) | collective-permute-done | bytes 18464 | tf_op jit(solution)/shard_map/ppermute | solution.py:252
  42.4 0.0 collective-permute-done.refs_0_
  42.4 0.1 shard_map.58
  42.6 1.3 %collective-permute-start.3 = (bf16[72,128]{1,0:T(8,128)(2,1)S(1)}, bf16[72,128]{1,0:T(8,128)(2,1)S(1)}, u32[]{:S(2)}, u32[]{:S(2)}) collective-permute-start(bf16[72,128]{1,0:T(8,128)(2,1)S(1)} %get-tuple-element.21.after_ref), channel_id=1, source_target_pairs={{384,0},{448,64},{385,1},{449,65},{386,2},{450,66},{387,3},{451,67... | collective-permute-start | bytes 55304 | tf_op jit(solution)/shard_map/ppermute | solution.py:252
  43.9 1.3 %collective-permute-start.2 = (bf16[72,128]{1,0:T(8,128)(2,1)S(1)}, bf16[72,128]{1,0:T(8,128)(2,1)S(1)}, u32[]{:S(2)}, u32[]{:S(2)}) collective-permute-start(bf16[72,128]{1,0:T(8,128)(2,1)S(1)} %get-tuple-element.21.after_ref), channel_id=1, source_target_pairs={{192,0},{256,64},{320,128},{384,192},{448,256},{193,1},{257,65},{3... | collective-permute-start | bytes 55304 | tf_op jit(solution)/shard_map/ppermute | solution.py:252
  45.2 3.2 %shard_map.59 = (f32[128,2048]{1,0:T(8,128)S(1)}, f32[128,32]{1,0:T(8,128)S(1)}, bf16[128,2048]{1,0:T(8,128)(2,1)S(1)}) custom-call(s32[1]{0:T(128)} %bitcast.base_ref, s32[8]{0:T(128)S(1)} %copy-done.4, bf16[128,4096]{1,0:T(8,128)(2,1)S(1)} %copy-done, bf16[128,4096]{1,0:T(8,128)(2,1)S(1)} %copy-done.2, bf16[128,4096]{1,0:T(8,128)(2,1)S(1)} %copy-done.1, ...), custom_call_target="tpu_custom_call" | custom-call | tf_op jit(solution)/shard_map/pallas_call | solution.py:240
  48.4 7.0 %collective-permute-done.3.refs_1_ = bf16[72,128]{1,0:T(8,128)(2,1)S(1)} collective-permute-done((bf16[72,128]{1,0:T(8,128)(2,1)S(1)}, bf16[72,128]{1,0:T(8,128)(2,1)S(1)}, u32[]{:S(2)}, u32[]{:S(2)}) %collective-permute-start.3) | collective-permute-done | bytes 18464 | tf_op jit(solution)/shard_map/ppermute | solution.py:252
  55.4 0.0 collective-permute-done.2.refs_0_
  55.4 0.3 shard_map.60
  55.7 24.3 %all_to_all.11 = bf16[64,64,128]{2,1,0:T(8,128)(2,1)S(1)} all-to-all(bf16[64,64,128]{2,1,0:T(8,128)(2,1)S(1)} %shard_map.60), channel_id=1, replica_groups=mesh['zh'=8,'zl'=2,'core'=2,'x'=4,'y'=4] {'zl','core','x','y'}, dimensions={0} | all-to-all | bytes 2097152 | tf_op jit(solution)/shard_map/all_to_all | solution.py:312
  80.0 1.6 %shard_map.61 = bf16[128,4096]{1,0:T(8,128)(2,1)} custom-call(f32[128,32]{1,0:T(8,128)S(1)} %get-tuple-element.18.after_ref.tail_ref, bf16[32,128,128]{2,1,0:T(8,128)(2,1)S(1)} %bitcast.3, bf16[128,2048]{1,0:T(8,128)(2,1)S(1)} %get-tuple-element.25.refs_0_, f32[128,2048]{1,0:T(8,128)S(1)} %get-tuple-element.26.refs_1_, ...), custom_call_target="tpu_custom_call" | custom-call | tf_op jit(solution)/shard_map/pallas_call | solution.py:240
Async XLA Ops:
  3.6 31.4 %copy-start.1 = (bf16[128,4096]{1,0:T(8,128)(2,1)S(1)}, bf16[128,4096]{1,0:T(8,128)(2,1)}, u32[]{:S(2)}) copy-start(bf16[128,4096]{1,0:T(8,128)(2,1)} %g_ref.3) | copy-start | bytes 3145732
  3.7 31.4 %copy-start.2 = (bf16[128,4096]{1,0:T(8,128)(2,1)S(1)}, bf16[128,4096]{1,0:T(8,128)(2,1)}, u32[]{:S(2)}) copy-start(bf16[128,4096]{1,0:T(8,128)(2,1)} %k_ref.3) | copy-start | bytes 3145732
  32.1 3.0 %copy-start = (bf16[128,4096]{1,0:T(8,128)(2,1)S(1)}, bf16[128,4096]{1,0:T(8,128)(2,1)}, u32[]{:S(2)}) copy-start(bf16[128,4096]{1,0:T(8,128)(2,1)} %q_ref.3) | copy-start | bytes 3145732
  32.1 3.0 %copy-start.3 = (bf16[128,32]{0,1:T(8,128)(2,1)S(1)}, bf16[128,32]{0,1:T(8,128)(2,1)}, u32[]{:S(2)}) copy-start(bf16[128,32]{0,1:T(8,128)(2,1)} %param.8) | copy-start | bytes 24580
  32.1 3.0 %copy-start.4 = (s32[8]{0:T(128)S(1)}, s32[8]{0:T(128)}, u32[]{:S(2)}) copy-start(s32[8]{0:T(128)} %lengths_ref.3) | copy-start | bytes 100
  32.5 10.0 %collective-permute-start.1 = (bf16[72,128]{1,0:T(8,128)(2,1)S(1)}, bf16[72,128]{1,0:T(8,128)(2,1)S(1)}, u32[]{:S(2)}, u32[]{:S(2)}) collective-permute-start(bf16[72,128]{1,0:T(8,128)(2,1)S(1)} %get-tuple-element.17.after_ref), channel_id=1, source_target_pairs={{128,0},{192,64},{256,128},{320,192},{384,256},{448,320},{129,1},{... | collective-permute-start | bytes 55304 | tf_op jit(solution)/shard_map/ppermute | solution.py:252
  33.8 8.7 %collective-permute-start = (bf16[72,128]{1,0:T(8,128)(2,1)S(1)}, bf16[72,128]{1,0:T(8,128)(2,1)S(1)}, u32[]{:S(2)}, u32[]{:S(2)}) collective-permute-start(bf16[72,128]{1,0:T(8,128)(2,1)S(1)} %get-tuple-element.17.after_ref), channel_id=1, source_target_pairs={{64,0},{128,64},{192,128},{256,192},{320,256},{384,320},{448,384},... | collective-permute-start | bytes 55304 | tf_op jit(solution)/shard_map/ppermute | solution.py:252
  42.6 12.8 %collective-permute-start.3 = (bf16[72,128]{1,0:T(8,128)(2,1)S(1)}, bf16[72,128]{1,0:T(8,128)(2,1)S(1)}, u32[]{:S(2)}, u32[]{:S(2)}) collective-permute-start(bf16[72,128]{1,0:T(8,128)(2,1)S(1)} %get-tuple-element.21.after_ref), channel_id=1, source_target_pairs={{384,0},{448,64},{385,1},{449,65},{386,2},{450,66},{387,3},{451,67... | collective-permute-start | bytes 55304 | tf_op jit(solution)/shard_map/ppermute | solution.py:252
  43.9 11.5 %collective-permute-start.2 = (bf16[72,128]{1,0:T(8,128)(2,1)S(1)}, bf16[72,128]{1,0:T(8,128)(2,1)S(1)}, u32[]{:S(2)}, u32[]{:S(2)}) collective-permute-start(bf16[72,128]{1,0:T(8,128)(2,1)S(1)} %get-tuple-element.21.after_ref), channel_id=1, source_target_pairs={{192,0},{256,64},{320,128},{384,192},{448,256},{193,1},{257,65},{3... | collective-permute-start | bytes 55304 | tf_op jit(solution)/shard_map/ppermute | solution.py:252

commit v4 on v3

--- a/solution.py
+++ b/solution.py
@@ -9,10 +9,13 @@
 HEAD = 128
 PAD = 8
 HALF = 64
+RADICES = (2, 4)
+ORDERS = ((1,), (2, 6, 4))
+ROW_PARTS = 1
 NEG = -1e30
 TINY = 1e-36
 OCTAVES = 120.0
-GROUPS = 4
+GROUPS = 2
 GROUP = ("zl", "core", "x", "y")
 
 
@@ -66,7 +69,7 @@
 ):
     rows = q_buf.shape[0]
     heads = decay_ref.shape[0]
-    groups = sems.shape[1]
+    groups = sems.shape[1] // ROW_PARTS
     width = q_buf.shape[1] // groups
     small = [
         pltpu.make_async_copy(lengths_hbm, lengths_ref, small_sems.at[0]),
@@ -77,10 +80,13 @@
     large = []
     for n in range(groups):
         span = slice(n * width, (n + 1) * width)
-        pair = [
-            pltpu.make_async_copy(q_hbm.at[:, span], q_buf.at[:, span], sems.at[0, n]),
-            pltpu.make_async_copy(g_hbm.at[:, span], g_buf.at[:, span], sems.at[1, n]),
-        ]
+        pair = []
+        for r in range(ROW_PARTS):
+            band = slice(r * rows // ROW_PARTS, (r + 1) * rows // ROW_PARTS)
+            pair += [
+                pltpu.make_async_copy(q_hbm.at[band, span], q_buf.at[band, span], sems.at[0, n * ROW_PARTS + r]),
+                pltpu.make_async_copy(g_hbm.at[band, span], g_buf.at[band, span], sems.at[1, n * ROW_PARTS + r]),
+            ]
         for copy in pair:
             copy.start()
         large.append(pair)
@@ -177,45 +183,51 @@
     write_packet(packet_ref, state, factor)
 
 
-def join(refs):
-    state, factor = read_packet(refs[-1])
-    for ref in reversed(refs[:-1]):
+def join(shifts, refs):
+    state = jnp.zeros((HALF, HEAD), jnp.float32)
+    factor = jnp.ones((1, HEAD), jnp.float32)
+    for by, ref in sorted(zip(shifts, refs), key=lambda item: -item[0]):
         s, f = read_packet(ref)
         state = s + f * state
         factor = f * factor
     return state, factor
 
 
-def join_kernel(after_ref, total_ref, factor_ref, *refs):
-    near_ref, near_factor_ref, packet_ref = refs[-3:]
-    state, factor = join(refs[:-3])
+def join_kernel(shifts, after_ref, total_ref, factor_ref, *refs):
+    refs, outs = refs[:-3], refs[-3:]
+    near_ref, near_factor_ref, packet_ref = outs
+    state, factor = join(shifts, refs[-len(shifts) :])
+    if len(refs) > len(shifts):
+        state = refs[0][...] + refs[1][...] * state
+        factor = refs[1][...] * factor
     near_ref[...] = state
     near_factor_ref[...] = factor
     own = factor_ref[...]
     write_packet(packet_ref, total_ref[...] + own * state, own * factor)
 
 
-def states_kernel(after_ref, parts_ref, near_ref, near_factor_ref, *refs):
+def states_kernel(shifts, after_ref, parts_ref, near_ref, near_factor_ref, *refs):
     out_ref = refs[-1]
-    far, far_factor = join(refs[:-1])
+    far, far_factor = join(shifts, refs[:-1])
     state = near_ref[...] + near_factor_ref[...] * far
     for p in reversed(range(parts_ref.shape[0])):
         out_ref[p] = state.astype(jnp.bfloat16)
         state = parts_ref[p, 0:HALF, :].astype(jnp.float32) + factor_row(parts_ref, p) * state
 
 
-def output_kernel(tail_ref, states_ref, *refs):
-    halves = refs[:-3]
+def output_kernel(pieces, tail_ref, states_ref, *refs):
+    parts = refs[:-3]
     out_hbm, out_buf, sems = refs[-3:]
+    owner = [(n, h - first) for n, (first, count) in enumerate(pieces) for h in range(first, first + count)]
     groups = sems.shape[0]
     width = out_buf.shape[1] // groups
     tail = tail_ref[...]
     copies = []
-    each = states_ref.shape[0] // (len(halves) // 2)
     for h in range(states_ref.shape[0]):
-        keys_ref, inside_ref = halves[h // each * 2 : h // each * 2 + 2]
+        n, place = owner[h]
+        keys_ref, inside_ref = parts[2 * n : 2 * n + 2]
         cols = slice(h * HEAD, (h + 1) * HEAD)
-        here = slice(h % each * HEAD, (h % each + 1) * HEAD)
+        here = slice(place * HEAD, (place + 1) * HEAD)
         carried = lax.dot_general(
             keys_ref[:, here], states_ref[h], (((1,), (1,)), ((), ())), preferred_element_type=jnp.float32
         )
@@ -274,7 +286,7 @@
             pltpu.VMEM((rows, columns), jnp.bfloat16),
             pltpu.VMEM((heads, rows), jnp.bfloat16),
             pltpu.SMEM(doc_lengths.shape, jnp.int32),
-            dma((2, GROUPS)),
+            dma((2, GROUPS * ROW_PARTS)),
             dma((2,)),
         ),
     )
@@ -284,38 +296,52 @@
     packet = shape((HALF + PAD, HEAD), jnp.bfloat16)
     total, total_factor, own = call(reduce_kernel, (state, factor, packet), [VMEM], (parts,))
 
+    count = len(RADICES)
+    edges = [heads * n // count for n in range(count + 1)]
+    pieces = tuple((edges[n], edges[n + 1] - edges[n]) for n in range(count))
+
     def inside_part(number, after):
+        first, here = pieces[number]
         return call(
-            functools.partial(inside_kernel, number * heads // 2),
+            functools.partial(inside_kernel, first),
             (
-                shape((rows, columns // 2), jnp.float32),
+                shape((rows, here * HEAD), jnp.float32),
                 shape((rows, heads), jnp.float32),
-                shape((rows, columns // 2), jnp.bfloat16),
+                shape((rows, here * HEAD), jnp.bfloat16),
             ),
             [SMEM] * 2 + [VMEM] * 5,
             (base, doc_lengths, query_vectors, key_vectors, out_grad, decay_rows, after),
         )
 
-    ahead = [from_ahead(own, by) for by in (1, 2)]
-    inside_a, tail, keys_a = inside_part(0, own)
-    near, near_factor, wide = call(
-        join_kernel, (state, factor, packet), [VMEM] * 5, (tail, total, total_factor, *ahead)
-    )
-    far = [from_ahead(wide, by) for by in (3, 6)]
-    inside_b, tail_b, keys_b = inside_part(1, wide)
+    step = 1
+    near = ()
+    done = []
+    for number, radix in enumerate(RADICES):
+        shifts = ORDERS[number]
+        ahead = [from_ahead(own, by) for by in shifts]
+        inside, tail, keys = inside_part(number, own)
+        done += [keys, inside]
+        step *= radix
+        if number + 1 < count:
+            *near, own = call(
+                functools.partial(join_kernel, shifts),
+                (state, factor, packet),
+                [VMEM] * (3 + len(near) + len(ahead)),
+                (tail, total, total_factor, *near, *ahead),
+            )
     states = call(
-        states_kernel,
+        functools.partial(states_kernel, shifts),
         shape((slots, HALF, HEAD), jnp.bfloat16),
-        [VMEM] * 6,
-        (tail_b, parts, near, near_factor, *far),
+        [VMEM] * (4 + len(ahead)),
+        (tail, parts, *near, *ahead),
     )
     mine = lax.all_to_all(states, GROUP, split_axis=0, concat_axis=0, tiled=True)
     mine = mine.reshape(heads, HEAD, HEAD)
     return call(
-        output_kernel,
+        functools.partial(output_kernel, pieces),
         shape((rows, columns), jnp.bfloat16),
-        [VMEM] * 6,
-        (tail, mine, keys_a, inside_a, keys_b, inside_b),
+        [VMEM] * (2 + len(done)),
+        (tail, mine, *done),
         out_specs=REST,
         scratch=(pltpu.VMEM((rows, columns), jnp.bfloat16), dma((GROUPS,))),
     )

time: 81.9 us -> 81.5 us (level)
  transfers between devices with their start and end apart: 4 -> 4, of which waited for: 2 -> 3; matrix products, arithmetic and copies ran while one was open for 0% -> 0% of each run, Pallas kernels for 8% -> 8%
where the time goes in v4:
time: 81.5 us; the launch traced here: 80.5 us
  blocking collectives  52.2 us (64%)
  Pallas kernels  11.9 us (15%)
  waiting for transfers between devices  11 us (13%)
  starting transfers between devices  5.17 us (6%)
    all_to_all x1, blocking collectives, body(): lax.all_to_all(summaries, GROUP, split_axis=0, concat_axis=0, tiled=True)  28.4 us
    all_to_all x1, blocking collectives, body(): lax.all_to_all(states, GROUP, split_axis=0, concat_axis=0, tiled=True)  23.8 us
    pallas_call x7, Pallas kernels, call(): pl.pallas_call(kernel, out_shape=out_shape, in_specs=in_specs, out_specs=...  11.9 us
    ppermute x4, waiting for transfers between devices, from_ahead(): return lax.ppermute(x, 'zh', [(i + by, i) for i in range(size - by)])  11 us
    ppermute x4, starting transfers between devices, from_ahead(): return lax.ppermute(x, 'zh', [(i + by, i) for i in range(size - by)])  5.17 us
  transfers between devices with their start and end apart: 4, of which 3 were waited for; matrix products, arithmetic and copies ran while one was open for 0% of the time, Pallas kernels for 8%

profile of v4, /device:TPU:1, one launch (start us, length us, event | category | flops | bytes accessed | tf_op | source)
XLA Modules:
  0.0 80.5 jit_solution(2143444790935710050)
XLA Ops:
  0.0 3.0 %shard_map.55 = bf16[64,72,128]{2,1,0:T(8,128)(2,1)S(1)} custom-call(s32[1]{0:T(128)} %bitcast.base_ref, s32[8]{0:T(128)} %lengths_ref.3, bf16[128,4096]{1,0:T(8,128)(2,1)} %q_ref.3, bf16[128,4096]{1,0:T(8,128)(2,1)} %g_ref.3, bf16[32,128]{1,0:T(8,128)(2,1)} %bitcast.4), custom_call_target="tpu_custom_call" | custom-call | tf_op jit(solution)/shard_map/pallas_call | solution.py:252
  3.0 0.0 copy-start.1
  3.1 0.0 copy-start.2
  3.1 28.4 %all_to_all.10.parts_ref = bf16[64,72,128]{2,1,0:T(8,128)(2,1)S(1)} all-to-all(bf16[64,72,128]{2,1,0:T(8,128)(2,1)S(1)} %shard_map.55), channel_id=1, replica_groups=mesh['zh'=8,'zl'=2,'core'=2,'x'=4,'y'=4] {'zl','core','x','y'}, dimensions={0} | all-to-all | bytes 2359296 | tf_op jit(solution)/shard_map/all_to_all | solution.py:293
  31.5 0.0 copy-start
  31.5 0.0 copy-start.3
  31.5 0.0 copy-start.4
  31.5 0.4 shard_map.56
  31.9 1.3 %collective-permute-start = (bf16[72,128]{1,0:T(8,128)(2,1)S(1)}, bf16[72,128]{1,0:T(8,128)(2,1)S(1)}, u32[]{:S(2)}, u32[]{:S(2)}) collective-permute-start(bf16[72,128]{1,0:T(8,128)(2,1)S(1)} %get-tuple-element.17.after_ref), channel_id=1, source_target_pairs={{64,0},{128,64},{192,128},{256,192},{320,256},{384,320},{448,384},... | collective-permute-start | bytes 55304 | tf_op jit(solution)/shard_map/ppermute | solution.py:264
  33.2 0.0 copy-done.1
  33.2 0.0 copy-done.2
  33.2 0.0 copy-done
  33.2 0.0 copy-done.3
  33.2 0.0 copy-done.4
  33.2 3.2 %shard_map.57 = (f32[128,2048]{1,0:T(8,128)S(1)}, f32[128,32]{1,0:T(8,128)S(1)}, bf16[128,2048]{1,0:T(8,128)(2,1)S(1)}) custom-call(s32[1]{0:T(128)} %bitcast.base_ref, s32[8]{0:T(128)S(1)} %copy-done.4, bf16[128,4096]{1,0:T(8,128)(2,1)S(1)} %copy-done, bf16[128,4096]{1,0:T(8,128)(2,1)S(1)} %copy-done.2, bf16[128,4096]{1,0:T(8,128)(2,1)S(1)} %copy-done.1, ...), custom_call_target="tpu_custom_call" | custom-call | tf_op jit(solution)/shard_map/pallas_call | solution.py:252
  36.4 1.5 %collective-permute-done.refs_0_ = bf16[72,128]{1,0:T(8,128)(2,1)S(1)} collective-permute-done((bf16[72,128]{1,0:T(8,128)(2,1)S(1)}, bf16[72,128]{1,0:T(8,128)(2,1)S(1)}, u32[]{:S(2)}, u32[]{:S(2)}) %collective-permute-start) | collective-permute-done | bytes 18464 | tf_op jit(solution)/shard_map/ppermute | solution.py:264
  37.9 0.1 shard_map.58
  38.1 1.3 %collective-permute-start.3 = (bf16[72,128]{1,0:T(8,128)(2,1)S(1)}, bf16[72,128]{1,0:T(8,128)(2,1)S(1)}, u32[]{:S(2)}, u32[]{:S(2)}) collective-permute-start(bf16[72,128]{1,0:T(8,128)(2,1)S(1)} %get-tuple-element.21.after_ref), channel_id=1, source_target_pairs={{256,0},{320,64},{384,128},{448,192},{257,1},{321,65},{385,129},{4... | collective-permute-start | bytes 55304 | tf_op jit(solution)/shard_map/ppermute | solution.py:264
  39.4 1.3 %collective-permute-start.2 = (bf16[72,128]{1,0:T(8,128)(2,1)S(1)}, bf16[72,128]{1,0:T(8,128)(2,1)S(1)}, u32[]{:S(2)}, u32[]{:S(2)}) collective-permute-start(bf16[72,128]{1,0:T(8,128)(2,1)S(1)} %get-tuple-element.21.after_ref), channel_id=1, source_target_pairs={{384,0},{448,64},{385,1},{449,65},{386,2},{450,66},{387,3},{451,67... | collective-permute-start | bytes 55304 | tf_op jit(solution)/shard_map/ppermute | solution.py:264
  40.7 1.3 %collective-permute-start.1 = (bf16[72,128]{1,0:T(8,128)(2,1)S(1)}, bf16[72,128]{1,0:T(8,128)(2,1)S(1)}, u32[]{:S(2)}, u32[]{:S(2)}) collective-permute-start(bf16[72,128]{1,0:T(8,128)(2,1)S(1)} %get-tuple-element.21.after_ref), channel_id=1, source_target_pairs={{128,0},{192,64},{256,128},{320,192},{384,256},{448,320},{129,1},{... | collective-permute-start | bytes 55304 | tf_op jit(solution)/shard_map/ppermute | solution.py:264
  42.0 3.2 %shard_map.59 = (f32[128,2048]{1,0:T(8,128)S(1)}, f32[128,32]{1,0:T(8,128)S(1)}, bf16[128,2048]{1,0:T(8,128)(2,1)S(1)}) custom-call(s32[1]{0:T(128)} %bitcast.base_ref, s32[8]{0:T(128)S(1)} %copy-done.4, bf16[128,4096]{1,0:T(8,128)(2,1)S(1)} %copy-done, bf16[128,4096]{1,0:T(8,128)(2,1)S(1)} %copy-done.2, bf16[128,4096]{1,0:T(8,128)(2,1)S(1)} %copy-done.1, ...), custom_call_target="tpu_custom_call" | custom-call | tf_op jit(solution)/shard_map/pallas_call | solution.py:252
  45.1 7.4 %collective-permute-done.3.refs_2_ = bf16[72,128]{1,0:T(8,128)(2,1)S(1)} collective-permute-done((bf16[72,128]{1,0:T(8,128)(2,1)S(1)}, bf16[72,128]{1,0:T(8,128)(2,1)S(1)}, u32[]{:S(2)}, u32[]{:S(2)}) %collective-permute-start.3) | collective-permute-done | bytes 18464 | tf_op jit(solution)/shard_map/ppermute | solution.py:264
  52.5 2.2 %collective-permute-done.2.refs_1_ = bf16[72,128]{1,0:T(8,128)(2,1)S(1)} collective-permute-done((bf16[72,128]{1,0:T(8,128)(2,1)S(1)}, bf16[72,128]{1,0:T(8,128)(2,1)S(1)}, u32[]{:S(2)}, u32[]{:S(2)}) %collective-permute-start.2) | collective-permute-done | bytes 18464 | tf_op jit(solution)/shard_map/ppermute | solution.py:264
  54.7 0.0 collective-permute-done.1.refs_0_
  54.7 0.3 shard_map.60
  55.0 23.8 %all_to_all.11 = bf16[64,64,128]{2,1,0:T(8,128)(2,1)S(1)} all-to-all(bf16[64,64,128]{2,1,0:T(8,128)(2,1)S(1)} %shard_map.60), channel_id=1, replica_groups=mesh['zh'=8,'zl'=2,'core'=2,'x'=4,'y'=4] {'zl','core','x','y'}, dimensions={0} | all-to-all | bytes 2097152 | tf_op jit(solution)/shard_map/all_to_all | solution.py:338
  78.8 1.7 %shard_map.61 = bf16[128,4096]{1,0:T(8,128)(2,1)} custom-call(f32[128,32]{1,0:T(8,128)S(1)} %get-tuple-element.22.after_ref.tail_ref, bf16[32,128,128]{2,1,0:T(8,128)(2,1)S(1)} %bitcast.3, bf16[128,2048]{1,0:T(8,128)(2,1)S(1)} %get-tuple-element.25.refs_0_, f32[128,2048]{1,0:T(8,128)S(1)} %get-tuple-element.26.refs_1_, ...), custom_call_target="tpu_custom_call" | custom-call | tf_op jit(solution)/shard_map/pallas_call | solution.py:252
Async XLA Ops:
  3.0 30.1 %copy-start.1 = (bf16[128,4096]{1,0:T(8,128)(2,1)S(1)}, bf16[128,4096]{1,0:T(8,128)(2,1)}, u32[]{:S(2)}) copy-start(bf16[128,4096]{1,0:T(8,128)(2,1)} %g_ref.3) | copy-start | bytes 3145732
  3.1 30.1 %copy-start.2 = (bf16[128,4096]{1,0:T(8,128)(2,1)S(1)}, bf16[128,4096]{1,0:T(8,128)(2,1)}, u32[]{:S(2)}) copy-start(bf16[128,4096]{1,0:T(8,128)(2,1)} %k_ref.3) | copy-start | bytes 3145732
  31.5 1.7 %copy-start = (bf16[128,4096]{1,0:T(8,128)(2,1)S(1)}, bf16[128,4096]{1,0:T(8,128)(2,1)}, u32[]{:S(2)}) copy-start(bf16[128,4096]{1,0:T(8,128)(2,1)} %q_ref.3) | copy-start | bytes 3145732
  31.5 1.7 %copy-start.3 = (bf16[128,32]{0,1:T(8,128)(2,1)S(1)}, bf16[128,32]{0,1:T(8,128)(2,1)}, u32[]{:S(2)}) copy-start(bf16[128,32]{0,1:T(8,128)(2,1)} %param.8) | copy-start | bytes 24580
  31.5 1.7 %copy-start.4 = (s32[8]{0:T(128)S(1)}, s32[8]{0:T(128)}, u32[]{:S(2)}) copy-start(s32[8]{0:T(128)} %lengths_ref.3) | copy-start | bytes 100
  31.9 6.0 %collective-permute-start = (bf16[72,128]{1,0:T(8,128)(2,1)S(1)}, bf16[72,128]{1,0:T(8,128)(2,1)S(1)}, u32[]{:S(2)}, u32[]{:S(2)}) collective-permute-start(bf16[72,128]{1,0:T(8,128)(2,1)S(1)} %get-tuple-element.17.after_ref), channel_id=1, source_target_pairs={{64,0},{128,64},{192,128},{256,192},{320,256},{384,320},{448,384},... | collective-permute-start | bytes 55304 | tf_op jit(solution)/shard_map/ppermute | solution.py:264
  38.1 14.5 %collective-permute-start.3 = (bf16[72,128]{1,0:T(8,128)(2,1)S(1)}, bf16[72,128]{1,0:T(8,128)(2,1)S(1)}, u32[]{:S(2)}, u32[]{:S(2)}) collective-permute-start(bf16[72,128]{1,0:T(8,128)(2,1)S(1)} %get-tuple-element.21.after_ref), channel_id=1, source_target_pairs={{256,0},{320,64},{384,128},{448,192},{257,1},{321,65},{385,129},{4... | collective-permute-start | bytes 55304 | tf_op jit(solution)/shard_map/ppermute | solution.py:264
  39.4 15.3 %collective-permute-start.2 = (bf16[72,128]{1,0:T(8,128)(2,1)S(1)}, bf16[72,128]{1,0:T(8,128)(2,1)S(1)}, u32[]{:S(2)}, u32[]{:S(2)}) collective-permute-start(bf16[72,128]{1,0:T(8,128)(2,1)S(1)} %get-tuple-element.21.after_ref), channel_id=1, source_target_pairs={{384,0},{448,64},{385,1},{449,65},{386,2},{450,66},{387,3},{451,67... | collective-permute-start | bytes 55304 | tf_op jit(solution)/shard_map/ppermute | solution.py:264
  40.7 14.0 %collective-permute-start.1 = (bf16[72,128]{1,0:T(8,128)(2,1)S(1)}, bf16[72,128]{1,0:T(8,128)(2,1)S(1)}, u32[]{:S(2)}, u32[]{:S(2)}) collective-permute-start(bf16[72,128]{1,0:T(8,128)(2,1)S(1)} %get-tuple-element.21.after_ref), channel_id=1, source_target_pairs={{128,0},{192,64},{256,128},{320,192},{384,256},{448,320},{129,1},{... | collective-permute-start | bytes 55304 | tf_op jit(solution)/shard_map/ppermute | solution.py:264

commit v5 on v4

--- a/solution.py
+++ b/solution.py
@@ -9,8 +9,8 @@
 HEAD = 128
 PAD = 8
 HALF = 64
-RADICES = (2, 4)
-ORDERS = ((1,), (2, 6, 4))
+FIRST = (1, 4, 5)
+SECOND = (2, 6)
 ROW_PARTS = 1
 NEG = -1e30
 TINY = 1e-36
@@ -193,13 +193,8 @@
     return state, factor
 
 
-def join_kernel(shifts, after_ref, total_ref, factor_ref, *refs):
-    refs, outs = refs[:-3], refs[-3:]
-    near_ref, near_factor_ref, packet_ref = outs
-    state, factor = join(shifts, refs[-len(shifts) :])
-    if len(refs) > len(shifts):
-        state = refs[0][...] + refs[1][...] * state
-        factor = refs[1][...] * factor
+def join_kernel(total_ref, factor_ref, next_ref, near_ref, near_factor_ref, packet_ref):
+    state, factor = read_packet(next_ref)
     near_ref[...] = state
     near_factor_ref[...] = factor
     own = factor_ref[...]
@@ -296,7 +291,7 @@
     packet = shape((HALF + PAD, HEAD), jnp.bfloat16)
     total, total_factor, own = call(reduce_kernel, (state, factor, packet), [VMEM], (parts,))
 
-    count = len(RADICES)
+    count = 1
     edges = [heads * n // count for n in range(count + 1)]
     pieces = tuple((edges[n], edges[n + 1] - edges[n]) for n in range(count))
 
@@ -313,27 +308,19 @@
             (base, doc_lengths, query_vectors, key_vectors, out_grad, decay_rows, after),
         )
 
-    step = 1
-    near = ()
-    done = []
-    for number, radix in enumerate(RADICES):
-        shifts = ORDERS[number]
-        ahead = [from_ahead(own, by) for by in shifts]
-        inside, tail, keys = inside_part(number, own)
-        done += [keys, inside]
-        step *= radix
-        if number + 1 < count:
-            *near, own = call(
-                functools.partial(join_kernel, shifts),
-                (state, factor, packet),
-                [VMEM] * (3 + len(near) + len(ahead)),
-                (tail, total, total_factor, *near, *ahead),
-            )
+    ahead = {by: from_ahead(own, by) for by in FIRST}
+    near, near_factor, wide = call(
+        join_kernel, (state, factor, packet), [VMEM] * 3, (total, total_factor, ahead.pop(1))
+    )
+    ahead.update({by: from_ahead(wide, by) for by in SECOND})
+    inside, tail, keys = inside_part(0, wide)
+    done = [keys, inside]
+    shifts = tuple(sorted(ahead))
     states = call(
         functools.partial(states_kernel, shifts),
         shape((slots, HALF, HEAD), jnp.bfloat16),
-        [VMEM] * (4 + len(ahead)),
-        (tail, parts, *near, *ahead),
+        [VMEM] * (4 + len(shifts)),
+        (tail, parts, near, near_factor, *[ahead[by] for by in shifts]),
     )
     mine = lax.all_to_all(states, GROUP, split_axis=0, concat_axis=0, tiled=True)
     mine = mine.reshape(heads, HEAD, HEAD)

time: 81.5 us -> 77.2 us (0.947)
  waiting for transfers between devices: 11 us -> 7.65 us
  starting transfers between devices: 5.17 us -> 6.46 us
    ppermute x4 -> x5, waiting for transfers between devices: 11 us -> 7.65 us  [from_ahead(): return lax.ppermute(x, 'zh', [(i + by, i) for i in range(size - by)])]
    ppermute x4 -> x5, starting transfers between devices: 5.17 us -> 6.46 us  [from_ahead(): return lax.ppermute(x, 'zh', [(i + by, i) for i in range(size - by)])]
    all_to_all x1, blocking collectives: 23.8 us -> 22.9 us  [body(): lax.all_to_all(states, GROUP, split_axis=0, concat_axis=0, tiled=True)]
    pallas_call x7 -> x6, Pallas kernels: 11.9 us -> 11.3 us  [call(): pl.pallas_call(kernel, out_shape=out_shape, in_specs=in_specs, out_specs=...]
  transfers between devices with their start and end apart: 4 -> 5, of which waited for: 3 -> 4; matrix products, arithmetic and copies ran while one was open for 0% -> 0% of each run, Pallas kernels for 8% -> 8%
where the time goes in v5:
time: 77.2 us; the launch traced here: 76.9 us
  blocking collectives  51.4 us (67%)
  Pallas kernels  11.3 us (15%)
  waiting for transfers between devices  7.65 us (10%)
  starting transfers between devices  6.46 us (8%)
    all_to_all x1, blocking collectives, body(): lax.all_to_all(summaries, GROUP, split_axis=0, concat_axis=0, tiled=True)  28.4 us
    all_to_all x1, blocking collectives, body(): lax.all_to_all(states, GROUP, split_axis=0, concat_axis=0, tiled=True)  22.9 us
    pallas_call x6, Pallas kernels, call(): pl.pallas_call(kernel, out_shape=out_shape, in_specs=in_specs, out_specs=...  11.3 us
    ppermute x5, waiting for transfers between devices, from_ahead(): return lax.ppermute(x, 'zh', [(i + by, i) for i in range(size - by)])  7.65 us
    ppermute x5, starting transfers between devices, from_ahead(): return lax.ppermute(x, 'zh', [(i + by, i) for i in range(size - by)])  6.46 us
  transfers between devices with their start and end apart: 5, of which 4 were waited for; matrix products, arithmetic and copies ran while one was open for 0% of the time, Pallas kernels for 8%

profile of v5, /device:TPU:1, one launch (start us, length us, event | category | flops | bytes accessed | tf_op | source)
XLA Modules:
  0.0 76.9 jit_solution(9389288605917106878)
XLA Ops:
  0.0 3.0 %shard_map.55 = bf16[64,72,128]{2,1,0:T(8,128)(2,1)S(1)} custom-call(s32[1]{0:T(128)} %bitcast.base_ref, s32[8]{0:T(128)} %lengths_ref.1, bf16[128,4096]{1,0:T(8,128)(2,1)} %q_ref.1, bf16[128,4096]{1,0:T(8,128)(2,1)} %g_ref.1, bf16[32,128]{1,0:T(8,128)(2,1)} %bitcast.4), custom_call_target="tpu_custom_call" | custom-call | tf_op jit(solution)/shard_map/pallas_call | solution.py:247
  3.0 0.0 copy-start.1
  3.1 0.0 copy-start.2
  3.1 28.4 %all_to_all.10.parts_ref = bf16[64,72,128]{2,1,0:T(8,128)(2,1)S(1)} all-to-all(bf16[64,72,128]{2,1,0:T(8,128)(2,1)S(1)} %shard_map.55), channel_id=1, replica_groups=mesh['zh'=8,'zl'=2,'core'=2,'x'=4,'y'=4] {'zl','core','x','y'}, dimensions={0} | all-to-all | bytes 2359296 | tf_op jit(solution)/shard_map/all_to_all | solution.py:288
  31.5 0.0 copy-start
  31.5 0.0 copy-start.3
  31.5 0.0 copy-start.4
  31.5 0.4 shard_map.56
  31.9 1.3 %collective-permute-start = (bf16[72,128]{1,0:T(8,128)(2,1)S(1)}, bf16[72,128]{1,0:T(8,128)(2,1)S(1)}, u32[]{:S(2)}, u32[]{:S(2)}) collective-permute-start(bf16[72,128]{1,0:T(8,128)(2,1)S(1)} %get-tuple-element.16), channel_id=1, source_target_pairs={{64,0},{128,64},{192,128},{256,192},{320,256},{384,320},{448,384},... | collective-permute-start | bytes 55304 | tf_op jit(solution)/shard_map/ppermute | solution.py:259
  33.2 1.3 %collective-permute-start.3 = (bf16[72,128]{1,0:T(8,128)(2,1)S(1)}, bf16[72,128]{1,0:T(8,128)(2,1)S(1)}, u32[]{:S(2)}, u32[]{:S(2)}) collective-permute-start(bf16[72,128]{1,0:T(8,128)(2,1)S(1)} %get-tuple-element.16), channel_id=1, source_target_pairs={{320,0},{384,64},{448,128},{321,1},{385,65},{449,129},{322,2},{386... | collective-permute-start | bytes 55304 | tf_op jit(solution)/shard_map/ppermute | solution.py:259
  34.5 1.3 %collective-permute-start.2 = (bf16[72,128]{1,0:T(8,128)(2,1)S(1)}, bf16[72,128]{1,0:T(8,128)(2,1)S(1)}, u32[]{:S(2)}, u32[]{:S(2)}) collective-permute-start(bf16[72,128]{1,0:T(8,128)(2,1)S(1)} %get-tuple-element.16), channel_id=1, source_target_pairs={{256,0},{320,64},{384,128},{448,192},{257,1},{321,65},{385,129},{4... | collective-permute-start | bytes 55304 | tf_op jit(solution)/shard_map/ppermute | solution.py:259
  35.8 2.1 %collective-permute-done.next_ref = bf16[72,128]{1,0:T(8,128)(2,1)S(1)} collective-permute-done((bf16[72,128]{1,0:T(8,128)(2,1)S(1)}, bf16[72,128]{1,0:T(8,128)(2,1)S(1)}, u32[]{:S(2)}, u32[]{:S(2)}) %collective-permute-start) | collective-permute-done | bytes 18464 | tf_op jit(solution)/shard_map/ppermute | solution.py:259
  37.9 0.1 shard_map.57
  38.1 1.3 %collective-permute-start.4 = (bf16[72,128]{1,0:T(8,128)(2,1)S(1)}, bf16[72,128]{1,0:T(8,128)(2,1)S(1)}, u32[]{:S(2)}, u32[]{:S(2)}) collective-permute-start(bf16[72,128]{1,0:T(8,128)(2,1)S(1)} %get-tuple-element.17.after_ref), channel_id=1, source_target_pairs={{384,0},{448,64},{385,1},{449,65},{386,2},{450,66},{387,3},{451,67... | collective-permute-start | bytes 55304 | tf_op jit(solution)/shard_map/ppermute | solution.py:259
  39.4 1.3 %collective-permute-start.1 = (bf16[72,128]{1,0:T(8,128)(2,1)S(1)}, bf16[72,128]{1,0:T(8,128)(2,1)S(1)}, u32[]{:S(2)}, u32[]{:S(2)}) collective-permute-start(bf16[72,128]{1,0:T(8,128)(2,1)S(1)} %get-tuple-element.17.after_ref), channel_id=1, source_target_pairs={{128,0},{192,64},{256,128},{320,192},{384,256},{448,320},{129,1},{... | collective-permute-start | bytes 55304 | tf_op jit(solution)/shard_map/ppermute | solution.py:259
  40.7 0.0 copy-done.1
  40.7 0.0 copy-done.2
  40.7 0.0 copy-done
  40.7 0.0 copy-done.3
  40.7 0.0 copy-done.4
  40.7 5.7 %shard_map.58 = (f32[128,4096]{1,0:T(8,128)S(1)}, f32[128,32]{1,0:T(8,128)S(1)}, bf16[128,4096]{1,0:T(8,128)(2,1)S(1)}) custom-call(s32[1]{0:T(128)} %bitcast.base_ref, s32[8]{0:T(128)S(1)} %copy-done.4, bf16[128,4096]{1,0:T(8,128)(2,1)S(1)} %copy-done, bf16[128,4096]{1,0:T(8,128)(2,1)S(1)} %copy-done.2, bf16[128,4096]{1,0:T(8,128)(2,1)S(1)} %copy-done.1, ...), custom_call_target="tpu_custom_call" | custom-call | tf_op jit(solution)/shard_map/pallas_call | solution.py:247
  46.4 2.8 %collective-permute-done.3.refs_2_ = bf16[72,128]{1,0:T(8,128)(2,1)S(1)} collective-permute-done((bf16[72,128]{1,0:T(8,128)(2,1)S(1)}, bf16[72,128]{1,0:T(8,128)(2,1)S(1)}, u32[]{:S(2)}, u32[]{:S(2)}) %collective-permute-start.3) | collective-permute-done | bytes 18464 | tf_op jit(solution)/shard_map/ppermute | solution.py:259
  49.2 0.7 collective-permute-done.2.refs_1_
  49.8 2.1 %collective-permute-done.4.refs_3_ = bf16[72,128]{1,0:T(8,128)(2,1)S(1)} collective-permute-done((bf16[72,128]{1,0:T(8,128)(2,1)S(1)}, bf16[72,128]{1,0:T(8,128)(2,1)S(1)}, u32[]{:S(2)}, u32[]{:S(2)}) %collective-permute-start.4) | collective-permute-done | bytes 18464 | tf_op jit(solution)/shard_map/ppermute | solution.py:259
  51.9 0.0 collective-permute-done.1.refs_0_
  51.9 0.3 shard_map.59
  52.2 22.9 %all_to_all.11 = bf16[64,64,128]{2,1,0:T(8,128)(2,1)S(1)} all-to-all(bf16[64,64,128]{2,1,0:T(8,128)(2,1)S(1)} %shard_map.59), channel_id=1, replica_groups=mesh['zh'=8,'zl'=2,'core'=2,'x'=4,'y'=4] {'zl','core','x','y'}, dimensions={0} | all-to-all | bytes 2097152 | tf_op jit(solution)/shard_map/all_to_all | solution.py:325
  75.2 1.7 %shard_map.60 = bf16[128,4096]{1,0:T(8,128)(2,1)} custom-call(f32[128,32]{1,0:T(8,128)S(1)} %get-tuple-element.18.after_ref.tail_ref, bf16[32,128,128]{2,1,0:T(8,128)(2,1)S(1)} %bitcast.3, bf16[128,4096]{1,0:T(8,128)(2,1)S(1)} %get-tuple-element.21.refs_0_, f32[128,4096]{1,0:T(8,128)S(1)} %get-tuple-element.22.refs_1_), custom_call_target="tpu_custom_call" | custom-call | tf_op jit(solution)/shard_map/pallas_call | solution.py:247
Async XLA Ops:
  3.0 37.6 %copy-start.1 = (bf16[128,4096]{1,0:T(8,128)(2,1)S(1)}, bf16[128,4096]{1,0:T(8,128)(2,1)}, u32[]{:S(2)}) copy-start(bf16[128,4096]{1,0:T(8,128)(2,1)} %g_ref.1) | copy-start | bytes 3145732
  3.1 37.6 %copy-start.2 = (bf16[128,4096]{1,0:T(8,128)(2,1)S(1)}, bf16[128,4096]{1,0:T(8,128)(2,1)}, u32[]{:S(2)}) copy-start(bf16[128,4096]{1,0:T(8,128)(2,1)} %k_ref.1) | copy-start | bytes 3145732
  31.5 9.2 %copy-start = (bf16[128,4096]{1,0:T(8,128)(2,1)S(1)}, bf16[128,4096]{1,0:T(8,128)(2,1)}, u32[]{:S(2)}) copy-start(bf16[128,4096]{1,0:T(8,128)(2,1)} %q_ref.1) | copy-start | bytes 3145732
  31.5 9.2 %copy-start.3 = (bf16[128,32]{0,1:T(8,128)(2,1)S(1)}, bf16[128,32]{0,1:T(8,128)(2,1)}, u32[]{:S(2)}) copy-start(bf16[128,32]{0,1:T(8,128)(2,1)} %param.8) | copy-start | bytes 24580
  31.5 9.2 %copy-start.4 = (s32[8]{0:T(128)S(1)}, s32[8]{0:T(128)}, u32[]{:S(2)}) copy-start(s32[8]{0:T(128)} %lengths_ref.1) | copy-start | bytes 100
  31.9 6.0 %collective-permute-start = (bf16[72,128]{1,0:T(8,128)(2,1)S(1)}, bf16[72,128]{1,0:T(8,128)(2,1)S(1)}, u32[]{:S(2)}, u32[]{:S(2)}) collective-permute-start(bf16[72,128]{1,0:T(8,128)(2,1)S(1)} %get-tuple-element.16), channel_id=1, source_target_pairs={{64,0},{128,64},{192,128},{256,192},{320,256},{384,320},{448,384},... | collective-permute-start | bytes 55304 | tf_op jit(solution)/shard_map/ppermute | solution.py:259
  33.2 16.0 %collective-permute-start.3 = (bf16[72,128]{1,0:T(8,128)(2,1)S(1)}, bf16[72,128]{1,0:T(8,128)(2,1)S(1)}, u32[]{:S(2)}, u32[]{:S(2)}) collective-permute-start(bf16[72,128]{1,0:T(8,128)(2,1)S(1)} %get-tuple-element.16), channel_id=1, source_target_pairs={{320,0},{384,64},{448,128},{321,1},{385,65},{449,129},{322,2},{386... | collective-permute-start | bytes 55304 | tf_op jit(solution)/shard_map/ppermute | solution.py:259
  34.5 15.3 %collective-permute-start.2 = (bf16[72,128]{1,0:T(8,128)(2,1)S(1)}, bf16[72,128]{1,0:T(8,128)(2,1)S(1)}, u32[]{:S(2)}, u32[]{:S(2)}) collective-permute-start(bf16[72,128]{1,0:T(8,128)(2,1)S(1)} %get-tuple-element.16), channel_id=1, source_target_pairs={{256,0},{320,64},{384,128},{448,192},{257,1},{321,65},{385,129},{4... | collective-permute-start | bytes 55304 | tf_op jit(solution)/shard_map/ppermute | solution.py:259
  38.1 13.8 %collective-permute-start.4 = (bf16[72,128]{1,0:T(8,128)(2,1)S(1)}, bf16[72,128]{1,0:T(8,128)(2,1)S(1)}, u32[]{:S(2)}, u32[]{:S(2)}) collective-permute-start(bf16[72,128]{1,0:T(8,128)(2,1)S(1)} %get-tuple-element.17.after_ref), channel_id=1, source_target_pairs={{384,0},{448,64},{385,1},{449,65},{386,2},{450,66},{387,3},{451,67... | collective-permute-start | bytes 55304 | tf_op jit(solution)/shard_map/ppermute | solution.py:259
  39.4 12.5 %collective-permute-start.1 = (bf16[72,128]{1,0:T(8,128)(2,1)S(1)}, bf16[72,128]{1,0:T(8,128)(2,1)S(1)}, u32[]{:S(2)}, u32[]{:S(2)}) collective-permute-start(bf16[72,128]{1,0:T(8,128)(2,1)S(1)} %get-tuple-element.17.after_ref), channel_id=1, source_target_pairs={{128,0},{192,64},{256,128},{320,192},{384,256},{448,320},{129,1},{... | collective-permute-start | bytes 55304 | tf_op jit(solution)/shard_map/ppermute | solution.py:259

commit v6 on v5

--- a/solution.py
+++ b/solution.py
@@ -9,8 +9,8 @@
 HEAD = 128
 PAD = 8
 HALF = 64
-FIRST = (1, 4, 5)
-SECOND = (2, 6)
+FIRST = (1, 4, 5, 6, 7)
+SECOND = (2,)
 ROW_PARTS = 1
 NEG = -1e30
 TINY = 1e-36

time: 77.2 us -> 77 us (level)
  waiting for transfers between devices: 7.65 us -> 5.62 us
  starting transfers between devices: 6.46 us -> 7.75 us
    ppermute x5 -> x6, waiting for transfers between devices: 7.65 us -> 5.62 us  [from_ahead(): return lax.ppermute(x, 'zh', [(i + by, i) for i in range(size - by)])]
    ppermute x5 -> x6, starting transfers between devices: 6.46 us -> 7.75 us  [from_ahead(): return lax.ppermute(x, 'zh', [(i + by, i) for i in range(size - by)])]
  transfers between devices with their start and end apart: 5 -> 6, of which waited for: 4 -> 4; matrix products, arithmetic and copies ran while one was open for 0% -> 0% of each run, Pallas kernels for 8% -> 8%
where the time goes in v6:
time: 77 us; the launch traced here: 76.7 us
  blocking collectives  51.8 us (67%)
  Pallas kernels  11.3 us (15%)
  starting transfers between devices  7.75 us (10%)
  waiting for transfers between devices  5.62 us (7%)
    all_to_all x1, blocking collectives, body(): lax.all_to_all(summaries, GROUP, split_axis=0, concat_axis=0, tiled=True)  28.4 us
    all_to_all x1, blocking collectives, body(): lax.all_to_all(states, GROUP, split_axis=0, concat_axis=0, tiled=True)  23.4 us
    pallas_call x6, Pallas kernels, call(): pl.pallas_call(kernel, out_shape=out_shape, in_specs=in_specs, out_specs=...  11.3 us
    ppermute x6, starting transfers between devices, from_ahead(): return lax.ppermute(x, 'zh', [(i + by, i) for i in range(size - by)])  7.75 us
    ppermute x6, waiting for transfers between devices, from_ahead(): return lax.ppermute(x, 'zh', [(i + by, i) for i in range(size - by)])  5.62 us
  transfers between devices with their start and end apart: 6, of which 4 were waited for; matrix products, arithmetic and copies ran while one was open for 0% of the time, Pallas kernels for 8%

profile of v6, /device:TPU:1, one launch (start us, length us, event | category | flops | bytes accessed | tf_op | source)
XLA Modules:
  0.0 76.7 jit_solution(2514103704632192034)
XLA Ops:
  0.0 3.0 %shard_map.55 = bf16[64,72,128]{2,1,0:T(8,128)(2,1)S(1)} custom-call(s32[1]{0:T(128)} %bitcast.base_ref, s32[8]{0:T(128)} %lengths_ref.1, bf16[128,4096]{1,0:T(8,128)(2,1)} %q_ref.1, bf16[128,4096]{1,0:T(8,128)(2,1)} %g_ref.1, bf16[32,128]{1,0:T(8,128)(2,1)} %bitcast.4), custom_call_target="tpu_custom_call" | custom-call | tf_op jit(solution)/shard_map/pallas_call | solution.py:247
  3.0 0.0 copy-start.1
  3.1 0.0 copy-start.2
  3.1 28.4 %all_to_all.10.parts_ref = bf16[64,72,128]{2,1,0:T(8,128)(2,1)S(1)} all-to-all(bf16[64,72,128]{2,1,0:T(8,128)(2,1)S(1)} %shard_map.55), channel_id=1, replica_groups=mesh['zh'=8,'zl'=2,'core'=2,'x'=4,'y'=4] {'zl','core','x','y'}, dimensions={0} | all-to-all | bytes 2359296 | tf_op jit(solution)/shard_map/all_to_all | solution.py:288
  31.5 0.0 copy-start
  31.5 0.0 copy-start.3
  31.5 0.0 copy-start.4
  31.5 0.4 shard_map.56
  31.9 1.3 %collective-permute-start = (bf16[72,128]{1,0:T(8,128)(2,1)S(1)}, bf16[72,128]{1,0:T(8,128)(2,1)S(1)}, u32[]{:S(2)}, u32[]{:S(2)}) collective-permute-start(bf16[72,128]{1,0:T(8,128)(2,1)S(1)} %get-tuple-element.16), channel_id=1, source_target_pairs={{64,0},{128,64},{192,128},{256,192},{320,256},{384,320},{448,384},... | collective-permute-start | bytes 55304 | tf_op jit(solution)/shard_map/ppermute | solution.py:259
  33.2 1.3 %collective-permute-start.5 = (bf16[72,128]{1,0:T(8,128)(2,1)S(1)}, bf16[72,128]{1,0:T(8,128)(2,1)S(1)}, u32[]{:S(2)}, u32[]{:S(2)}) collective-permute-start(bf16[72,128]{1,0:T(8,128)(2,1)S(1)} %get-tuple-element.16), channel_id=1, source_target_pairs={{448,0},{449,1},{450,2},{451,3},{452,4},{453,5},{454,6},{455,7},{4... | collective-permute-start | bytes 55304 | tf_op jit(solution)/shard_map/ppermute | solution.py:259
  34.5 1.3 %collective-permute-start.4 = (bf16[72,128]{1,0:T(8,128)(2,1)S(1)}, bf16[72,128]{1,0:T(8,128)(2,1)S(1)}, u32[]{:S(2)}, u32[]{:S(2)}) collective-permute-start(bf16[72,128]{1,0:T(8,128)(2,1)S(1)} %get-tuple-element.16), channel_id=1, source_target_pairs={{384,0},{448,64},{385,1},{449,65},{386,2},{450,66},{387,3},{451,67... | collective-permute-start | bytes 55304 | tf_op jit(solution)/shard_map/ppermute | solution.py:259
  35.8 1.3 %collective-permute-start.3 = (bf16[72,128]{1,0:T(8,128)(2,1)S(1)}, bf16[72,128]{1,0:T(8,128)(2,1)S(1)}, u32[]{:S(2)}, u32[]{:S(2)}) collective-permute-start(bf16[72,128]{1,0:T(8,128)(2,1)S(1)} %get-tuple-element.16), channel_id=1, source_target_pairs={{320,0},{384,64},{448,128},{321,1},{385,65},{449,129},{322,2},{386... | collective-permute-start | bytes 55304 | tf_op jit(solution)/shard_map/ppermute | solution.py:259
  37.1 1.3 %collective-permute-start.2 = (bf16[72,128]{1,0:T(8,128)(2,1)S(1)}, bf16[72,128]{1,0:T(8,128)(2,1)S(1)}, u32[]{:S(2)}, u32[]{:S(2)}) collective-permute-start(bf16[72,128]{1,0:T(8,128)(2,1)S(1)} %get-tuple-element.16), channel_id=1, source_target_pairs={{256,0},{320,64},{384,128},{448,192},{257,1},{321,65},{385,129},{4... | collective-permute-start | bytes 55304 | tf_op jit(solution)/shard_map/ppermute | solution.py:259
  38.4 0.0 collective-permute-done.next_ref
  38.4 0.1 shard_map.57
  38.5 1.3 %collective-permute-start.1 = (bf16[72,128]{1,0:T(8,128)(2,1)S(1)}, bf16[72,128]{1,0:T(8,128)(2,1)S(1)}, u32[]{:S(2)}, u32[]{:S(2)}) collective-permute-start(bf16[72,128]{1,0:T(8,128)(2,1)S(1)} %get-tuple-element.17.after_ref), channel_id=1, source_target_pairs={{128,0},{192,64},{256,128},{320,192},{384,256},{448,320},{129,1},{... | collective-permute-start | bytes 55304 | tf_op jit(solution)/shard_map/ppermute | solution.py:259
  39.8 0.0 copy-done.1
  39.8 0.0 copy-done.2
  39.9 0.0 copy-done
  39.9 0.0 copy-done.3
  39.9 0.0 copy-done.4
  39.9 5.7 %shard_map.58 = (f32[128,4096]{1,0:T(8,128)S(1)}, f32[128,32]{1,0:T(8,128)S(1)}, bf16[128,4096]{1,0:T(8,128)(2,1)S(1)}) custom-call(s32[1]{0:T(128)} %bitcast.base_ref, s32[8]{0:T(128)S(1)} %copy-done.4, bf16[128,4096]{1,0:T(8,128)(2,1)S(1)} %copy-done, bf16[128,4096]{1,0:T(8,128)(2,1)S(1)} %copy-done.2, bf16[128,4096]{1,0:T(8,128)(2,1)S(1)} %copy-done.1, ...), custom_call_target="tpu_custom_call" | custom-call | tf_op jit(solution)/shard_map/pallas_call | solution.py:247
  45.6 0.6 collective-permute-done.5.refs_4_
  46.1 2.8 %collective-permute-done.4.refs_3_ = bf16[72,128]{1,0:T(8,128)(2,1)S(1)} collective-permute-done((bf16[72,128]{1,0:T(8,128)(2,1)S(1)}, bf16[72,128]{1,0:T(8,128)(2,1)S(1)}, u32[]{:S(2)}, u32[]{:S(2)}) %collective-permute-start.4) | collective-permute-done | bytes 18464 | tf_op jit(solution)/shard_map/ppermute | solution.py:259
  48.9 1.6 %collective-permute-done.3.refs_2_ = bf16[72,128]{1,0:T(8,128)(2,1)S(1)} collective-permute-done((bf16[72,128]{1,0:T(8,128)(2,1)S(1)}, bf16[72,128]{1,0:T(8,128)(2,1)S(1)}, u32[]{:S(2)}, u32[]{:S(2)}) %collective-permute-start.3) | collective-permute-done | bytes 18464 | tf_op jit(solution)/shard_map/ppermute | solution.py:259
  50.5 0.7 collective-permute-done.2.refs_1_
  51.2 0.0 collective-permute-done.1.refs_0_
  51.2 0.4 shard_map.59
  51.5 23.4 %all_to_all.11 = bf16[64,64,128]{2,1,0:T(8,128)(2,1)S(1)} all-to-all(bf16[64,64,128]{2,1,0:T(8,128)(2,1)S(1)} %shard_map.59), channel_id=1, replica_groups=mesh['zh'=8,'zl'=2,'core'=2,'x'=4,'y'=4] {'zl','core','x','y'}, dimensions={0} | all-to-all | bytes 2097152 | tf_op jit(solution)/shard_map/all_to_all | solution.py:325
  74.9 1.7 %shard_map.60 = bf16[128,4096]{1,0:T(8,128)(2,1)} custom-call(f32[128,32]{1,0:T(8,128)S(1)} %get-tuple-element.18.after_ref.tail_ref, bf16[32,128,128]{2,1,0:T(8,128)(2,1)S(1)} %bitcast.3, bf16[128,4096]{1,0:T(8,128)(2,1)S(1)} %get-tuple-element.21.refs_0_, f32[128,4096]{1,0:T(8,128)S(1)} %get-tuple-element.22.refs_1_), custom_call_target="tpu_custom_call" | custom-call | tf_op jit(solution)/shard_map/pallas_call | solution.py:247
Async XLA Ops:
  3.0 36.8 %copy-start.1 = (bf16[128,4096]{1,0:T(8,128)(2,1)S(1)}, bf16[128,4096]{1,0:T(8,128)(2,1)}, u32[]{:S(2)}) copy-start(bf16[128,4096]{1,0:T(8,128)(2,1)} %g_ref.1) | copy-start | bytes 3145732
  3.1 36.8 %copy-start.2 = (bf16[128,4096]{1,0:T(8,128)(2,1)S(1)}, bf16[128,4096]{1,0:T(8,128)(2,1)}, u32[]{:S(2)}) copy-start(bf16[128,4096]{1,0:T(8,128)(2,1)} %k_ref.1) | copy-start | bytes 3145732
  31.5 8.3 %copy-start = (bf16[128,4096]{1,0:T(8,128)(2,1)S(1)}, bf16[128,4096]{1,0:T(8,128)(2,1)}, u32[]{:S(2)}) copy-start(bf16[128,4096]{1,0:T(8,128)(2,1)} %q_ref.1) | copy-start | bytes 3145732
  31.5 8.4 %copy-start.3 = (bf16[128,32]{0,1:T(8,128)(2,1)S(1)}, bf16[128,32]{0,1:T(8,128)(2,1)}, u32[]{:S(2)}) copy-start(bf16[128,32]{0,1:T(8,128)(2,1)} %param.8) | copy-start | bytes 24580
  31.5 8.4 %copy-start.4 = (s32[8]{0:T(128)S(1)}, s32[8]{0:T(128)}, u32[]{:S(2)}) copy-start(s32[8]{0:T(128)} %lengths_ref.1) | copy-start | bytes 100
  31.9 6.5 %collective-permute-start = (bf16[72,128]{1,0:T(8,128)(2,1)S(1)}, bf16[72,128]{1,0:T(8,128)(2,1)S(1)}, u32[]{:S(2)}, u32[]{:S(2)}) collective-permute-start(bf16[72,128]{1,0:T(8,128)(2,1)S(1)} %get-tuple-element.16), channel_id=1, source_target_pairs={{64,0},{128,64},{192,128},{256,192},{320,256},{384,320},{448,384},... | collective-permute-start | bytes 55304 | tf_op jit(solution)/shard_map/ppermute | solution.py:259
  33.2 13.0 %collective-permute-start.5 = (bf16[72,128]{1,0:T(8,128)(2,1)S(1)}, bf16[72,128]{1,0:T(8,128)(2,1)S(1)}, u32[]{:S(2)}, u32[]{:S(2)}) collective-permute-start(bf16[72,128]{1,0:T(8,128)(2,1)S(1)} %get-tuple-element.16), channel_id=1, source_target_pairs={{448,0},{449,1},{450,2},{451,3},{452,4},{453,5},{454,6},{455,7},{4... | collective-permute-start | bytes 55304 | tf_op jit(solution)/shard_map/ppermute | solution.py:259
  34.5 14.4 %collective-permute-start.4 = (bf16[72,128]{1,0:T(8,128)(2,1)S(1)}, bf16[72,128]{1,0:T(8,128)(2,1)S(1)}, u32[]{:S(2)}, u32[]{:S(2)}) collective-permute-start(bf16[72,128]{1,0:T(8,128)(2,1)S(1)} %get-tuple-element.16), channel_id=1, source_target_pairs={{384,0},{448,64},{385,1},{449,65},{386,2},{450,66},{387,3},{451,67... | collective-permute-start | bytes 55304 | tf_op jit(solution)/shard_map/ppermute | solution.py:259
  35.8 14.7 %collective-permute-start.3 = (bf16[72,128]{1,0:T(8,128)(2,1)S(1)}, bf16[72,128]{1,0:T(8,128)(2,1)S(1)}, u32[]{:S(2)}, u32[]{:S(2)}) collective-permute-start(bf16[72,128]{1,0:T(8,128)(2,1)S(1)} %get-tuple-element.16), channel_id=1, source_target_pairs={{320,0},{384,64},{448,128},{321,1},{385,65},{449,129},{322,2},{386... | collective-permute-start | bytes 55304 | tf_op jit(solution)/shard_map/ppermute | solution.py:259
  37.1 14.1 %collective-permute-start.2 = (bf16[72,128]{1,0:T(8,128)(2,1)S(1)}, bf16[72,128]{1,0:T(8,128)(2,1)S(1)}, u32[]{:S(2)}, u32[]{:S(2)}) collective-permute-start(bf16[72,128]{1,0:T(8,128)(2,1)S(1)} %get-tuple-element.16), channel_id=1, source_target_pairs={{256,0},{320,64},{384,128},{448,192},{257,1},{321,65},{385,129},{4... | collective-permute-start | bytes 55304 | tf_op jit(solution)/shard_map/ppermute | solution.py:259
  38.5 12.6 %collective-permute-start.1 = (bf16[72,128]{1,0:T(8,128)(2,1)S(1)}, bf16[72,128]{1,0:T(8,128)(2,1)S(1)}, u32[]{:S(2)}, u32[]{:S(2)}) collective-permute-start(bf16[72,128]{1,0:T(8,128)(2,1)S(1)} %get-tuple-element.17.after_ref), channel_id=1, source_target_pairs={{128,0},{192,64},{256,128},{320,192},{384,256},{448,320},{129,1},{... | collective-permute-start | bytes 55304 | tf_op jit(solution)/shard_map/ppermute | solution.py:259

commit v7 on v6

--- a/solution.py
+++ b/solution.py
@@ -17,6 +17,7 @@
 OCTAVES = 120.0
 GROUPS = 2
 GROUP = ("zl", "core", "x", "y")
+PEERS = ("x", "y", "zl", "core")
 
 
 def token_segments(lengths_ref, positions):
@@ -149,6 +150,11 @@
         inside_ref[:, here] = jnp.dot(weights, g_ref[:, cols], preferred_element_type=jnp.float32)
 
 
+def peer_order(count):
+    planes = 4
+    return [(p % (count // planes)) * planes + p // (count // planes) for p in range(count)]
+
+
 def factor_row(ref, p):
     tail = ref[p, HALF : HALF + PAD, :].astype(jnp.float32)
     return tail[0:1, :] + tail[1:2, :] + tail[2:3, :]
@@ -174,7 +180,7 @@
 def reduce_kernel(parts_ref, total_ref, factor_ref, packet_ref):
     state = jnp.zeros((HALF, HEAD), jnp.float32)
     factor = jnp.ones((1, HEAD), jnp.float32)
-    for p in reversed(range(parts_ref.shape[0])):
+    for p in reversed(peer_order(parts_ref.shape[0])):
         f = factor_row(parts_ref, p)
         state = parts_ref[p, 0:HALF, :].astype(jnp.float32) + f * state
         factor = factor * f
@@ -205,7 +211,7 @@
     out_ref = refs[-1]
     far, far_factor = join(shifts, refs[:-1])
     state = near_ref[...] + near_factor_ref[...] * far
-    for p in reversed(range(parts_ref.shape[0])):
+    for p in reversed(peer_order(parts_ref.shape[0])):
         out_ref[p] = state.astype(jnp.bfloat16)
         state = parts_ref[p, 0:HALF, :].astype(jnp.float32) + factor_row(parts_ref, p) * state
 
@@ -285,7 +291,7 @@
             dma((2,)),
         ),
     )
-    parts = lax.all_to_all(summaries, GROUP, split_axis=0, concat_axis=0, tiled=True)
+    parts = lax.all_to_all(summaries, PEERS, split_axis=0, concat_axis=0, tiled=True)
     state = shape((HALF, HEAD), jnp.float32)
     factor = shape((1, HEAD), jnp.float32)
     packet = shape((HALF + PAD, HEAD), jnp.bfloat16)
@@ -322,7 +328,7 @@
         [VMEM] * (4 + len(shifts)),
         (tail, parts, near, near_factor, *[ahead[by] for by in shifts]),
     )
-    mine = lax.all_to_all(states, GROUP, split_axis=0, concat_axis=0, tiled=True)
+    mine = lax.all_to_all(states, PEERS, split_axis=0, concat_axis=0, tiled=True)
     mine = mine.reshape(heads, HEAD, HEAD)
     return call(
         functools.partial(output_kernel, pieces),

time: 77 us -> 78.7 us (1.022)
  blocking collectives: 51.8 us -> 53.7 us
    all_to_all x2, blocking collectives: 51.8 us -> 53.7 us  [the longest x1 30.1 us: body(): lax.all_to_all(summaries, PEERS, split_axis=0, concat_axis=0, tiled=True)]
  transfers between devices with their start and end apart: 6 -> 6, of which waited for: 4 -> 4; matrix products, arithmetic and copies ran while one was open for 0% -> 0% of each run, Pallas kernels for 8% -> 7%
where the time goes in v7:
time: 78.7 us; the launch traced here: 78.4 us
  blocking collectives  53.7 us (68%)
  Pallas kernels  11.3 us (14%)
  starting transfers between devices  7.75 us (10%)
  waiting for transfers between devices  5.49 us (7%)
    all_to_all x1, blocking collectives, body(): lax.all_to_all(summaries, PEERS, split_axis=0, concat_axis=0, tiled=True)  30.1 us
    all_to_all x1, blocking collectives, body(): lax.all_to_all(states, PEERS, split_axis=0, concat_axis=0, tiled=True)  23.6 us
    pallas_call x6, Pallas kernels, call(): pl.pallas_call(kernel, out_shape=out_shape, in_specs=in_specs, out_specs=...  11.3 us
    ppermute x6, starting transfers between devices, from_ahead(): return lax.ppermute(x, 'zh', [(i + by, i) for i in range(size - by)])  7.75 us
    ppermute x6, waiting for transfers between devices, from_ahead(): return lax.ppermute(x, 'zh', [(i + by, i) for i in range(size - by)])  5.49 us
  transfers between devices with their start and end apart: 6, of which 4 were waited for; matrix products, arithmetic and copies ran while one was open for 0% of the time, Pallas kernels for 7%

profile of v7, /device:TPU:1, one launch (start us, length us, event | category | flops | bytes accessed | tf_op | source)
XLA Modules:
  0.0 78.4 jit_solution(8865422110382390572)
XLA Ops:
  0.0 3.0 %shard_map.55 = bf16[64,72,128]{2,1,0:T(8,128)(2,1)S(1)} custom-call(s32[1]{0:T(128)} %bitcast.base_ref, s32[8]{0:T(128)} %lengths_ref.1, bf16[128,4096]{1,0:T(8,128)(2,1)} %q_ref.1, bf16[128,4096]{1,0:T(8,128)(2,1)} %g_ref.1, bf16[32,128]{1,0:T(8,128)(2,1)} %bitcast.4), custom_call_target="tpu_custom_call" | custom-call | tf_op jit(solution)/shard_map/pallas_call | solution.py:253
  3.0 0.0 copy-start.1
  3.1 0.0 copy-start.2
  3.1 30.1 %all_to_all.10.parts_ref = bf16[64,72,128]{2,1,0:T(8,128)(2,1)S(1)} all-to-all(bf16[64,72,128]{2,1,0:T(8,128)(2,1)S(1)} %shard_map.55), channel_id=1, replica_groups=mesh['zh'=8,'zl'=2,'core'=2,'x'=4,'y'=4] {'x','y','zl','core'}, dimensions={0} | all-to-all | bytes 2359296 | tf_op jit(solution)/shard_map/all_to_all | solution.py:294
  33.2 0.0 copy-start
  33.2 0.0 copy-start.3
  33.2 0.0 copy-start.4
  33.2 0.4 shard_map.56
  33.5 1.3 %collective-permute-start = (bf16[72,128]{1,0:T(8,128)(2,1)S(1)}, bf16[72,128]{1,0:T(8,128)(2,1)S(1)}, u32[]{:S(2)}, u32[]{:S(2)}) collective-permute-start(bf16[72,128]{1,0:T(8,128)(2,1)S(1)} %get-tuple-element.16), channel_id=1, source_target_pairs={{64,0},{128,64},{192,128},{256,192},{320,256},{384,320},{448,384},... | collective-permute-start | bytes 55304 | tf_op jit(solution)/shard_map/ppermute | solution.py:265
  34.8 1.3 %collective-permute-start.5 = (bf16[72,128]{1,0:T(8,128)(2,1)S(1)}, bf16[72,128]{1,0:T(8,128)(2,1)S(1)}, u32[]{:S(2)}, u32[]{:S(2)}) collective-permute-start(bf16[72,128]{1,0:T(8,128)(2,1)S(1)} %get-tuple-element.16), channel_id=1, source_target_pairs={{448,0},{449,1},{450,2},{451,3},{452,4},{453,5},{454,6},{455,7},{4... | collective-permute-start | bytes 55304 | tf_op jit(solution)/shard_map/ppermute | solution.py:265
  36.1 1.3 %collective-permute-start.4 = (bf16[72,128]{1,0:T(8,128)(2,1)S(1)}, bf16[72,128]{1,0:T(8,128)(2,1)S(1)}, u32[]{:S(2)}, u32[]{:S(2)}) collective-permute-start(bf16[72,128]{1,0:T(8,128)(2,1)S(1)} %get-tuple-element.16), channel_id=1, source_target_pairs={{384,0},{448,64},{385,1},{449,65},{386,2},{450,66},{387,3},{451,67... | collective-permute-start | bytes 55304 | tf_op jit(solution)/shard_map/ppermute | solution.py:265
  37.4 1.3 %collective-permute-start.3 = (bf16[72,128]{1,0:T(8,128)(2,1)S(1)}, bf16[72,128]{1,0:T(8,128)(2,1)S(1)}, u32[]{:S(2)}, u32[]{:S(2)}) collective-permute-start(bf16[72,128]{1,0:T(8,128)(2,1)S(1)} %get-tuple-element.16), channel_id=1, source_target_pairs={{320,0},{384,64},{448,128},{321,1},{385,65},{449,129},{322,2},{386... | collective-permute-start | bytes 55304 | tf_op jit(solution)/shard_map/ppermute | solution.py:265
  38.7 1.3 %collective-permute-start.2 = (bf16[72,128]{1,0:T(8,128)(2,1)S(1)}, bf16[72,128]{1,0:T(8,128)(2,1)S(1)}, u32[]{:S(2)}, u32[]{:S(2)}) collective-permute-start(bf16[72,128]{1,0:T(8,128)(2,1)S(1)} %get-tuple-element.16), channel_id=1, source_target_pairs={{256,0},{320,64},{384,128},{448,192},{257,1},{321,65},{385,129},{4... | collective-permute-start | bytes 55304 | tf_op jit(solution)/shard_map/ppermute | solution.py:265
  40.0 0.0 collective-permute-done.next_ref
  40.1 0.1 shard_map.57
  40.2 1.3 %collective-permute-start.1 = (bf16[72,128]{1,0:T(8,128)(2,1)S(1)}, bf16[72,128]{1,0:T(8,128)(2,1)S(1)}, u32[]{:S(2)}, u32[]{:S(2)}) collective-permute-start(bf16[72,128]{1,0:T(8,128)(2,1)S(1)} %get-tuple-element.17.after_ref), channel_id=1, source_target_pairs={{128,0},{192,64},{256,128},{320,192},{384,256},{448,320},{129,1},{... | collective-permute-start | bytes 55304 | tf_op jit(solution)/shard_map/ppermute | solution.py:265
  41.5 0.0 copy-done.1
  41.5 0.0 copy-done.2
  41.5 0.0 copy-done
  41.5 0.0 copy-done.3
  41.5 0.0 copy-done.4
  41.5 5.7 %shard_map.58 = (f32[128,4096]{1,0:T(8,128)S(1)}, f32[128,32]{1,0:T(8,128)S(1)}, bf16[128,4096]{1,0:T(8,128)(2,1)S(1)}) custom-call(s32[1]{0:T(128)} %bitcast.base_ref, s32[8]{0:T(128)S(1)} %copy-done.4, bf16[128,4096]{1,0:T(8,128)(2,1)S(1)} %copy-done, bf16[128,4096]{1,0:T(8,128)(2,1)S(1)} %copy-done.2, bf16[128,4096]{1,0:T(8,128)(2,1)S(1)} %copy-done.1, ...), custom_call_target="tpu_custom_call" | custom-call | tf_op jit(solution)/shard_map/pallas_call | solution.py:253
  47.2 0.5 collective-permute-done.5.refs_4_
  47.8 2.8 %collective-permute-done.4.refs_3_ = bf16[72,128]{1,0:T(8,128)(2,1)S(1)} collective-permute-done((bf16[72,128]{1,0:T(8,128)(2,1)S(1)}, bf16[72,128]{1,0:T(8,128)(2,1)S(1)}, u32[]{:S(2)}, u32[]{:S(2)}) %collective-permute-start.4) | collective-permute-done | bytes 18464 | tf_op jit(solution)/shard_map/ppermute | solution.py:265
  50.5 1.7 %collective-permute-done.3.refs_2_ = bf16[72,128]{1,0:T(8,128)(2,1)S(1)} collective-permute-done((bf16[72,128]{1,0:T(8,128)(2,1)S(1)}, bf16[72,128]{1,0:T(8,128)(2,1)S(1)}, u32[]{:S(2)}, u32[]{:S(2)}) %collective-permute-start.3) | collective-permute-done | bytes 18464 | tf_op jit(solution)/shard_map/ppermute | solution.py:265
  52.2 0.5 collective-permute-done.2.refs_1_
  52.7 0.0 collective-permute-done.1.refs_0_
  52.7 0.4 shard_map.59
  53.1 23.6 %all_to_all.11 = bf16[64,64,128]{2,1,0:T(8,128)(2,1)S(1)} all-to-all(bf16[64,64,128]{2,1,0:T(8,128)(2,1)S(1)} %shard_map.59), channel_id=1, replica_groups=mesh['zh'=8,'zl'=2,'core'=2,'x'=4,'y'=4] {'x','y','zl','core'}, dimensions={0} | all-to-all | bytes 2097152 | tf_op jit(solution)/shard_map/all_to_all | solution.py:331
  76.6 1.7 %shard_map.60 = bf16[128,4096]{1,0:T(8,128)(2,1)} custom-call(f32[128,32]{1,0:T(8,128)S(1)} %get-tuple-element.18.after_ref.tail_ref, bf16[32,128,128]{2,1,0:T(8,128)(2,1)S(1)} %bitcast.3, bf16[128,4096]{1,0:T(8,128)(2,1)S(1)} %get-tuple-element.21.refs_0_, f32[128,4096]{1,0:T(8,128)S(1)} %get-tuple-element.22.refs_1_), custom_call_target="tpu_custom_call" | custom-call | tf_op jit(solution)/shard_map/pallas_call | solution.py:253
Async XLA Ops:
  3.0 38.4 %copy-start.1 = (bf16[128,4096]{1,0:T(8,128)(2,1)S(1)}, bf16[128,4096]{1,0:T(8,128)(2,1)}, u32[]{:S(2)}) copy-start(bf16[128,4096]{1,0:T(8,128)(2,1)} %g_ref.1) | copy-start | bytes 3145732
  3.1 38.4 %copy-start.2 = (bf16[128,4096]{1,0:T(8,128)(2,1)S(1)}, bf16[128,4096]{1,0:T(8,128)(2,1)}, u32[]{:S(2)}) copy-start(bf16[128,4096]{1,0:T(8,128)(2,1)} %k_ref.1) | copy-start | bytes 3145732
  33.2 8.3 %copy-start = (bf16[128,4096]{1,0:T(8,128)(2,1)S(1)}, bf16[128,4096]{1,0:T(8,128)(2,1)}, u32[]{:S(2)}) copy-start(bf16[128,4096]{1,0:T(8,128)(2,1)} %q_ref.1) | copy-start | bytes 3145732
  33.2 8.4 %copy-start.3 = (bf16[128,32]{0,1:T(8,128)(2,1)S(1)}, bf16[128,32]{0,1:T(8,128)(2,1)}, u32[]{:S(2)}) copy-start(bf16[128,32]{0,1:T(8,128)(2,1)} %param.8) | copy-start | bytes 24580
  33.2 8.4 %copy-start.4 = (s32[8]{0:T(128)S(1)}, s32[8]{0:T(128)}, u32[]{:S(2)}) copy-start(s32[8]{0:T(128)} %lengths_ref.1) | copy-start | bytes 100
  33.5 6.5 %collective-permute-start = (bf16[72,128]{1,0:T(8,128)(2,1)S(1)}, bf16[72,128]{1,0:T(8,128)(2,1)S(1)}, u32[]{:S(2)}, u32[]{:S(2)}) collective-permute-start(bf16[72,128]{1,0:T(8,128)(2,1)S(1)} %get-tuple-element.16), channel_id=1, source_target_pairs={{64,0},{128,64},{192,128},{256,192},{320,256},{384,320},{448,384},... | collective-permute-start | bytes 55304 | tf_op jit(solution)/shard_map/ppermute | solution.py:265
  34.8 12.9 %collective-permute-start.5 = (bf16[72,128]{1,0:T(8,128)(2,1)S(1)}, bf16[72,128]{1,0:T(8,128)(2,1)S(1)}, u32[]{:S(2)}, u32[]{:S(2)}) collective-permute-start(bf16[72,128]{1,0:T(8,128)(2,1)S(1)} %get-tuple-element.16), channel_id=1, source_target_pairs={{448,0},{449,1},{450,2},{451,3},{452,4},{453,5},{454,6},{455,7},{4... | collective-permute-start | bytes 55304 | tf_op jit(solution)/shard_map/ppermute | solution.py:265
  36.1 14.4 %collective-permute-start.4 = (bf16[72,128]{1,0:T(8,128)(2,1)S(1)}, bf16[72,128]{1,0:T(8,128)(2,1)S(1)}, u32[]{:S(2)}, u32[]{:S(2)}) collective-permute-start(bf16[72,128]{1,0:T(8,128)(2,1)S(1)} %get-tuple-element.16), channel_id=1, source_target_pairs={{384,0},{448,64},{385,1},{449,65},{386,2},{450,66},{387,3},{451,67... | collective-permute-start | bytes 55304 | tf_op jit(solution)/shard_map/ppermute | solution.py:265
  37.4 14.8 %collective-permute-start.3 = (bf16[72,128]{1,0:T(8,128)(2,1)S(1)}, bf16[72,128]{1,0:T(8,128)(2,1)S(1)}, u32[]{:S(2)}, u32[]{:S(2)}) collective-permute-start(bf16[72,128]{1,0:T(8,128)(2,1)S(1)} %get-tuple-element.16), channel_id=1, source_target_pairs={{320,0},{384,64},{448,128},{321,1},{385,65},{449,129},{322,2},{386... | collective-permute-start | bytes 55304 | tf_op jit(solution)/shard_map/ppermute | solution.py:265
  38.7 14.0 %collective-permute-start.2 = (bf16[72,128]{1,0:T(8,128)(2,1)S(1)}, bf16[72,128]{1,0:T(8,128)(2,1)S(1)}, u32[]{:S(2)}, u32[]{:S(2)}) collective-permute-start(bf16[72,128]{1,0:T(8,128)(2,1)S(1)} %get-tuple-element.16), channel_id=1, source_target_pairs={{256,0},{320,64},{384,128},{448,192},{257,1},{321,65},{385,129},{4... | collective-permute-start | bytes 55304 | tf_op jit(solution)/shard_map/ppermute | solution.py:265
  40.2 12.5 %collective-permute-start.1 = (bf16[72,128]{1,0:T(8,128)(2,1)S(1)}, bf16[72,128]{1,0:T(8,128)(2,1)S(1)}, u32[]{:S(2)}, u32[]{:S(2)}) collective-permute-start(bf16[72,128]{1,0:T(8,128)(2,1)S(1)} %get-tuple-element.17.after_ref), channel_id=1, source_target_pairs={{128,0},{192,64},{256,128},{320,192},{384,256},{448,320},{129,1},{... | collective-permute-start | bytes 55304 | tf_op jit(solution)/shard_map/ppermute | solution.py:265
